TPU v7x, 128 devices: a whole 4x4x4 slice. The times are simulated.
128 devices in a mesh: section: 4 (over x), tensor: 32 (over y, z, core).
Axes of the slice: x: 4, y: 4, z: 4, core: 2. Of those that a mesh axis runs over, the one named last changes fastest.
Arguments:
- hidden_last: bfloat16 [512, 6656], P(None, 'tensor'), may hold values from -6 to 6
- labels: int32 [512], replicated, may hold values from 0 to 31999
- head_weight: bfloat16 [6656, 32000], P(None, 'tensor'), may hold values from -0.21875 to 0.21875
- layer_inputs: bfloat16 [4, 512, 6656], P('section', None, 'tensor'), may hold values from -6 to 6
- weights: bfloat16 [4, 6656, 6656], P('section', 'tensor'), may hold values from -0.078125 to 0.078125
- row_state: float32 [4, 6656], P('section', 'tensor'), may hold values from 1.173753e-06 to 0.000498845
- col_state: float32 [4, 6656], P('section'), may hold values from 1e-08 to 1e-06
Outputs:
- loss: float32 [], replicated
- input_grads: bfloat16 [4, 512, 6656], P('section', None, 'tensor')
- new_weights: bfloat16 [4, 6656, 6656], P('section', 'tensor')
- new_row_state: float32 [4, 6656], P('section', 'tensor')
- new_col_state: float32 [4, 6656], P('section')
All inputs are finite; a program needn't handle non-finite values.
Results may differ from a plain program's by a relative error of at most 0.007.
Values may be sent and summed in bfloat16 or wider, within the bound.
No kernel may reach another device: no remote copies, remote signals or barrier semaphores. Data moves between devices by JAX's collectives and lax.ppermute only.
A program may use at most 128 MiB of HBM per device.

v0:
```python
import jax
import jax.numpy as jnp
from jax import lax
from jax.experimental import pallas as pl
from jax.experimental.pallas import tpu as pltpu
from jax.sharding import Mesh, PartitionSpec as P

decay_rate = 0.9
learn_rate = 0.3
tiny_term = 1e-30
bf16_largest = 3.3895e38
wide_vmem = 48 * 1024 * 1024


def from_ring(block, axis):
    size = lax.axis_size(axis)
    return [block] + [
        lax.ppermute(block, axis, [(i, (i - step) % size) for i in range(size)])
        for step in range(1, size)
    ]


def rotated(pieces, index, axis=0):
    count = len(pieces)
    placed = []
    for k in range(count):
        chosen = pieces[k]
        for shift in range(1, count):
            chosen = jnp.where(index == shift, pieces[(k - shift) % count], chosen)
        placed.append(chosen)
    return jnp.stack(placed, axis=axis)


def tensor_pieces(block):
    mine = from_ring(jnp.stack(from_ring(block, "z")), "y")
    return mine + [lax.ppermute(piece, "c", [(0, 1), (1, 0)]) for piece in mine]


def summed(x, axis):
    pieces = from_ring(x, axis)
    if len(pieces) == 2:
        return pieces[0] + pieces[1]
    return (pieces[0] + pieces[2]) + (pieces[1] + pieces[3])


def summed_tensor(x):
    return summed(summed(summed(x, "c"), "z"), "y")


def scattered(blocks, axis):
    size = len(blocks)
    total = blocks[0].astype(jnp.float32)
    for step in range(1, size):
        piece = lax.ppermute(blocks[step], axis, [(i, (i + step) % size) for i in range(size)])
        total = total + piece.astype(jnp.float32)
    return total


def exchanged(blocks, axis):
    size = lax.axis_size(axis)
    index = lax.axis_index(axis)
    pieces = []
    for step in range(size):
        piece = blocks[step]
        for shift in range(1, size):
            piece = jnp.where(index == shift, blocks[(step + shift) % size], piece)
        if step:
            piece = lax.ppermute(piece, axis, [(i, (i + step) % size) for i in range(size)])
        pieces.append(piece)
    return rotated([pieces[-k % size] for k in range(size)], index, 1)


def place(pieces, place_ref, full_ref):
    y, z, c = place_ref[0], place_ref[1], place_ref[2]
    rows = pieces[0].shape[1]
    for side in range(2):
        for step_y in range(4):
            for step_z in range(4):
                chip = lax.rem(y + step_y, 4) * 4 + lax.rem(z + step_z, 4)
                core = c if side == 0 else 1 - c
                start = pl.multiple_of((chip * 2 + core) * rows, 16)
                full_ref[pl.ds(start, rows), :] = pieces[side * 4 + step_y][step_z]


def logits_kernel(place_ref, *refs):
    pieces, (labels_ref, weight_ref, both_ref, sums_ref, full_ref, total_ref) = refs[:8], refs[8:]
    step = pl.program_id(0)
    depth = weight_ref.shape[1]
    share = labels_ref.shape[1]

    @pl.when(step == 0)
    def _():
        place(pieces, place_ref, full_ref)
        total_ref[...] = jnp.zeros_like(total_ref)

    rows = full_ref[pl.ds(pl.multiple_of(step * depth, depth), depth), :]
    total_ref[...] += jnp.dot(weight_ref[...], rows, preferred_element_type=jnp.float32)

    @pl.when(step == pl.num_programs(0) - 1)
    def _():
        logits = total_ref[...]
        exponent = jnp.exp(logits)
        columns = place_ref[3] + lax.broadcasted_iota(jnp.int32, logits.shape, 0)
        label_hit = columns == labels_ref[...]
        sums_ref[0:1, :] = jnp.sum(exponent, axis=0, keepdims=True)
        sums_ref[1:2, :] = jnp.sum(jnp.where(label_hit, logits, 0.0), axis=0, keepdims=True)
        both_ref[:, :share] = jnp.minimum(exponent, bf16_largest).astype(jnp.bfloat16)
        both_ref[:, share:] = jnp.where(label_hit, 1.0, 0.0).astype(jnp.bfloat16)


def head_logits(where, pieces, labels, weight, tile=512):
    vocab_local, model_width = weight.shape
    share = labels.shape[1]
    whole = lambda shape: pl.BlockSpec(shape, lambda i, s: (0,) * len(shape))
    return pl.pallas_call(
        logits_kernel,
        grid_spec=pltpu.PrefetchScalarGridSpec(
            num_scalar_prefetch=1,
            grid=(model_width // tile,),
            in_specs=[whole(p.shape) for p in pieces]
            + [whole(labels.shape), pl.BlockSpec((vocab_local, tile), lambda i, s: (0, i))],
            out_specs=[whole((vocab_local, 2 * share)), whole((2, share))],
            scratch_shapes=[
                pltpu.VMEM((model_width, share), jnp.bfloat16),
                pltpu.VMEM((vocab_local, share), jnp.float32),
            ],
        ),
        out_shape=[
            jax.ShapeDtypeStruct((vocab_local, 2 * share), jnp.bfloat16),
            jax.ShapeDtypeStruct((2, share), jnp.float32),
        ],
        compiler_params=pltpu.CompilerParams(vmem_limit_bytes=wide_vmem),
    )(where, *pieces, labels, weight)


def combine_kernel(place_ref, product_ref, sums_ref, keep_ref, send_ref, turned_ref):
    share = sums_ref.shape[1]
    rows = keep_ref.shape[2]
    z, c = place_ref[1], place_ref[2]
    scale = (1.0 / place_ref[4].astype(jnp.float32)) / sums_ref[0:1, :]
    scale = jnp.broadcast_to(scale, (share, share)).T
    unit = 1.0 / place_ref[4].astype(jnp.float32)
    for at in range(0, product_ref.shape[1], share):
        block = product_ref[:share, at : at + share] * scale - product_ref[share:, at : at + share] * unit
        turned_ref[at : at + share, :] = block.T
    for step in range(4):
        chip = lax.rem(z + step, 4) * 2
        keep_ref[0, step] = turned_ref[pl.ds(pl.multiple_of((chip + c) * rows, 16), rows), :]
        send_ref[0, step] = turned_ref[pl.ds(pl.multiple_of((chip + 1 - c) * rows, 16), rows), :].astype(jnp.bfloat16)


def head_combine(where, product, sums, rows_local):
    width, model_width = product.shape
    share = sums.shape[1]
    tile = model_width // 4
    out_spec = pl.BlockSpec((1, 4, rows_local, share), lambda i, s: (i, 0, 0, 0))
    return pl.pallas_call(
        combine_kernel,
        grid_spec=pltpu.PrefetchScalarGridSpec(
            num_scalar_prefetch=1,
            grid=(4,),
            in_specs=[
                pl.BlockSpec((width, tile), lambda i, s: (0, lax.rem(s[0] + i, 4))),
                pl.BlockSpec(sums.shape, lambda i, s: (0, 0)),
            ],
            out_specs=[out_spec, out_spec],
            scratch_shapes=[pltpu.VMEM((tile, share), jnp.float32)],
        ),
        out_shape=[
            jax.ShapeDtypeStruct((4, 4, rows_local, share), jnp.float32),
            jax.ShapeDtypeStruct((4, 4, rows_local, share), jnp.bfloat16),
        ],
        compiler_params=pltpu.CompilerParams(vmem_limit_bytes=wide_vmem),
    )(where, product, sums)


def layer_kernel(place_ref, *refs):
    pieces, (carried_ref, weight_ref, out_ref, full_ref) = refs[:8], refs[8:]
    place(pieces, place_ref, full_ref)
    backward = jnp.dot(weight_ref[0], full_ref[...], preferred_element_type=jnp.float32)
    out_ref[...] = (carried_ref[...].astype(jnp.float32) + backward).astype(jnp.bfloat16)


def layer_back(where, carried, all_weights):
    pieces = tensor_pieces(carried)
    rows_local, model_width = all_weights.shape[1:]
    whole = lambda shape: pl.BlockSpec(shape, lambda i, s: (0,) * len(shape))
    return pl.pallas_call(
        layer_kernel,
        grid_spec=pltpu.PrefetchScalarGridSpec(
            num_scalar_prefetch=1,
            grid=(1,),
            in_specs=[whole(p.shape) for p in pieces]
            + [
                whole(carried.shape),
                pl.BlockSpec((1, rows_local, model_width), lambda i, s: (s[5], 0, 0)),
            ],
            out_specs=whole(carried.shape),
            scratch_shapes=[pltpu.VMEM((model_width, carried.shape[1]), jnp.bfloat16)],
        ),
        out_shape=jax.ShapeDtypeStruct(carried.shape, jnp.bfloat16),
        compiler_params=pltpu.CompilerParams(vmem_limit_bytes=wide_vmem),
    )(where, *pieces, carried, all_weights)


def body(hidden_last, labels, head_weight, layer_inputs, weights, row_state, col_state):
    section_count = lax.axis_size("x")
    section_index = lax.axis_index("x")
    all_rows = labels.shape[0]
    model_width, vocab_local = head_weight.shape
    local_weight = weights[0]
    rows_local = local_weight.shape[0]
    saved_all = layer_inputs[0]
    share = all_rows // section_count
    row_start = section_index * share
    entries = float(model_width * model_width)
    tensor_index = lax.axis_index(("y", "z", "c"))

    def where(layer):
        return jnp.stack(
            [
                lax.axis_index("y"),
                lax.axis_index("z"),
                lax.axis_index("c"),
                tensor_index * vocab_local,
                jnp.int32(all_rows),
                jnp.asarray(layer, jnp.int32),
            ]
        )

    all_weights = lax.all_gather(local_weight, "x", axis=0)
    hidden_rows = lax.dynamic_slice_in_dim(hidden_last, row_start, share, 0).T
    labels_here = lax.dynamic_slice_in_dim(labels, row_start, share, 0)[None, :]
    both, sums = head_logits(where(0), tensor_pieces(hidden_rows), labels_here, head_weight.T)
    sums = summed_tensor(sums)
    product = lax.dot_general(
        both, head_weight, (((0,), (1,)), ((), ())), preferred_element_type=jnp.float32
    )
    keep, send = head_combine(where(0), product, sums, rows_local)
    part = keep + lax.ppermute(send, "c", [(0, 1), (1, 0)]).astype(jnp.float32)
    part = scattered([part[0]] + [part[k].astype(jnp.bfloat16) for k in range(1, 4)], "y")
    part = scattered([part[0]] + [part[k].astype(jnp.bfloat16) for k in range(1, 4)], "z")
    carried = part.astype(jnp.bfloat16)

    def advance(step, state):
        carried, chain = state
        layer = section_count - 1 - step
        carried = layer_back(where(layer), carried, all_weights)
        return carried, lax.dynamic_update_index_in_dim(chain, carried, layer, 0)

    chain = jnp.zeros((section_count + 1, *carried.shape), jnp.bfloat16)
    chain = chain.at[section_count].set(carried)
    carried, chain = lax.fori_loop(0, section_count - 1, advance, (carried, chain))

    dy = exchanged([chain[k + 1] for k in range(section_count)], "x").reshape(rows_local, all_rows)
    dy, carried, local_weight, sums = lax.optimization_barrier((dy, carried, local_weight, sums))
    full = lax.all_gather(dy, ("y", "z", "c"), axis=0, tiled=True)
    carried = layer_back(where(0), carried, all_weights)
    outputs = exchanged([carried] + [chain[k] for k in range(1, section_count)], "x")
    outputs = outputs.reshape(rows_local, all_rows)
    loss = summed(jnp.sum(jnp.log(sums[0]) - sums[1])[None], "x")[0] / all_rows
    gradient = lax.dot_general(
        saved_all, full, (((0,), (1,)), ((), ())), preferred_element_type=jnp.float32
    )

    squares = gradient * gradient
    row_new = decay_rate * row_state[0] + (1.0 - decay_rate) * jnp.mean(squares + tiny_term, axis=1)
    col_part = jnp.sum(squares + tiny_term, axis=0)
    scaled_part = jnp.sum(squares * (1.0 / row_new)[:, None], axis=0)
    weight_float = local_weight.astype(jnp.float32)
    weight_part = jnp.broadcast_to(jnp.sum(weight_float * weight_float), (128,))
    row_part = jnp.broadcast_to(jnp.sum(row_new), (128,))
    payload = jnp.concatenate([col_part, scaled_part, row_part, weight_part]).reshape(-1, 128)
    payload = summed_tensor(payload).reshape(-1)
    col_sum = payload[:model_width]
    scaled_sum = payload[model_width : 2 * model_width]
    row_total = payload[2 * model_width]
    weight_total = payload[2 * model_width + 128]
    col_new = decay_rate * col_state[0] + (1.0 - decay_rate) * (col_sum / model_width)
    update_total = row_total * jnp.sum(scaled_sum / col_new)
    factor = (
        learn_rate
        * jnp.sqrt(weight_total / entries)
        / jnp.maximum(1.0, jnp.sqrt(update_total / entries))
    )
    row_scale = factor * jnp.sqrt(row_total / row_new)
    col_scale = 1.0 / jnp.sqrt(col_new)
    new_weight = (weight_float - gradient * row_scale[:, None] * col_scale[None, :]).astype(jnp.bfloat16)
    return (loss, outputs.T[None], new_weight[None], row_new[None], col_new[None])


def solution(mesh):
    fine = Mesh(mesh.devices.reshape(4, 4, 4, 2), ("x", "y", "z", "c"))
    tensor = ("y", "z", "c")
    return jax.shard_map(
        body,
        mesh=fine,
        in_specs=(
            P(None, tensor),
            P(),
            P(None, tensor),
            P("x", None, tensor),
            P("x", tensor, None),
            P("x", tensor),
            P("x", None),
        ),
        out_specs=(
            P(),
            P("x", None, tensor),
            P("x", tensor, None),
            P("x", tensor),
            P("x", None),
        ),
        check_vma=False,
    )
```

profile of v0, /device:TPU:0, one launch (start us, length us, event | category | flops | bytes accessed | tf_op | source)
XLA Modules:
  0.0 300.9 jit_solution(1772811289068690433)
XLA Ops:
  8.8 2.1 collective-permute-start.12
  10.9 3.6 %collective-permute-start.11 = (bf16[208,128]{1,0:T(8,128)(2,1)S(1)}, bf16[208,128]{1,0:T(8,128)(2,1)S(1)}, u32[]{:S(2)}, u32[]{:S(2)}) collective-permute-start(bf16[208,128]{1,0:T(8,128)(2,1)S(1)} %get-tuple-element.206), channel_id=1, source_target_pairs={{0,4},{2,6},{4,0},{6,2},{1,5},{3,7},{5,1},{7,3},{8,12},{10,14},{12... | collective-permute-start | bytes 159752 | tf_op jit(solution)/shard_map/ppermute | solution.py:18
  15.5 1.7 collective-permute-done.11
  18.6 3.1 %collective-permute-start.13 = (bf16[4,208,128]{2,1,0:T(8,128)(2,1)S(1)}, bf16[4,208,128]{2,1,0:T(8,128)(2,1)S(1)}, u32[]{:S(2)}, u32[]{:S(2)}) collective-permute-start(bf16[4,208,128]{2,1,0:T(8,128)(2,1)S(1)} %pad_maximum_fusion.1.refs_0_), channel_id=1, source_target_pairs={{0,24},{8,0},{16,8},{24,16},{1,25},{9,1},{17,9},{25,17},{2,26},{10... | collective-permute-start | bytes 638984 | tf_op jit(solution)/shard_map/ppermute | solution.py:18
  23.3 6.1 %collective-permute-done.13.refs_1_ = bf16[4,208,128]{2,1,0:T(8,128)(2,1)S(1)} collective-permute-done((bf16[4,208,128]{2,1,0:T(8,128)(2,1)S(1)}, bf16[4,208,128]{2,1,0:T(8,128)(2,1)S(1)}, u32[]{:S(2)}, u32[]{:S(2)}) %collective-permute-start.13) | collective-permute-done | bytes 213024 | tf_op jit(solution)/shard_map/ppermute | solution.py:18
  29.4 1.5 collective-permute-done.14.refs_2_
  30.9 2.2 collective-permute-done.15.refs_3_
  34.5 12.9 %shard_map.110 = (bf16[1000,256]{1,0:T(8,128)(2,1)S(1)}, f32[2,128]{1,0:T(2,128)S(1)}) custom-call(s32[6]{0:T(128)S(1)} %stack.185.place_ref, bf16[4,208,128]{2,1,0:T(8,128)(2,1)S(1)} %pad_maximum_fusion.1.refs_0_, bf16[4,208,128]{2,1,0:T(8,128)(2,1)S(1)} %collective-permute-done.13.refs_1_, bf16[4,208,128]{2,1,0:T(8,128)(2,1)S(1)} %collective-permute-done.14.refs_2_, ...), custom_call_target="tpu_custom_call" | custom-call | tf_op jit(solution)/shard_map/pallas_call | solution.py:115
  48.7 2.1 collective-permute-start.22
  50.8 1.5 collective-permute-start.21
  52.3 3.3 %collective-permute-done.23 = f32[2,128]{1,0:T(2,128)S(1)} collective-permute-done((f32[2,128]{1,0:T(2,128)S(1)}, f32[2,128]{1,0:T(2,128)S(1)}, u32[]{:S(2)}, u32[]{:S(2)}) %collective-permute-start.23) | collective-permute-done | bytes 1056 | tf_op jit(solution)/shard_map/ppermute | solution.py:18
  58.5 10.8 %fusion.33.product_ref = f32[256,6656]{1,0:T(8,128)} fusion(bf16[1000,256]{1,0:T(8,128)(2,1)S(1)} %get-tuple-element.155, bf16[6656,1000]{0,1:T(8,128)(2,1)} %param.13), kind=kOutput, calls=%fused_computation.90 | convolution fusion | flops 3407872000 | bytes 20639744 | tf_op jit(solution)/shard_map/dot_general | solution.py:236
  69.4 5.1 %shard_map.111 = (f32[4,4,208,128]{3,2,1,0:T(8,128)S(1)}, bf16[4,4,208,128]{3,2,1,0:T(8,128)(2,1)S(1)}) custom-call(s32[6]{0:T(128)S(1)} %stack.185.place_ref, f32[256,6656]{1,0:T(8,128)} %fusion.33.product_ref, f32[2,128]{1,0:T(2,128)S(1)} %add_add_fusion.2.sums_ref), custom_call_target="tpu_custom_call" | custom-call | tf_op jit(solution)/shard_map/pallas_call | solution.py:157
  74.5 2.4 collective-permute-done.27
  77.2 2.1 collective-permute-start.30
  79.3 2.0 collective-permute-start.29
  81.6 7.1 %collective-permute-done.30 = bf16[4,208,128]{2,1,0:T(8,128)(2,1)S(1)} collective-permute-done((bf16[4,208,128]{2,1,0:T(8,128)(2,1)S(1)}, bf16[4,208,128]{2,1,0:T(8,128)(2,1)S(1)}, u32[]{:S(2)}, u32[]{:S(2)}) %collective-permute-start.30) | collective-permute-done | bytes 213024 | tf_op jit(solution)/shard_map/ppermute | solution.py:54
  89.0 3.4 %collective-permute-done.28 = bf16[4,208,128]{2,1,0:T(8,128)(2,1)S(1)} collective-permute-done((bf16[4,208,128]{2,1,0:T(8,128)(2,1)S(1)}, bf16[4,208,128]{2,1,0:T(8,128)(2,1)S(1)}, u32[]{:S(2)}, u32[]{:S(2)}) %collective-permute-start.28) | collective-permute-done | bytes 213024 | tf_op jit(solution)/shard_map/ppermute | solution.py:54
  92.5 3.3 %collective-permute-start.33 = (bf16[208,128]{1,0:T(8,128)(2,1)S(1)}, bf16[208,128]{1,0:T(8,128)(2,1)S(1)}, u32[]{:S(2)}, u32[]{:S(2)}) collective-permute-start(bf16[208,128]{1,0:T(8,128)(2,1)S(1)} %get-tuple-element.203), channel_id=1, source_target_pairs={{0,6},{2,0},{4,2},{6,4},{1,7},{3,1},{5,3},{7,5},{8,14},{10,8},{12,... | collective-permute-start | bytes 159752 | tf_op jit(solution)/shard_map/ppermute | solution.py:54
  96.8 1.6 collective-permute-done.33
  98.4 3.2 %collective-permute-done.32 = bf16[208,128]{1,0:T(8,128)(2,1)S(1)} collective-permute-done((bf16[208,128]{1,0:T(8,128)(2,1)S(1)}, bf16[208,128]{1,0:T(8,128)(2,1)S(1)}, u32[]{:S(2)}, u32[]{:S(2)}) %collective-permute-start.32) | collective-permute-done | bytes 53280 | tf_op jit(solution)/shard_map/ppermute | solution.py:54
  101.8 16.2 %all-gather.3.cloned.1.call-done.refs_9_ = bf16[4,208,6656]{2,1,0:T(8,128)(2,1)} async-done(((bf16[1,208,6656]{2,1,0:T(8,128)(2,1)}), bf16[4,208,6656]{2,1,0:T(8,128)(2,1)}) %all-gather.3.cloned.1.call-update) | async-done | bytes 11075600 | tf_op jit(solution)/shard_map/all_gather | solution.py:231
  118.0 78.6 %while.18 = (s32[]{:T(128)}, bf16[208,128]{1,0:T(8,128)(2,1)S(1)}, bf16[5,208,128]{2,1,0:T(8,128)(2,1)S(1)}, s32[]{:T(128)}, bf16[4,208,6656]{2,1,0:T(8,128)(2,1...) while((s32[]{:T(128)}, bf16[208,128]{1,0:T(8,128)(2,1)S(1)}, ...), condition=%wide.region_1.2_spmd, body=%wide.region_0.0_spmd.sunk | while | flops 319502 | bytes 7242435 | solution.py:253
  118.0 1.6 collective-permute-start
  119.6 2.9 collective-permute-start.1
  126.6 2.8 collective-permute-start.3
  131.1 6.0 %collective-permute-done.3.refs_1_ = bf16[4,208,128]{2,1,0:T(8,128)(2,1)S(1)} collective-permute-done((bf16[4,208,128]{2,1,0:T(8,128)(2,1)S(1)}, bf16[4,208,128]{2,1,0:T(8,128)(2,1)S(1)}, u32[]{:S(2)}, u32[]{:S(2)}) %collective-permute-start.3) | collective-permute-done | bytes 213024 | tf_op jit(solution)/shard_map/while/body/eval_jaxpr/ppermute | solution.py:18
  137.1 1.5 collective-permute-done.4.refs_2_
  138.6 2.2 collective-permute-done.5.refs_3_
  142.2 3.3 %eval_jaxpr.8 = bf16[208,128]{1,0:T(8,128)(2,1)S(1)} custom-call(s32[6]{0:T(128)S(1)} %stack.207.place_ref, bf16[4,208,128]{2,1,0:T(8,128)(2,1)S(1)} %pad_maximum_fusion.4.refs_0_, bf16[4,208,128]{2,1,0:T(8,128)(2,1)S(1)} %collective-permute-done.3.refs_1_, bf16[4,208,128]{2,1,0:T(8,128)(2,1)S(1)} %collective-permute-done.4.refs_2_, ...), custom_call_target="tpu_custom_call" | custom-call | tf_op jit(solution)/shard_map/while/body/eval_jaxpr/pallas_call | solution.py:188
  145.9 3.6 %collective-permute-start.1 = (bf16[208,128]{1,0:T(8,128)(2,1)S(1)}, bf16[208,128]{1,0:T(8,128)(2,1)S(1)}, u32[]{:S(2)}, u32[]{:S(2)}) collective-permute-start(bf16[208,128]{1,0:T(8,128)(2,1)S(1)} %copy.33.refs_8_), channel_id=1, source_target_pairs={{0,4},{2,6},{4,0},{6,2},{1,5},{3,7},{5,1},{7,3},{8,12},{10,14},{12... | collective-permute-start | bytes 159752 | tf_op jit(solution)/shard_map/while/body/eval_jaxpr/ppermute | solution.py:18
  149.8 1.8 collective-permute-done
  155.9 6.0 %collective-permute-done.3.refs_1_ = bf16[4,208,128]{2,1,0:T(8,128)(2,1)S(1)} collective-permute-done((bf16[4,208,128]{2,1,0:T(8,128)(2,1)S(1)}, bf16[4,208,128]{2,1,0:T(8,128)(2,1)S(1)}, u32[]{:S(2)}, u32[]{:S(2)}) %collective-permute-start.3) | collective-permute-done | bytes 213024 | tf_op jit(solution)/shard_map/while/body/eval_jaxpr/ppermute | solution.py:18
  161.9 2.1 collective-permute-done.4.refs_2_
  164.0 2.3 collective-permute-done.5.refs_3_
  167.7 3.3 %eval_jaxpr.8 = bf16[208,128]{1,0:T(8,128)(2,1)S(1)} custom-call(s32[6]{0:T(128)S(1)} %stack.207.place_ref, bf16[4,208,128]{2,1,0:T(8,128)(2,1)S(1)} %pad_maximum_fusion.4.refs_0_, bf16[4,208,128]{2,1,0:T(8,128)(2,1)S(1)} %collective-permute-done.3.refs_1_, bf16[4,208,128]{2,1,0:T(8,128)(2,1)S(1)} %collective-permute-done.4.refs_2_, ...), custom_call_target="tpu_custom_call" | custom-call | tf_op jit(solution)/shard_map/while/body/eval_jaxpr/pallas_call | solution.py:188
  171.6 3.0 %collective-permute-start.1 = (bf16[208,128]{1,0:T(8,128)(2,1)S(1)}, bf16[208,128]{1,0:T(8,128)(2,1)S(1)}, u32[]{:S(2)}, u32[]{:S(2)}) collective-permute-start(bf16[208,128]{1,0:T(8,128)(2,1)S(1)} %copy.33.refs_8_), channel_id=1, source_target_pairs={{0,4},{2,6},{4,0},{6,2},{1,5},{3,7},{5,1},{7,3},{8,12},{10,14},{12... | collective-permute-start | bytes 159752 | tf_op jit(solution)/shard_map/while/body/eval_jaxpr/ppermute | solution.py:18
  175.1 1.9 collective-permute-done
  180.9 6.2 %collective-permute-done.3.refs_1_ = bf16[4,208,128]{2,1,0:T(8,128)(2,1)S(1)} collective-permute-done((bf16[4,208,128]{2,1,0:T(8,128)(2,1)S(1)}, bf16[4,208,128]{2,1,0:T(8,128)(2,1)S(1)}, u32[]{:S(2)}, u32[]{:S(2)}) %collective-permute-start.3) | collective-permute-done | bytes 213024 | tf_op jit(solution)/shard_map/while/body/eval_jaxpr/ppermute | solution.py:18
  187.0 2.5 collective-permute-done.4.refs_2_
  189.5 2.3 collective-permute-done.5.refs_3_
  193.3 3.3 %eval_jaxpr.8 = bf16[208,128]{1,0:T(8,128)(2,1)S(1)} custom-call(s32[6]{0:T(128)S(1)} %stack.207.place_ref, bf16[4,208,128]{2,1,0:T(8,128)(2,1)S(1)} %pad_maximum_fusion.4.refs_0_, bf16[4,208,128]{2,1,0:T(8,128)(2,1)S(1)} %collective-permute-done.3.refs_1_, bf16[4,208,128]{2,1,0:T(8,128)(2,1)S(1)} %collective-permute-done.4.refs_2_, ...), custom_call_target="tpu_custom_call" | custom-call | tf_op jit(solution)/shard_map/while/body/eval_jaxpr/pallas_call | solution.py:188
  196.6 2.8 collective-permute-start.35
  199.4 3.2 %collective-permute-start.34 = (bf16[208,128]{1,0:T(8,128)(2,1)S(1)}, bf16[208,128]{1,0:T(8,128)(2,1)S(1)}, u32[]{:S(2)}, u32[]{:S(2)}) collective-permute-start(bf16[208,128]{1,0:T(8,128)(2,1)S(1)} %get-tuple-element.195), channel_id=1, source_target_pairs={{0,96},{32,0},{64,32},{96,64},{1,97},{33,1},{65,33},{97,65},{2,98}... | collective-permute-start | bytes 159752 | tf_op jit(solution)/shard_map/ppermute | solution.py:68
  202.7 2.1 collective-permute-done.36
  206.4 2.7 collective-permute-start.41
  216.1 1.7 collective-permute-start.37
  217.8 4.0 %collective-permute-done.43.refs_1_ = bf16[4,208,128]{2,1,0:T(8,128)(2,1)S(1)} collective-permute-done((bf16[4,208,128]{2,1,0:T(8,128)(2,1)S(1)}, bf16[4,208,128]{2,1,0:T(8,128)(2,1)S(1)}, u32[]{:S(2)}, u32[]{:S(2)}) %collective-permute-start.43) | collective-permute-done | bytes 213024 | tf_op jit(solution)/shard_map/ppermute | solution.py:18
  221.9 2.8 collective-permute-done.44.refs_2_
  224.7 3.0 collective-permute-done.45.refs_3_
  227.7 3.8 %fusion = f32[]{:T(128)} fusion(bf16[208,6656]{1,0:T(8,128)(2,1)} %bitcast.216), kind=kLoop, calls=%fused_computation.4 | loop fusion | flops 4153343 | bytes 2768900 | tf_op jit(solution)/shard_map/reduce_sum | solution.py:271
  231.5 2.6 collective-permute-start.38
  236.4 4.2 %collective-permute-done.39 = f32[1]{0:T(128)} collective-permute-done((f32[1]{0:T(128)}, f32[1]{0:T(128)}, u32[]{:S(2)}, u32[]{:S(2)}) %collective-permute-start.39) | collective-permute-done | bytes 36 | tf_op jit(solution)/shard_map/ppermute | solution.py:18
  242.0 3.4 %shard_map.112 = bf16[208,128]{1,0:T(8,128)(2,1)S(1)} custom-call(s32[6]{0:T(128)S(1)} %stack.185.place_ref, bf16[4,208,128]{2,1,0:T(8,128)(2,1)S(1)} %pad_maximum_fusion.2.refs_0_, bf16[4,208,128]{2,1,0:T(8,128)(2,1)S(1)} %collective-permute-done.43.refs_1_, bf16[4,208,128]{2,1,0:T(8,128)(2,1)S(1)} %collective-permute-done.44.refs_2_, ...), custom_call_target="tpu_custom_call" | custom-call | tf_op jit(solution)/shard_map/pallas_call | solution.py:188
  247.1 1.9 collective-permute-start.52
  250.3 6.1 %all-gather.5.cloned.1.call-done = bf16[6656,512]{1,0:T(8,128)(2,1)} async-done(((bf16[208,512]{1,0:T(8,128)(2,1)}), bf16[6656,512]{1,0:T(8,128)(2,1)}) %all-gather.5.cloned.1.call-update) | async-done | bytes 6815760 | tf_op jit(solution)/shard_map/all_gather | solution.py:257
  256.5 5.3 %add_reduce_fusion = (f32[208]{0:T(256)S(1)}, f32[6656,208]{0,1:T(8,128)S(1)}) fusion(bf16[6656,512]{1,0:T(8,128)(2,1)} %all-gather.5.cloned.1.call-done, bf16[1,512,208]{1,2,0:T(8,128)(2,1)S(1)} %copy-done), kind=kOutput, calls=%fused_computation.7 | convolution fusion | flops 1421827840 | bytes 12567360 | tf_op jit(solution)/shard_map/dot_general | solution.py:262
  267.3 1.9 collective-permute-start.55
  269.4 2.1 collective-permute-start.54
  271.5 3.9 %collective-permute-done.56 = f32[106,128]{1,0:T(8,128)S(1)} collective-permute-done((f32[106,128]{1,0:T(8,128)S(1)}, f32[106,128]{1,0:T(8,128)S(1)}, u32[]{:S(2)}, u32[]{:S(2)}) %collective-permute-start.56) | collective-permute-done | bytes 54304 | tf_op jit(solution)/shard_map/ppermute | solution.py:18
  275.5 1.7 collective-permute-start.58
  277.6 1.9 collective-permute-start.57
  280.1 2.4 collective-permute-done.59
  287.8 5.1 %fusion.2 = bf16[1,208,6656]{2,1,0:T(8,128)(2,1)} fusion(f32[6656,208]{0,1:T(8,128)} %copy-done.2, bf16[208,6656]{1,0:T(8,128)(2,1)S(1)} %bitcast.217, f32[6656]{0:T(1024)S(1)} %get-tuple-element.177, f32[208]{0:T(256)S(1)} %sqrt_multiply_fusion), kind=kLoop, calls=%fused_computation.9 | loop fusion | flops 6922240 | bytes 11103040 | tf_op jit(solution)/shard_map/broadcast_in_dim | solution.py:289
  (173 shorter events, 56.6 us)
Async XLA Ops:
  7.2 110.8 %all-gather.3.cloned.1.call-start = ((), (), s32[]{:S(2)}) async-start(), calls=%async_computation | async-start | bytes 13844480 | tf_op jit(solution)/shard_map/all_gather | solution.py:231
  7.9 248.6 %all-gather.5.cloned.1.call-start = ((), (), s32[]{:S(2)}) async-start(), calls=%async_computation.1 | async-start | bytes 7028736 | tf_op jit(solution)/shard_map/all_gather | solution.py:257
  8.8 6.7 %collective-permute-start.12 = (bf16[208,128]{1,0:T(8,128)(2,1)S(1)}, bf16[208,128]{1,0:T(8,128)(2,1)S(1)}, u32[]{:S(2)}, u32[]{:S(2)}) collective-permute-start(bf16[208,128]{1,0:T(8,128)(2,1)S(1)} %get-tuple-element.206), channel_id=1, source_target_pairs={{0,2},{2,4},{4,6},{6,0},{1,3},{3,5},{5,7},{7,1},{8,10},{10,12},{12... | collective-permute-start | bytes 159752 | tf_op jit(solution)/shard_map/ppermute | solution.py:18
  10.9 6.3 %collective-permute-start.11 = (bf16[208,128]{1,0:T(8,128)(2,1)S(1)}, bf16[208,128]{1,0:T(8,128)(2,1)S(1)}, u32[]{:S(2)}, u32[]{:S(2)}) collective-permute-start(bf16[208,128]{1,0:T(8,128)(2,1)S(1)} %get-tuple-element.206), channel_id=1, source_target_pairs={{0,4},{2,6},{4,0},{6,2},{1,5},{3,7},{5,1},{7,3},{8,12},{10,14},{12... | collective-permute-start | bytes 159752 | tf_op jit(solution)/shard_map/ppermute | solution.py:18
  18.6 10.7 %collective-permute-start.13 = (bf16[4,208,128]{2,1,0:T(8,128)(2,1)S(1)}, bf16[4,208,128]{2,1,0:T(8,128)(2,1)S(1)}, u32[]{:S(2)}, u32[]{:S(2)}) collective-permute-start(bf16[4,208,128]{2,1,0:T(8,128)(2,1)S(1)} %pad_maximum_fusion.1.refs_0_), channel_id=1, source_target_pairs={{0,24},{8,0},{16,8},{24,16},{1,25},{9,1},{17,9},{25,17},{2,26},{10... | collective-permute-start | bytes 638984 | tf_op jit(solution)/shard_map/ppermute | solution.py:18
  21.7 9.2 %collective-permute-start.14 = (bf16[4,208,128]{2,1,0:T(8,128)(2,1)S(1)}, bf16[4,208,128]{2,1,0:T(8,128)(2,1)S(1)}, u32[]{:S(2)}, u32[]{:S(2)}) collective-permute-start(bf16[4,208,128]{2,1,0:T(8,128)(2,1)S(1)} %pad_maximum_fusion.1.refs_0_), channel_id=1, source_target_pairs={{0,16},{8,24},{16,0},{24,8},{1,17},{9,25},{17,1},{25,9},{2,18},{10... | collective-permute-start | bytes 638984 | tf_op jit(solution)/shard_map/ppermute | solution.py:18
  22.3 10.8 %collective-permute-start.15 = (bf16[4,208,128]{2,1,0:T(8,128)(2,1)S(1)}, bf16[4,208,128]{2,1,0:T(8,128)(2,1)S(1)}, u32[]{:S(2)}, u32[]{:S(2)}) collective-permute-start(bf16[4,208,128]{2,1,0:T(8,128)(2,1)S(1)} %pad_maximum_fusion.1.refs_0_), channel_id=1, source_target_pairs={{0,8},{8,16},{16,24},{24,0},{1,9},{9,17},{17,25},{25,1},{2,10},{10... | collective-permute-start | bytes 638984 | tf_op jit(solution)/shard_map/ppermute | solution.py:18
  23.3 10.6 %collective-permute-start.16 = (bf16[4,208,128]{2,1,0:T(8,128)(2,1)S(1)}, bf16[4,208,128]{2,1,0:T(8,128)(2,1)S(1)}, u32[]{:S(2)}, u32[]{:S(2)}) collective-permute-start(bf16[4,208,128]{2,1,0:T(8,128)(2,1)S(1)} %pad_maximum_fusion.1.refs_0_), channel_id=1, source_target_pairs={{0,1},{1,0},{2,3},{3,2},{4,5},{5,4},{6,7},{7,6},{8,9},{9,8},{10,11... | collective-permute-start | bytes 638984 | tf_op jit(solution)/shard_map/ppermute | solution.py:36
  29.4 4.6 %collective-permute-start.17 = (bf16[4,208,128]{2,1,0:T(8,128)(2,1)S(1)}, bf16[4,208,128]{2,1,0:T(8,128)(2,1)S(1)}, u32[]{:S(2)}, u32[]{:S(2)}) collective-permute-start(bf16[4,208,128]{2,1,0:T(8,128)(2,1)S(1)} %collective-permute-done.13.refs_1_), channel_id=1, source_target_pairs={{0,1},{1,0},{2,3},{3,2},{4,5},{5,4},{6,7},{7,6},{8,9},{9,8},{10,11... | collective-permute-start | bytes 638984 | tf_op jit(solution)/shard_map/ppermute | solution.py:36
  50.8 4.8 %collective-permute-start.23 = (f32[2,128]{1,0:T(2,128)S(1)}, f32[2,128]{1,0:T(2,128)S(1)}, u32[]{:S(2)}, u32[]{:S(2)}) collective-permute-start(f32[2,128]{1,0:T(2,128)S(1)} %add.146), channel_id=1, source_target_pairs={{0,2},{2,4},{4,6},{6,0},{1,3},{3,5},{5,7},{7,1},{8,10},{10,12},{12... | collective-permute-start | bytes 3080 | tf_op jit(solution)/shard_map/ppermute | solution.py:18
  50.8 5.1 %collective-permute-start.21 = (f32[2,128]{1,0:T(2,128)S(1)}, f32[2,128]{1,0:T(2,128)S(1)}, u32[]{:S(2)}, u32[]{:S(2)}) collective-permute-start(f32[2,128]{1,0:T(2,128)S(1)} %add.146), channel_id=1, source_target_pairs={{0,4},{2,6},{4,0},{6,2},{1,5},{3,7},{5,1},{7,3},{8,12},{10,14},{12... | collective-permute-start | bytes 3080 | tf_op jit(solution)/shard_map/ppermute | solution.py:18
  55.9 13.5 %collective-permute-start.25 = (f32[2,128]{1,0:T(2,128)S(1)}, f32[2,128]{1,0:T(2,128)S(1)}, u32[]{:S(2)}, u32[]{:S(2)}) collective-permute-start(f32[2,128]{1,0:T(2,128)S(1)} %add_add_fusion.3), channel_id=1, source_target_pairs={{0,24},{8,0},{16,8},{24,16},{1,25},{9,1},{17,9},{25,17},{2,26},{10... | collective-permute-start | bytes 3080 | tf_op jit(solution)/shard_map/ppermute | solution.py:18
  56.4 12.9 %collective-permute-start.26 = (f32[2,128]{1,0:T(2,128)S(1)}, f32[2,128]{1,0:T(2,128)S(1)}, u32[]{:S(2)}, u32[]{:S(2)}) collective-permute-start(f32[2,128]{1,0:T(2,128)S(1)} %add_add_fusion.3), channel_id=1, source_target_pairs={{0,8},{8,16},{16,24},{24,0},{1,9},{9,17},{17,25},{25,1},{2,10},{10... | collective-permute-start | bytes 3080 | tf_op jit(solution)/shard_map/ppermute | solution.py:18
  57.9 11.5 %collective-permute-start.24 = (f32[2,128]{1,0:T(2,128)S(1)}, f32[2,128]{1,0:T(2,128)S(1)}, u32[]{:S(2)}, u32[]{:S(2)}) collective-permute-start(f32[2,128]{1,0:T(2,128)S(1)} %add_add_fusion.3), channel_id=1, source_target_pairs={{0,16},{8,24},{16,0},{24,8},{1,17},{9,25},{17,1},{25,9},{2,18},{10... | collective-permute-start | bytes 3080 | tf_op jit(solution)/shard_map/ppermute | solution.py:18
  77.2 11.5 %collective-permute-start.30 = (bf16[4,208,128]{2,1,0:T(8,128)(2,1)S(1)}, bf16[4,208,128]{2,1,0:T(8,128)(2,1)S(1)}, u32[]{:S(2)}, u32[]{:S(2)}) collective-permute-start(bf16[4,208,128]{2,1,0:T(8,128)(2,1)S(1)} %get-tuple-element.189), channel_id=1, source_target_pairs={{0,24},{8,0},{16,8},{24,16},{1,25},{9,1},{17,9},{25,17},{2,26},{10... | collective-permute-start | bytes 638984 | tf_op jit(solution)/shard_map/ppermute | solution.py:54
  79.3 9.7 %collective-permute-start.29 = (bf16[4,208,128]{2,1,0:T(8,128)(2,1)S(1)}, bf16[4,208,128]{2,1,0:T(8,128)(2,1)S(1)}, u32[]{:S(2)}, u32[]{:S(2)}) collective-permute-start(bf16[4,208,128]{2,1,0:T(8,128)(2,1)S(1)} %get-tuple-element.190), channel_id=1, source_target_pairs={{0,16},{8,24},{16,0},{24,8},{1,17},{9,25},{17,1},{25,9},{2,18},{10... | collective-permute-start | bytes 638984 | tf_op jit(solution)/shard_map/ppermute | solution.py:54
  81.4 11.1 %collective-permute-start.28 = (bf16[4,208,128]{2,1,0:T(8,128)(2,1)S(1)}, bf16[4,208,128]{2,1,0:T(8,128)(2,1)S(1)}, u32[]{:S(2)}, u32[]{:S(2)}) collective-permute-start(bf16[4,208,128]{2,1,0:T(8,128)(2,1)S(1)} %get-tuple-element.188), channel_id=1, source_target_pairs={{0,8},{8,16},{16,24},{24,0},{1,9},{9,17},{17,25},{25,1},{2,10},{10... | collective-permute-start | bytes 638984 | tf_op jit(solution)/shard_map/ppermute | solution.py:54
  92.5 5.8 %collective-permute-start.33 = (bf16[208,128]{1,0:T(8,128)(2,1)S(1)}, bf16[208,128]{1,0:T(8,128)(2,1)S(1)}, u32[]{:S(2)}, u32[]{:S(2)}) collective-permute-start(bf16[208,128]{1,0:T(8,128)(2,1)S(1)} %get-tuple-element.203), channel_id=1, source_target_pairs={{0,6},{2,0},{4,2},{6,4},{1,7},{3,1},{5,3},{7,5},{8,14},{10,8},{12,... | collective-permute-start | bytes 159752 | tf_op jit(solution)/shard_map/ppermute | solution.py:54
  95.8 5.7 %collective-permute-start.32 = (bf16[208,128]{1,0:T(8,128)(2,1)S(1)}, bf16[208,128]{1,0:T(8,128)(2,1)S(1)}, u32[]{:S(2)}, u32[]{:S(2)}) collective-permute-start(bf16[208,128]{1,0:T(8,128)(2,1)S(1)} %get-tuple-element.204), channel_id=1, source_target_pairs={{0,4},{2,6},{4,0},{6,2},{1,5},{3,7},{5,1},{7,3},{8,12},{10,14},{12... | collective-permute-start | bytes 159752 | tf_op jit(solution)/shard_map/ppermute | solution.py:54
  95.8 5.9 %collective-permute-start.31 = (bf16[208,128]{1,0:T(8,128)(2,1)S(1)}, bf16[208,128]{1,0:T(8,128)(2,1)S(1)}, u32[]{:S(2)}, u32[]{:S(2)}) collective-permute-start(bf16[208,128]{1,0:T(8,128)(2,1)S(1)} %get-tuple-element.202), channel_id=1, source_target_pairs={{0,2},{2,4},{4,6},{6,0},{1,3},{3,5},{5,7},{7,1},{8,10},{10,12},{12... | collective-permute-start | bytes 159752 | tf_op jit(solution)/shard_map/ppermute | solution.py:54
  118.0 5.8 %collective-permute-start = (bf16[208,128]{1,0:T(8,128)(2,1)S(1)}, bf16[208,128]{1,0:T(8,128)(2,1)S(1)}, u32[]{:S(2)}, u32[]{:S(2)}) collective-permute-start(bf16[208,128]{1,0:T(8,128)(2,1)S(1)} %copy.33.refs_8_), channel_id=1, source_target_pairs={{0,2},{2,4},{4,6},{6,0},{1,3},{3,5},{5,7},{7,1},{8,10},{10,12},{12... | collective-permute-start | bytes 159752 | tf_op jit(solution)/shard_map/while/body/eval_jaxpr/ppermute | solution.py:18
  119.6 5.6 %collective-permute-start.1 = (bf16[208,128]{1,0:T(8,128)(2,1)S(1)}, bf16[208,128]{1,0:T(8,128)(2,1)S(1)}, u32[]{:S(2)}, u32[]{:S(2)}) collective-permute-start(bf16[208,128]{1,0:T(8,128)(2,1)S(1)} %copy.33.refs_8_), channel_id=1, source_target_pairs={{0,4},{2,6},{4,0},{6,2},{1,5},{3,7},{5,1},{7,3},{8,12},{10,14},{12... | collective-permute-start | bytes 159752 | tf_op jit(solution)/shard_map/while/body/eval_jaxpr/ppermute | solution.py:18
  122.4 4.1 %collective-permute-start.2 = (bf16[208,128]{1,0:T(8,128)(2,1)S(1)}, bf16[208,128]{1,0:T(8,128)(2,1)S(1)}, u32[]{:S(2)}, u32[]{:S(2)}) collective-permute-start(bf16[208,128]{1,0:T(8,128)(2,1)S(1)} %copy.33.refs_8_), channel_id=1, source_target_pairs={{0,6},{2,0},{4,2},{6,4},{1,7},{3,1},{5,3},{7,5},{8,14},{10,8},{12,... | collective-permute-start | bytes 159752 | tf_op jit(solution)/shard_map/while/body/eval_jaxpr/ppermute | solution.py:18
  126.6 10.5 %collective-permute-start.3 = (bf16[4,208,128]{2,1,0:T(8,128)(2,1)S(1)}, bf16[4,208,128]{2,1,0:T(8,128)(2,1)S(1)}, u32[]{:S(2)}, u32[]{:S(2)}) collective-permute-start(bf16[4,208,128]{2,1,0:T(8,128)(2,1)S(1)} %pad_maximum_fusion.4.refs_0_), channel_id=1, source_target_pairs={{0,24},{8,0},{16,8},{24,16},{1,25},{9,1},{17,9},{25,17},{2,26},{10... | collective-permute-start | bytes 638984 | tf_op jit(solution)/shard_map/while/body/eval_jaxpr/ppermute | solution.py:18
  129.4 9.2 %collective-permute-start.4 = (bf16[4,208,128]{2,1,0:T(8,128)(2,1)S(1)}, bf16[4,208,128]{2,1,0:T(8,128)(2,1)S(1)}, u32[]{:S(2)}, u32[]{:S(2)}) collective-permute-start(bf16[4,208,128]{2,1,0:T(8,128)(2,1)S(1)} %pad_maximum_fusion.4.refs_0_), channel_id=1, source_target_pairs={{0,16},{8,24},{16,0},{24,8},{1,17},{9,25},{17,1},{25,9},{2,18},{10... | collective-permute-start | bytes 638984 | tf_op jit(solution)/shard_map/while/body/eval_jaxpr/ppermute | solution.py:18
  130.2 10.6 %collective-permute-start.5 = (bf16[4,208,128]{2,1,0:T(8,128)(2,1)S(1)}, bf16[4,208,128]{2,1,0:T(8,128)(2,1)S(1)}, u32[]{:S(2)}, u32[]{:S(2)}) collective-permute-start(bf16[4,208,128]{2,1,0:T(8,128)(2,1)S(1)} %pad_maximum_fusion.4.refs_0_), channel_id=1, source_target_pairs={{0,8},{8,16},{16,24},{24,0},{1,9},{9,17},{17,25},{25,1},{2,10},{10... | collective-permute-start | bytes 638984 | tf_op jit(solution)/shard_map/while/body/eval_jaxpr/ppermute | solution.py:18
  131.1 9.8 %collective-permute-start.6 = (bf16[4,208,128]{2,1,0:T(8,128)(2,1)S(1)}, bf16[4,208,128]{2,1,0:T(8,128)(2,1)S(1)}, u32[]{:S(2)}, u32[]{:S(2)}) collective-permute-start(bf16[4,208,128]{2,1,0:T(8,128)(2,1)S(1)} %pad_maximum_fusion.4.refs_0_), channel_id=1, source_target_pairs={{0,1},{1,0},{2,3},{3,2},{4,5},{5,4},{6,7},{7,6},{8,9},{9,8},{10,11... | collective-permute-start | bytes 638984 | tf_op jit(solution)/shard_map/while/body/eval_jaxpr/ppermute | solution.py:36
  145.6 5.9 %collective-permute-start = (bf16[208,128]{1,0:T(8,128)(2,1)S(1)}, bf16[208,128]{1,0:T(8,128)(2,1)S(1)}, u32[]{:S(2)}, u32[]{:S(2)}) collective-permute-start(bf16[208,128]{1,0:T(8,128)(2,1)S(1)} %copy.33.refs_8_), channel_id=1, source_target_pairs={{0,2},{2,4},{4,6},{6,0},{1,3},{3,5},{5,7},{7,1},{8,10},{10,12},{12... | collective-permute-start | bytes 159752 | tf_op jit(solution)/shard_map/while/body/eval_jaxpr/ppermute | solution.py:18
  145.9 6.6 %collective-permute-start.1 = (bf16[208,128]{1,0:T(8,128)(2,1)S(1)}, bf16[208,128]{1,0:T(8,128)(2,1)S(1)}, u32[]{:S(2)}, u32[]{:S(2)}) collective-permute-start(bf16[208,128]{1,0:T(8,128)(2,1)S(1)} %copy.33.refs_8_), channel_id=1, source_target_pairs={{0,4},{2,6},{4,0},{6,2},{1,5},{3,7},{5,1},{7,3},{8,12},{10,14},{12... | collective-permute-start | bytes 159752 | tf_op jit(solution)/shard_map/while/body/eval_jaxpr/ppermute | solution.py:18
  153.6 8.3 %collective-permute-start.3 = (bf16[4,208,128]{2,1,0:T(8,128)(2,1)S(1)}, bf16[4,208,128]{2,1,0:T(8,128)(2,1)S(1)}, u32[]{:S(2)}, u32[]{:S(2)}) collective-permute-start(bf16[4,208,128]{2,1,0:T(8,128)(2,1)S(1)} %pad_maximum_fusion.4.refs_0_), channel_id=1, source_target_pairs={{0,24},{8,0},{16,8},{24,16},{1,25},{9,1},{17,9},{25,17},{2,26},{10... | collective-permute-start | bytes 638984 | tf_op jit(solution)/shard_map/while/body/eval_jaxpr/ppermute | solution.py:18
  154.3 9.7 %collective-permute-start.4 = (bf16[4,208,128]{2,1,0:T(8,128)(2,1)S(1)}, bf16[4,208,128]{2,1,0:T(8,128)(2,1)S(1)}, u32[]{:S(2)}, u32[]{:S(2)}) collective-permute-start(bf16[4,208,128]{2,1,0:T(8,128)(2,1)S(1)} %pad_maximum_fusion.4.refs_0_), channel_id=1, source_target_pairs={{0,16},{8,24},{16,0},{24,8},{1,17},{9,25},{17,1},{25,9},{2,18},{10... | collective-permute-start | bytes 638984 | tf_op jit(solution)/shard_map/while/body/eval_jaxpr/ppermute | solution.py:18
  155.1 11.2 %collective-permute-start.5 = (bf16[4,208,128]{2,1,0:T(8,128)(2,1)S(1)}, bf16[4,208,128]{2,1,0:T(8,128)(2,1)S(1)}, u32[]{:S(2)}, u32[]{:S(2)}) collective-permute-start(bf16[4,208,128]{2,1,0:T(8,128)(2,1)S(1)} %pad_maximum_fusion.4.refs_0_), channel_id=1, source_target_pairs={{0,8},{8,16},{16,24},{24,0},{1,9},{9,17},{17,25},{25,1},{2,10},{10... | collective-permute-start | bytes 638984 | tf_op jit(solution)/shard_map/while/body/eval_jaxpr/ppermute | solution.py:18
  155.9 10.4 %collective-permute-start.6 = (bf16[4,208,128]{2,1,0:T(8,128)(2,1)S(1)}, bf16[4,208,128]{2,1,0:T(8,128)(2,1)S(1)}, u32[]{:S(2)}, u32[]{:S(2)}) collective-permute-start(bf16[4,208,128]{2,1,0:T(8,128)(2,1)S(1)} %pad_maximum_fusion.4.refs_0_), channel_id=1, source_target_pairs={{0,1},{1,0},{2,3},{3,2},{4,5},{5,4},{6,7},{7,6},{8,9},{9,8},{10,11... | collective-permute-start | bytes 638984 | tf_op jit(solution)/shard_map/while/body/eval_jaxpr/ppermute | solution.py:36
  161.9 4.4 %collective-permute-start.7 = (bf16[4,208,128]{2,1,0:T(8,128)(2,1)S(1)}, bf16[4,208,128]{2,1,0:T(8,128)(2,1)S(1)}, u32[]{:S(2)}, u32[]{:S(2)}) collective-permute-start(bf16[4,208,128]{2,1,0:T(8,128)(2,1)S(1)} %collective-permute-done.3.refs_1_), channel_id=1, source_target_pairs={{0,1},{1,0},{2,3},{3,2},{4,5},{5,4},{6,7},{7,6},{8,9},{9,8},{10,11... | collective-permute-start | bytes 638984 | tf_op jit(solution)/shard_map/while/body/eval_jaxpr/ppermute | solution.py:36
  171.1 5.9 %collective-permute-start = (bf16[208,128]{1,0:T(8,128)(2,1)S(1)}, bf16[208,128]{1,0:T(8,128)(2,1)S(1)}, u32[]{:S(2)}, u32[]{:S(2)}) collective-permute-start(bf16[208,128]{1,0:T(8,128)(2,1)S(1)} %copy.33.refs_8_), channel_id=1, source_target_pairs={{0,2},{2,4},{4,6},{6,0},{1,3},{3,5},{5,7},{7,1},{8,10},{10,12},{12... | collective-permute-start | bytes 159752 | tf_op jit(solution)/shard_map/while/body/eval_jaxpr/ppermute | solution.py:18
  171.6 6.0 %collective-permute-start.1 = (bf16[208,128]{1,0:T(8,128)(2,1)S(1)}, bf16[208,128]{1,0:T(8,128)(2,1)S(1)}, u32[]{:S(2)}, u32[]{:S(2)}) collective-permute-start(bf16[208,128]{1,0:T(8,128)(2,1)S(1)} %copy.33.refs_8_), channel_id=1, source_target_pairs={{0,4},{2,6},{4,0},{6,2},{1,5},{3,7},{5,1},{7,3},{8,12},{10,14},{12... | collective-permute-start | bytes 159752 | tf_op jit(solution)/shard_map/while/body/eval_jaxpr/ppermute | solution.py:18
  178.8 8.3 %collective-permute-start.3 = (bf16[4,208,128]{2,1,0:T(8,128)(2,1)S(1)}, bf16[4,208,128]{2,1,0:T(8,128)(2,1)S(1)}, u32[]{:S(2)}, u32[]{:S(2)}) collective-permute-start(bf16[4,208,128]{2,1,0:T(8,128)(2,1)S(1)} %pad_maximum_fusion.4.refs_0_), channel_id=1, source_target_pairs={{0,24},{8,0},{16,8},{24,16},{1,25},{9,1},{17,9},{25,17},{2,26},{10... | collective-permute-start | bytes 638984 | tf_op jit(solution)/shard_map/while/body/eval_jaxpr/ppermute | solution.py:18
  179.8 9.7 %collective-permute-start.4 = (bf16[4,208,128]{2,1,0:T(8,128)(2,1)S(1)}, bf16[4,208,128]{2,1,0:T(8,128)(2,1)S(1)}, u32[]{:S(2)}, u32[]{:S(2)}) collective-permute-start(bf16[4,208,128]{2,1,0:T(8,128)(2,1)S(1)} %pad_maximum_fusion.4.refs_0_), channel_id=1, source_target_pairs={{0,16},{8,24},{16,0},{24,8},{1,17},{9,25},{17,1},{25,9},{2,18},{10... | collective-permute-start | bytes 638984 | tf_op jit(solution)/shard_map/while/body/eval_jaxpr/ppermute | solution.py:18
  179.9 11.9 %collective-permute-start.5 = (bf16[4,208,128]{2,1,0:T(8,128)(2,1)S(1)}, bf16[4,208,128]{2,1,0:T(8,128)(2,1)S(1)}, u32[]{:S(2)}, u32[]{:S(2)}) collective-permute-start(bf16[4,208,128]{2,1,0:T(8,128)(2,1)S(1)} %pad_maximum_fusion.4.refs_0_), channel_id=1, source_target_pairs={{0,8},{8,16},{16,24},{24,0},{1,9},{9,17},{17,25},{25,1},{2,10},{10... | collective-permute-start | bytes 638984 | tf_op jit(solution)/shard_map/while/body/eval_jaxpr/ppermute | solution.py:18
  180.9 11.0 %collective-permute-start.6 = (bf16[4,208,128]{2,1,0:T(8,128)(2,1)S(1)}, bf16[4,208,128]{2,1,0:T(8,128)(2,1)S(1)}, u32[]{:S(2)}, u32[]{:S(2)}) collective-permute-start(bf16[4,208,128]{2,1,0:T(8,128)(2,1)S(1)} %pad_maximum_fusion.4.refs_0_), channel_id=1, source_target_pairs={{0,1},{1,0},{2,3},{3,2},{4,5},{5,4},{6,7},{7,6},{8,9},{9,8},{10,11... | collective-permute-start | bytes 638984 | tf_op jit(solution)/shard_map/while/body/eval_jaxpr/ppermute | solution.py:36
  187.0 4.9 %collective-permute-start.7 = (bf16[4,208,128]{2,1,0:T(8,128)(2,1)S(1)}, bf16[4,208,128]{2,1,0:T(8,128)(2,1)S(1)}, u32[]{:S(2)}, u32[]{:S(2)}) collective-permute-start(bf16[4,208,128]{2,1,0:T(8,128)(2,1)S(1)} %collective-permute-done.3.refs_1_), channel_id=1, source_target_pairs={{0,1},{1,0},{2,3},{3,2},{4,5},{5,4},{6,7},{7,6},{8,9},{9,8},{10,11... | collective-permute-start | bytes 638984 | tf_op jit(solution)/shard_map/while/body/eval_jaxpr/ppermute | solution.py:36
  196.6 6.0 %collective-permute-start.35 = (bf16[208,128]{1,0:T(8,128)(2,1)S(1)}, bf16[208,128]{1,0:T(8,128)(2,1)S(1)}, u32[]{:S(2)}, u32[]{:S(2)}) collective-permute-start(bf16[208,128]{1,0:T(8,128)(2,1)S(1)} %get-tuple-element.194), channel_id=1, source_target_pairs={{0,64},{32,96},{64,0},{96,32},{1,65},{33,97},{65,1},{97,33},{2,66}... | collective-permute-start | bytes 159752 | tf_op jit(solution)/shard_map/ppermute | solution.py:68
  199.4 5.3 %collective-permute-start.36 = (bf16[208,128]{1,0:T(8,128)(2,1)S(1)}, bf16[208,128]{1,0:T(8,128)(2,1)S(1)}, u32[]{:S(2)}, u32[]{:S(2)}) collective-permute-start(bf16[208,128]{1,0:T(8,128)(2,1)S(1)} %get-tuple-element.193), channel_id=1, source_target_pairs={{0,32},{32,64},{64,96},{96,0},{1,33},{33,65},{65,97},{97,1},{2,34}... | collective-permute-start | bytes 159752 | tf_op jit(solution)/shard_map/ppermute | solution.py:68
  199.4 5.3 %collective-permute-start.34 = (bf16[208,128]{1,0:T(8,128)(2,1)S(1)}, bf16[208,128]{1,0:T(8,128)(2,1)S(1)}, u32[]{:S(2)}, u32[]{:S(2)}) collective-permute-start(bf16[208,128]{1,0:T(8,128)(2,1)S(1)} %get-tuple-element.195), channel_id=1, source_target_pairs={{0,96},{32,0},{64,32},{96,64},{1,97},{33,1},{65,33},{97,65},{2,98}... | collective-permute-start | bytes 159752 | tf_op jit(solution)/shard_map/ppermute | solution.py:68
  205.6 5.4 %collective-permute-start.42 = (bf16[208,128]{1,0:T(8,128)(2,1)S(1)}, bf16[208,128]{1,0:T(8,128)(2,1)S(1)}, u32[]{:S(2)}, u32[]{:S(2)}) collective-permute-start(bf16[208,128]{1,0:T(8,128)(2,1)S(1)} %get-tuple-element.162.refs_8_), channel_id=1, source_target_pairs={{0,2},{2,4},{4,6},{6,0},{1,3},{3,5},{5,7},{7,1},{8,10},{10,12},{12... | collective-permute-start | bytes 159752 | tf_op jit(solution)/shard_map/ppermute | solution.py:18
  206.4 5.6 %collective-permute-start.41 = (bf16[208,128]{1,0:T(8,128)(2,1)S(1)}, bf16[208,128]{1,0:T(8,128)(2,1)S(1)}, u32[]{:S(2)}, u32[]{:S(2)}) collective-permute-start(bf16[208,128]{1,0:T(8,128)(2,1)S(1)} %get-tuple-element.162.refs_8_), channel_id=1, source_target_pairs={{0,4},{2,6},{4,0},{6,2},{1,5},{3,7},{5,1},{7,3},{8,12},{10,14},{12... | collective-permute-start | bytes 159752 | tf_op jit(solution)/shard_map/ppermute | solution.py:18
  213.3 8.6 %collective-permute-start.43 = (bf16[4,208,128]{2,1,0:T(8,128)(2,1)S(1)}, bf16[4,208,128]{2,1,0:T(8,128)(2,1)S(1)}, u32[]{:S(2)}, u32[]{:S(2)}) collective-permute-start(bf16[4,208,128]{2,1,0:T(8,128)(2,1)S(1)} %pad_maximum_fusion.2.refs_0_), channel_id=1, source_target_pairs={{0,24},{8,0},{16,8},{24,16},{1,25},{9,1},{17,9},{25,17},{2,26},{10... | collective-permute-start | bytes 638984 | tf_op jit(solution)/shard_map/ppermute | solution.py:18
  214.1 10.6 %collective-permute-start.44 = (bf16[4,208,128]{2,1,0:T(8,128)(2,1)S(1)}, bf16[4,208,128]{2,1,0:T(8,128)(2,1)S(1)}, u32[]{:S(2)}, u32[]{:S(2)}) collective-permute-start(bf16[4,208,128]{2,1,0:T(8,128)(2,1)S(1)} %pad_maximum_fusion.2.refs_0_), channel_id=1, source_target_pairs={{0,16},{8,24},{16,0},{24,8},{1,17},{9,25},{17,1},{25,9},{2,18},{10... | collective-permute-start | bytes 638984 | tf_op jit(solution)/shard_map/ppermute | solution.py:18
  214.3 13.3 %collective-permute-start.45 = (bf16[4,208,128]{2,1,0:T(8,128)(2,1)S(1)}, bf16[4,208,128]{2,1,0:T(8,128)(2,1)S(1)}, u32[]{:S(2)}, u32[]{:S(2)}) collective-permute-start(bf16[4,208,128]{2,1,0:T(8,128)(2,1)S(1)} %pad_maximum_fusion.2.refs_0_), channel_id=1, source_target_pairs={{0,8},{8,16},{16,24},{24,0},{1,9},{9,17},{17,25},{25,1},{2,10},{10... | collective-permute-start | bytes 638984 | tf_op jit(solution)/shard_map/ppermute | solution.py:18
  216.1 15.4 %collective-permute-start.37 = (f32[1]{0:T(128)}, f32[1]{0:T(128)}, u32[]{:S(2)}, u32[]{:S(2)}) collective-permute-start(f32[1]{0:T(128)} %bitcast.39), channel_id=1, source_target_pairs={{0,64},{32,96},{64,0},{96,32},{1,65},{33,97},{65,1},{97,33},{2,66}... | collective-permute-start | bytes 20 | tf_op jit(solution)/shard_map/ppermute | solution.py:18
  217.8 24.1 %collective-permute-start.46 = (bf16[4,208,128]{2,1,0:T(8,128)(2,1)S(1)}, bf16[4,208,128]{2,1,0:T(8,128)(2,1)S(1)}, u32[]{:S(2)}, u32[]{:S(2)}) collective-permute-start(bf16[4,208,128]{2,1,0:T(8,128)(2,1)S(1)} %pad_maximum_fusion.2.refs_0_), channel_id=1, source_target_pairs={{0,1},{1,0},{2,3},{3,2},{4,5},{5,4},{6,7},{7,6},{8,9},{9,8},{10,11... | collective-permute-start | bytes 638984 | tf_op jit(solution)/shard_map/ppermute | solution.py:36
  221.9 20.1 %collective-permute-start.47 = (bf16[4,208,128]{2,1,0:T(8,128)(2,1)S(1)}, bf16[4,208,128]{2,1,0:T(8,128)(2,1)S(1)}, u32[]{:S(2)}, u32[]{:S(2)}) collective-permute-start(bf16[4,208,128]{2,1,0:T(8,128)(2,1)S(1)} %collective-permute-done.43.refs_1_), channel_id=1, source_target_pairs={{0,1},{1,0},{2,3},{3,2},{4,5},{5,4},{6,7},{7,6},{8,9},{9,8},{10,11... | collective-permute-start | bytes 638984 | tf_op jit(solution)/shard_map/ppermute | solution.py:36
  224.6 17.3 %collective-permute-start.48 = (bf16[4,208,128]{2,1,0:T(8,128)(2,1)S(1)}, bf16[4,208,128]{2,1,0:T(8,128)(2,1)S(1)}, u32[]{:S(2)}, u32[]{:S(2)}) collective-permute-start(bf16[4,208,128]{2,1,0:T(8,128)(2,1)S(1)} %collective-permute-done.44.refs_2_), channel_id=1, source_target_pairs={{0,1},{1,0},{2,3},{3,2},{4,5},{5,4},{6,7},{7,6},{8,9},{9,8},{10,11... | collective-permute-start | bytes 638984 | tf_op jit(solution)/shard_map/ppermute | solution.py:36
  227.6 14.3 %collective-permute-start.49 = (bf16[4,208,128]{2,1,0:T(8,128)(2,1)S(1)}, bf16[4,208,128]{2,1,0:T(8,128)(2,1)S(1)}, u32[]{:S(2)}, u32[]{:S(2)}) collective-permute-start(bf16[4,208,128]{2,1,0:T(8,128)(2,1)S(1)} %collective-permute-done.45.refs_3_), channel_id=1, source_target_pairs={{0,1},{1,0},{2,3},{3,2},{4,5},{5,4},{6,7},{7,6},{8,9},{9,8},{10,11... | collective-permute-start | bytes 638984 | tf_op jit(solution)/shard_map/ppermute | solution.py:36
  235.5 5.2 %collective-permute-start.39 = (f32[1]{0:T(128)}, f32[1]{0:T(128)}, u32[]{:S(2)}, u32[]{:S(2)}) collective-permute-start(f32[1]{0:T(128)} %bitcast.39), channel_id=1, source_target_pairs={{0,32},{32,64},{64,96},{96,0},{1,33},{33,65},{65,97},{97,1},{2,34}... | collective-permute-start | bytes 20 | tf_op jit(solution)/shard_map/ppermute | solution.py:18
  246.1 20.2 %collective-permute-start.51 = (bf16[208,128]{1,0:T(8,128)(2,1)}, bf16[208,128]{1,0:T(8,128)(2,1)S(1)}, u32[]{:S(2)}, u32[]{:S(2)}) collective-permute-start(bf16[208,128]{1,0:T(8,128)(2,1)} %get-tuple-element.191), channel_id=1, source_target_pairs={{0,64},{32,96},{64,0},{96,32},{1,65},{33,97},{65,1},{97,33},{2,66}... | collective-permute-start | bytes 159752 | tf_op jit(solution)/shard_map/ppermute | solution.py:68
  247.1 19.2 %collective-permute-start.52 = (bf16[208,128]{1,0:T(8,128)(2,1)}, bf16[208,128]{1,0:T(8,128)(2,1)S(1)}, u32[]{:S(2)}, u32[]{:S(2)}) collective-permute-start(bf16[208,128]{1,0:T(8,128)(2,1)} %get-tuple-element.211), channel_id=1, source_target_pairs={{0,32},{32,64},{64,96},{96,0},{1,33},{33,65},{65,97},{97,1},{2,34}... | collective-permute-start | bytes 159752 | tf_op jit(solution)/shard_map/ppermute | solution.py:68
  249.0 17.3 %collective-permute-start.50 = (bf16[208,128]{1,0:T(8,128)(2,1)}, bf16[208,128]{1,0:T(8,128)(2,1)S(1)}, u32[]{:S(2)}, u32[]{:S(2)}) collective-permute-start(bf16[208,128]{1,0:T(8,128)(2,1)} %get-tuple-element.192), channel_id=1, source_target_pairs={{0,96},{32,0},{64,32},{96,64},{1,97},{33,1},{65,33},{97,65},{2,98}... | collective-permute-start | bytes 159752 | tf_op jit(solution)/shard_map/ppermute | solution.py:68
  267.3 4.2 %collective-permute-start.55 = (f32[106,128]{1,0:T(8,128)S(1)}, f32[106,128]{1,0:T(8,128)S(1)}, u32[]{:S(2)}, u32[]{:S(2)}) collective-permute-start(f32[106,128]{1,0:T(8,128)S(1)} %fusion.26), channel_id=1, source_target_pairs={{0,6},{2,0},{4,2},{6,4},{1,7},{3,1},{5,3},{7,5},{8,14},{10,8},{12,... | collective-permute-start | bytes 162824 | tf_op jit(solution)/shard_map/ppermute | solution.py:18
  269.2 6.2 %collective-permute-start.56 = (f32[106,128]{1,0:T(8,128)S(1)}, f32[106,128]{1,0:T(8,128)S(1)}, u32[]{:S(2)}, u32[]{:S(2)}) collective-permute-start(f32[106,128]{1,0:T(8,128)S(1)} %fusion.26), channel_id=1, source_target_pairs={{0,2},{2,4},{4,6},{6,0},{1,3},{3,5},{5,7},{7,1},{8,10},{10,12},{12... | collective-permute-start | bytes 162824 | tf_op jit(solution)/shard_map/ppermute | solution.py:18
  269.4 6.1 %collective-permute-start.54 = (f32[106,128]{1,0:T(8,128)S(1)}, f32[106,128]{1,0:T(8,128)S(1)}, u32[]{:S(2)}, u32[]{:S(2)}) collective-permute-start(f32[106,128]{1,0:T(8,128)S(1)} %fusion.26), channel_id=1, source_target_pairs={{0,4},{2,6},{4,0},{6,2},{1,5},{3,7},{5,1},{7,3},{8,12},{10,14},{12... | collective-permute-start | bytes 162824 | tf_op jit(solution)/shard_map/ppermute | solution.py:18
  275.5 4.7 %collective-permute-start.58 = (f32[106,128]{1,0:T(8,128)S(1)}, f32[106,128]{1,0:T(8,128)S(1)}, u32[]{:S(2)}, u32[]{:S(2)}) collective-permute-start(f32[106,128]{1,0:T(8,128)S(1)} %add_add_fusion.1), channel_id=1, source_target_pairs={{0,24},{8,0},{16,8},{24,16},{1,25},{9,1},{17,9},{25,17},{2,26},{10... | collective-permute-start | bytes 162824 | tf_op jit(solution)/shard_map/ppermute | solution.py:18
  277.1 5.4 %collective-permute-start.59 = (f32[106,128]{1,0:T(8,128)S(1)}, f32[106,128]{1,0:T(8,128)S(1)}, u32[]{:S(2)}, u32[]{:S(2)}) collective-permute-start(f32[106,128]{1,0:T(8,128)S(1)} %add_add_fusion.1), channel_id=1, source_target_pairs={{0,8},{8,16},{16,24},{24,0},{1,9},{9,17},{17,25},{25,1},{2,10},{10... | collective-permute-start | bytes 162824 | tf_op jit(solution)/shard_map/ppermute | solution.py:18
  277.6 5.7 %collective-permute-start.57 = (f32[106,128]{1,0:T(8,128)S(1)}, f32[106,128]{1,0:T(8,128)S(1)}, u32[]{:S(2)}, u32[]{:S(2)}) collective-permute-start(f32[106,128]{1,0:T(8,128)S(1)} %add_add_fusion.1), channel_id=1, source_target_pairs={{0,16},{8,24},{16,0},{24,8},{1,17},{9,25},{17,1},{25,9},{2,18},{10... | collective-permute-start | bytes 162824 | tf_op jit(solution)/shard_map/ppermute | solution.py:18
  (23 other events, 438.9 us)
Sparse Core Ops, SparseCore 0:
  9.7 108.2 all-gather.2
  205.7 50.7 all-gather.4
where the time goes:
time: 302 us; the launch traced here: 301 us
  waiting for transfers between devices  133 us (44%)
  starting transfers between devices  79.5 us (26%)
  Pallas kernels  31.4 us (10%)
  between operations  20 us (7%)
  other arithmetic  16.6 us (5%)
  matrix products  16.1 us (5%)
  local copies, waits for them, and re-layouts  4.57 us (2%)
    ppermute x47, waiting for transfers between devices, from_ring(): lax.ppermute(block, axis, [(i, (i - step) % size) for i in range(size)])  84.6 us
    ppermute x47, starting transfers between devices, from_ring(): lax.ppermute(block, axis, [(i, (i - step) % size) for i in range(size)])  60.3 us
    all_gather x1, waiting for transfers between devices, body(): all_weights = lax.all_gather(local_weight, 'x', axis=0)  16.2 us
    ppermute x6, waiting for transfers between devices, scattered(): lax.ppermute(blocks[step], axis, [(i, (i + step) % size) for i in range(s...  15.8 us
    pallas_call x4, Pallas kernels, layer_back(): pl.pallas_call(layer_kernel, grid_spec=pltpu.PrefetchScalarGridSpec(num_s...  13.4 us
    pallas_call x1, Pallas kernels, head_logits(): pl.pallas_call(logits_kernel, grid_spec=pltpu.PrefetchScalarGridSpec(num_...  12.9 us
    dot_general x1, matrix products, body(): lax.dot_general(both, head_weight, (((0,), (1,)), ((), ())), preferred_el...  10.8 us
    ppermute x6, starting transfers between devices, exchanged(): lax.ppermute(piece, axis, [(i, (i + step) % size) for i in range(size)])  10.3 us
  transfers between devices with their start and end apart: 82, of which 52 were waited for; matrix products, arithmetic and copies ran while one was open for 10% of the time, Pallas kernels for 7%

commit v1 on v0

--- a/solution.py
+++ b/solution.py
@@ -203,6 +203,112 @@
     )(where, *pieces, carried, all_weights)
 
 
+def statistics_kernel(saved_ref, full_ref, row_ref, weight_ref, gradient_ref, row_new_ref, totals_ref, rows_ref, weights_ref):
+    step = pl.program_id(0)
+    tile = full_ref.shape[0]
+    width = gradient_ref.shape[1]
+
+    def lanes(x):
+        return sum(x[:, at : at + 128] for at in range(0, x.shape[1], 128))
+
+    @pl.when(step == 0)
+    def _():
+        rows_ref[...] = jnp.zeros_like(rows_ref)
+        weights_ref[...] = jnp.zeros_like(weights_ref)
+
+    gradient = lax.dot_general(
+        saved_ref[...], full_ref[...], (((1,), (1,)), ((), ())), preferred_element_type=jnp.float32
+    )
+    here = pl.ds(pl.multiple_of(step * tile, tile), tile)
+    gradient_ref[:, here] = gradient
+    squares = gradient * gradient + tiny_term
+    totals_ref[0:1, here] = jnp.sum(squares, axis=0, keepdims=True)
+    rows_ref[...] += lanes(squares)
+    weight = weight_ref[...].astype(jnp.float32)
+    weights_ref[...] += lanes(weight * weight)
+
+    @pl.when(step == pl.num_programs(0) - 1)
+    def _():
+        mean = jnp.sum(rows_ref[...], axis=1, keepdims=True) / width
+        row_new = decay_rate * row_ref[...] + (1.0 - decay_rate) * mean
+        row_new_ref[...] = row_new
+        inverse = jnp.broadcast_to(1.0 / row_new, rows_ref.shape)
+        for at in range(0, width, 128):
+            block = gradient_ref[:, at : at + 128]
+            totals_ref[1:2, at : at + 128] = jnp.sum(block * block * inverse, axis=0, keepdims=True)
+        row_total = jnp.sum(row_new, axis=0, keepdims=True)
+        weight_total = jnp.sum(jnp.sum(weights_ref[...], axis=0, keepdims=True), axis=1, keepdims=True)
+        totals_ref[0:1, width:] = jnp.broadcast_to(row_total, (1, 128))
+        totals_ref[1:2, width:] = jnp.broadcast_to(weight_total, (1, 128))
+
+
+def gradient_statistics(saved, full, row_state, weight, tile=512):
+    rows, tokens = saved.shape
+    width = full.shape[0]
+    whole = lambda shape: pl.BlockSpec(shape, lambda i: (0,) * len(shape))
+    return pl.pallas_call(
+        statistics_kernel,
+        grid=(width // tile,),
+        in_specs=[
+            whole(saved.shape),
+            pl.BlockSpec((tile, tokens), lambda i: (i, 0)),
+            whole(row_state.shape),
+            pl.BlockSpec((rows, tile), lambda i: (0, i)),
+        ],
+        out_specs=[whole((rows, width)), whole((rows, 1)), whole((2, width + 128))],
+        out_shape=[
+            jax.ShapeDtypeStruct((rows, width), jnp.float32),
+            jax.ShapeDtypeStruct((rows, 1), jnp.float32),
+            jax.ShapeDtypeStruct((2, width + 128), jnp.float32),
+        ],
+        scratch_shapes=[pltpu.VMEM((rows, 128), jnp.float32), pltpu.VMEM((rows, 128), jnp.float32)],
+        compiler_params=pltpu.CompilerParams(vmem_limit_bytes=wide_vmem),
+    )(saved, full, row_state, weight)
+
+
+def weights_kernel(totals_ref, row_new_ref, col_ref, gradient_ref, weight_ref, out_ref, col_new_ref, rows_ref, cols_ref):
+    step = pl.program_id(0)
+    tile = weight_ref.shape[1]
+    width = col_ref.shape[1]
+
+    @pl.when(step == 0)
+    def _():
+        entries = float(width) * float(width)
+        col_new = decay_rate * col_ref[...] + (1.0 - decay_rate) * (totals_ref[0:1, :width] / width)
+        col_new_ref[...] = col_new
+        cols_ref[...] = 1.0 / jnp.sqrt(col_new)
+        row_total = totals_ref[0:1, width : width + 1]
+        weight_total = totals_ref[1:2, width : width + 1]
+        update_total = row_total * jnp.sum(totals_ref[1:2, :width] / col_new, axis=1, keepdims=True)
+        factor = learn_rate * jnp.sqrt(weight_total / entries)
+        factor = factor / jnp.maximum(1.0, jnp.sqrt(update_total / entries))
+        rows_ref[...] = jnp.broadcast_to(factor * jnp.sqrt(row_total / row_new_ref[...]), rows_ref.shape)
+
+    for at in range(0, tile, 128):
+        here = pl.ds(pl.multiple_of(step * tile + at, 128), 128)
+        change = gradient_ref[:, at : at + 128] * rows_ref[...] * cols_ref[:, here]
+        weight = weight_ref[:, at : at + 128].astype(jnp.float32)
+        out_ref[:, at : at + 128] = (weight - change).astype(jnp.bfloat16)
+
+
+def updated_weights(totals, row_new, col_state, gradient, weight, tile=512):
+    rows, width = weight.shape
+    whole = lambda shape: pl.BlockSpec(shape, lambda i: (0,) * len(shape))
+    block = pl.BlockSpec((rows, tile), lambda i: (0, i))
+    return pl.pallas_call(
+        weights_kernel,
+        grid=(width // tile,),
+        in_specs=[whole(totals.shape), whole(row_new.shape), whole(col_state.shape), block, block],
+        out_specs=[block, whole(col_state.shape)],
+        out_shape=[
+            jax.ShapeDtypeStruct((rows, width), jnp.bfloat16),
+            jax.ShapeDtypeStruct(col_state.shape, jnp.float32),
+        ],
+        scratch_shapes=[pltpu.VMEM((rows, 128), jnp.float32), pltpu.VMEM((1, width), jnp.float32)],
+        compiler_params=pltpu.CompilerParams(vmem_limit_bytes=wide_vmem),
+    )(totals, row_new, col_state, gradient, weight)
+
+
 def body(hidden_last, labels, head_weight, layer_inputs, weights, row_state, col_state):
     section_count = lax.axis_size("x")
     section_index = lax.axis_index("x")
@@ -213,7 +319,6 @@
     saved_all = layer_inputs[0]
     share = all_rows // section_count
     row_start = section_index * share
-    entries = float(model_width * model_width)
     tensor_index = lax.axis_index(("y", "z", "c"))
 
     def where(layer):
@@ -242,51 +347,24 @@
     part = scattered([part[0]] + [part[k].astype(jnp.bfloat16) for k in range(1, 4)], "z")
     carried = part.astype(jnp.bfloat16)
 
-    def advance(step, state):
-        carried, chain = state
-        layer = section_count - 1 - step
+    chain = [carried]
+    for layer in reversed(range(1, section_count)):
         carried = layer_back(where(layer), carried, all_weights)
-        return carried, lax.dynamic_update_index_in_dim(chain, carried, layer, 0)
-
-    chain = jnp.zeros((section_count + 1, *carried.shape), jnp.bfloat16)
-    chain = chain.at[section_count].set(carried)
-    carried, chain = lax.fori_loop(0, section_count - 1, advance, (carried, chain))
-
-    dy = exchanged([chain[k + 1] for k in range(section_count)], "x").reshape(rows_local, all_rows)
-    dy, carried, local_weight, sums = lax.optimization_barrier((dy, carried, local_weight, sums))
+        chain.insert(0, carried)
+
+    dy = exchanged(chain, "x").reshape(rows_local, all_rows)
     full = lax.all_gather(dy, ("y", "z", "c"), axis=0, tiled=True)
-    carried = layer_back(where(0), carried, all_weights)
-    outputs = exchanged([carried] + [chain[k] for k in range(1, section_count)], "x")
-    outputs = outputs.reshape(rows_local, all_rows)
-    loss = summed(jnp.sum(jnp.log(sums[0]) - sums[1])[None], "x")[0] / all_rows
-    gradient = lax.dot_general(
-        saved_all, full, (((0,), (1,)), ((), ())), preferred_element_type=jnp.float32
-    )
-
-    squares = gradient * gradient
-    row_new = decay_rate * row_state[0] + (1.0 - decay_rate) * jnp.mean(squares + tiny_term, axis=1)
-    col_part = jnp.sum(squares + tiny_term, axis=0)
-    scaled_part = jnp.sum(squares * (1.0 / row_new)[:, None], axis=0)
-    weight_float = local_weight.astype(jnp.float32)
-    weight_part = jnp.broadcast_to(jnp.sum(weight_float * weight_float), (128,))
-    row_part = jnp.broadcast_to(jnp.sum(row_new), (128,))
-    payload = jnp.concatenate([col_part, scaled_part, row_part, weight_part]).reshape(-1, 128)
-    payload = summed_tensor(payload).reshape(-1)
-    col_sum = payload[:model_width]
-    scaled_sum = payload[model_width : 2 * model_width]
-    row_total = payload[2 * model_width]
-    weight_total = payload[2 * model_width + 128]
-    col_new = decay_rate * col_state[0] + (1.0 - decay_rate) * (col_sum / model_width)
-    update_total = row_total * jnp.sum(scaled_sum / col_new)
-    factor = (
-        learn_rate
-        * jnp.sqrt(weight_total / entries)
-        / jnp.maximum(1.0, jnp.sqrt(update_total / entries))
-    )
-    row_scale = factor * jnp.sqrt(row_total / row_new)
-    col_scale = 1.0 / jnp.sqrt(col_new)
-    new_weight = (weight_float - gradient * row_scale[:, None] * col_scale[None, :]).astype(jnp.bfloat16)
-    return (loss, outputs.T[None], new_weight[None], row_new[None], col_new[None])
+    loss = jnp.sum(jnp.log(sums[0]) - sums[1])[None]
+    for distance in (1, 2):
+        loss = loss + lax.ppermute(loss, "x", [(i, i ^ distance) for i in range(section_count)])
+    loss = loss[0] / all_rows
+    full, loss = lax.optimization_barrier((full, loss))
+    gradient, row_new, totals = gradient_statistics(saved_all.T, full, row_state.T, local_weight)
+    totals = summed_tensor(totals)
+    backward = jnp.dot(local_weight, full, preferred_element_type=jnp.float32)
+    outputs = (dy.astype(jnp.float32) + backward).astype(jnp.bfloat16)
+    new_weight, col_new = updated_weights(totals, row_new, col_state, gradient, local_weight)
+    return (loss, outputs.T[None], new_weight[None], row_new.T, col_new)
 
 
 def solution(mesh):

time: 302 us -> 285 us (0.944)
  Pallas kernels: 31.4 us -> 51.9 us
  other arithmetic: 16.6 us -> 2.75 us
  starting transfers between devices: 79.5 us -> 66.8 us
  local copies, waits for them, and re-layouts: 4.57 us -> 1.45 us
    all_gather x1, waiting for transfers between devices: 6.13 us -> 37.2 us  [body(): full = lax.all_gather(dy, ('y', 'z', 'c'), axis=0, tiled=True)]
    pallas_call x0 -> x2, Pallas kernels: none -> 23.4 us  [the longest x1 14 us: gradient_statistics(): pl.pallas_call(statistics_kernel, grid=(width // tile,), in_specs=[whole(...]
    ppermute x47 -> x38, waiting for transfers between devices: 84.6 us -> 61.7 us  [from_ring(): lax.ppermute(block, axis, [(i, (i - step) % size) for i in range(size)])]
    all_gather x1, waiting for transfers between devices: 16.2 us -> 0.01 us  [body(): all_weights = lax.all_gather(local_weight, 'x', axis=0)]
    ppermute x47 -> x38, starting transfers between devices: 60.3 us -> 47.9 us  [from_ring(): lax.ppermute(block, axis, [(i, (i - step) % size) for i in range(size)])]
    broadcast_in_dim x2 -> x0, other arithmetic: 5.83 us -> none  [the longest x1 5.12 us: body(): new_weight[None]]
    reduce_sum x4 -> x1, other arithmetic: 6.04 us -> 0.61 us  [body(): loss = jnp.sum(jnp.log(sums[0]) - sums[1])[None]]
    ppermute x0 -> x2, waiting for transfers between devices: none -> 4.96 us  [body(): lax.ppermute(loss, 'x', [(i, i ^ distance) for i in range(section_count)])]
  transfers between devices with their start and end apart: 82 -> 68, of which waited for: 52 -> 43; matrix products, arithmetic and copies ran while one was open for 10% -> 6% of each run, Pallas kernels for 7% -> 6%
where the time goes in v1:
time: 285 us; the launch traced here: 284 us
  waiting for transfers between devices  130 us (46%)
  starting transfers between devices  66.8 us (23%)
  Pallas kernels  51.9 us (18%)
  between operations  17.3 us (6%)
  matrix products  13.2 us (5%)
    ppermute x38, waiting for transfers between devices, from_ring(): lax.ppermute(block, axis, [(i, (i - step) % size) for i in range(size)])  61.7 us
    ppermute x38, starting transfers between devices, from_ring(): lax.ppermute(block, axis, [(i, (i - step) % size) for i in range(size)])  47.9 us
    all_gather x1, waiting for transfers between devices, body(): full = lax.all_gather(dy, ('y', 'z', 'c'), axis=0, tiled=True)  37.2 us
    ppermute x6, waiting for transfers between devices, scattered(): lax.ppermute(blocks[step], axis, [(i, (i + step) % size) for i in range(s...  15.8 us
    pallas_call x1, Pallas kernels, gradient_statistics(): pl.pallas_call(statistics_kernel, grid=(width // tile,), in_specs=[whole(...  14 us
    pallas_call x1, Pallas kernels, head_logits(): pl.pallas_call(logits_kernel, grid_spec=pltpu.PrefetchScalarGridSpec(num_...  12.9 us
    dot_general x1, matrix products, body(): lax.dot_general(both, head_weight, (((0,), (1,)), ((), ())), preferred_el...  10.8 us
    pallas_call x3, Pallas kernels, layer_back(): pl.pallas_call(layer_kernel, grid_spec=pltpu.PrefetchScalarGridSpec(num_s...  10.6 us
  transfers between devices with their start and end apart: 68, of which 43 were waited for; matrix products, arithmetic and copies ran while one was open for 6% of the time, Pallas kernels for 6%

profile of v1, /device:TPU:0, one launch (start us, length us, event | category | flops | bytes accessed | tf_op | source)
XLA Modules:
  0.0 283.8 jit_solution(6546243871195196646)
XLA Ops:
  8.8 2.1 collective-permute-start.2
  10.9 3.6 %collective-permute-start.1 = (bf16[208,128]{1,0:T(8,128)(2,1)S(1)}, bf16[208,128]{1,0:T(8,128)(2,1)S(1)}, u32[]{:S(2)}, u32[]{:S(2)}) collective-permute-start(bf16[208,128]{1,0:T(8,128)(2,1)S(1)} %get-tuple-element.46), channel_id=1, source_target_pairs={{0,4},{2,6},{4,0},{6,2},{1,5},{3,7},{5,1},{7,3},{8,12},{10,14},{12... | collective-permute-start | bytes 159752 | tf_op jit(solution)/shard_map/ppermute | solution.py:18
  15.5 1.7 collective-permute-done.1
  17.1 1.4 collective-permute-done
  18.6 3.1 %collective-permute-start.3 = (bf16[4,208,128]{2,1,0:T(8,128)(2,1)S(1)}, bf16[4,208,128]{2,1,0:T(8,128)(2,1)S(1)}, u32[]{:S(2)}, u32[]{:S(2)}) collective-permute-start(bf16[4,208,128]{2,1,0:T(8,128)(2,1)S(1)} %pad_maximum_fusion.refs_0_), channel_id=1, source_target_pairs={{0,24},{8,0},{16,8},{24,16},{1,25},{9,1},{17,9},{25,17},{2,26},{10... | collective-permute-start | bytes 638984 | tf_op jit(solution)/shard_map/ppermute | solution.py:18
  23.3 6.1 %collective-permute-done.3.refs_1_ = bf16[4,208,128]{2,1,0:T(8,128)(2,1)S(1)} collective-permute-done((bf16[4,208,128]{2,1,0:T(8,128)(2,1)S(1)}, bf16[4,208,128]{2,1,0:T(8,128)(2,1)S(1)}, u32[]{:S(2)}, u32[]{:S(2)}) %collective-permute-start.3) | collective-permute-done | bytes 213024 | tf_op jit(solution)/shard_map/ppermute | solution.py:18
  29.4 1.5 collective-permute-done.4.refs_2_
  30.9 2.2 collective-permute-done.5.refs_3_
  33.3 1.3 collective-permute-done.9.refs_7_
  34.6 12.9 %shard_map.110 = (bf16[1000,256]{1,0:T(8,128)(2,1)S(1)}, f32[2,128]{1,0:T(2,128)S(1)}) custom-call(s32[6]{0:T(128)S(1)} %stack.121.place_ref, bf16[4,208,128]{2,1,0:T(8,128)(2,1)S(1)} %pad_maximum_fusion.refs_0_, bf16[4,208,128]{2,1,0:T(8,128)(2,1)S(1)} %collective-permute-done.3.refs_1_, bf16[4,208,128]{2,1,0:T(8,128)(2,1)S(1)} %collective-permute-done.4.refs_2_, ...), custom_call_target="tpu_custom_call" | custom-call | tf_op jit(solution)/shard_map/pallas_call | solution.py:115
  48.7 2.1 collective-permute-start.12
  50.8 1.5 collective-permute-start.11
  52.3 3.3 %collective-permute-done.13 = f32[2,128]{1,0:T(2,128)S(1)} collective-permute-done((f32[2,128]{1,0:T(2,128)S(1)}, f32[2,128]{1,0:T(2,128)S(1)}, u32[]{:S(2)}, u32[]{:S(2)}) %collective-permute-start.13) | collective-permute-done | bytes 1056 | tf_op jit(solution)/shard_map/ppermute | solution.py:18
  56.4 1.4 collective-permute-start.16
  58.5 10.8 %fusion.14.product_ref = f32[256,6656]{1,0:T(8,128)} fusion(bf16[1000,256]{1,0:T(8,128)(2,1)S(1)} %get-tuple-element.16, bf16[6656,1000]{0,1:T(8,128)(2,1)} %param.9), kind=kOutput, calls=%fused_computation.45 | convolution fusion | flops 3407872000 | bytes 20639744 | tf_op jit(solution)/shard_map/dot_general | solution.py:341
  69.3 5.1 %shard_map.111 = (f32[4,4,208,128]{3,2,1,0:T(8,128)S(1)}, bf16[4,4,208,128]{3,2,1,0:T(8,128)(2,1)S(1)}) custom-call(s32[6]{0:T(128)S(1)} %stack.121.place_ref, f32[256,6656]{1,0:T(8,128)} %fusion.14.product_ref, f32[2,128]{1,0:T(2,128)S(1)} %add_add_fusion.2.sums_ref), custom_call_target="tpu_custom_call" | custom-call | tf_op jit(solution)/shard_map/pallas_call | solution.py:157
  74.5 2.4 collective-permute-done.17
  77.2 2.1 collective-permute-start.20
  79.3 2.0 collective-permute-start.19
  81.6 7.1 %collective-permute-done.20 = bf16[4,208,128]{2,1,0:T(8,128)(2,1)S(1)} collective-permute-done((bf16[4,208,128]{2,1,0:T(8,128)(2,1)S(1)}, bf16[4,208,128]{2,1,0:T(8,128)(2,1)S(1)}, u32[]{:S(2)}, u32[]{:S(2)}) %collective-permute-start.20) | collective-permute-done | bytes 213024 | tf_op jit(solution)/shard_map/ppermute | solution.py:54
  89.0 3.4 %collective-permute-done.18 = bf16[4,208,128]{2,1,0:T(8,128)(2,1)S(1)} collective-permute-done((bf16[4,208,128]{2,1,0:T(8,128)(2,1)S(1)}, bf16[4,208,128]{2,1,0:T(8,128)(2,1)S(1)}, u32[]{:S(2)}, u32[]{:S(2)}) %collective-permute-start.18) | collective-permute-done | bytes 213024 | tf_op jit(solution)/shard_map/ppermute | solution.py:54
  92.6 3.3 %collective-permute-start.23 = (bf16[208,128]{1,0:T(8,128)(2,1)S(1)}, bf16[208,128]{1,0:T(8,128)(2,1)S(1)}, u32[]{:S(2)}, u32[]{:S(2)}) collective-permute-start(bf16[208,128]{1,0:T(8,128)(2,1)S(1)} %get-tuple-element.43), channel_id=1, source_target_pairs={{0,6},{2,0},{4,2},{6,4},{1,7},{3,1},{5,3},{7,5},{8,14},{10,8},{12,... | collective-permute-start | bytes 159752 | tf_op jit(solution)/shard_map/ppermute | solution.py:54
  96.8 1.6 collective-permute-done.23
  98.4 3.2 %collective-permute-done.22 = bf16[208,128]{1,0:T(8,128)(2,1)S(1)} collective-permute-done((bf16[208,128]{1,0:T(8,128)(2,1)S(1)}, bf16[208,128]{1,0:T(8,128)(2,1)S(1)}, u32[]{:S(2)}, u32[]{:S(2)}) %collective-permute-start.22) | collective-permute-done | bytes 53280 | tf_op jit(solution)/shard_map/ppermute | solution.py:54
  102.1 2.3 collective-permute-start.25
  104.4 2.0 collective-permute-start.24
  106.4 1.5 collective-permute-done.26
  109.6 2.0 collective-permute-start.28
  112.1 4.3 %collective-permute-done.27.refs_1_ = bf16[4,208,128]{2,1,0:T(8,128)(2,1)S(1)} collective-permute-done((bf16[4,208,128]{2,1,0:T(8,128)(2,1)S(1)}, bf16[4,208,128]{2,1,0:T(8,128)(2,1)S(1)}, u32[]{:S(2)}, u32[]{:S(2)}) %collective-permute-start.27) | collective-permute-done | bytes 213024 | tf_op jit(solution)/shard_map/ppermute | solution.py:18
  116.5 1.7 collective-permute-done.28.refs_2_
  118.2 2.2 collective-permute-done.29.refs_3_
  120.4 1.4 collective-permute-done.33.refs_7_
  121.8 3.3 %shard_map.112.refs_8_ = bf16[208,128]{1,0:T(8,128)(2,1)S(1)} custom-call(s32[6]{0:T(128)S(1)} %stack.120.place_ref, bf16[4,208,128]{2,1,0:T(8,128)(2,1)S(1)} %pad_maximum_fusion.1.refs_0_, bf16[4,208,128]{2,1,0:T(8,128)(2,1)S(1)} %collective-permute-done.27.refs_1_, bf16[4,208,128]{2,1,0:T(8,128)(2,1)S(1)} %collective-permute-done.28.refs_2_, ...), custom_call_target="tpu_custom_call" | custom-call | tf_op jit(solution)/shard_map/pallas_call | solution.py:188
  125.1 1.2 collective-permute-start.36
  126.4 3.0 %collective-permute-start.35 = (bf16[208,128]{1,0:T(8,128)(2,1)S(1)}, bf16[208,128]{1,0:T(8,128)(2,1)S(1)}, u32[]{:S(2)}, u32[]{:S(2)}) collective-permute-start(bf16[208,128]{1,0:T(8,128)(2,1)S(1)} %shard_map.112.refs_8_), channel_id=1, source_target_pairs={{0,4},{2,6},{4,0},{6,2},{1,5},{3,7},{5,1},{7,3},{8,12},{10,14},{12... | collective-permute-start | bytes 159752 | tf_op jit(solution)/shard_map/ppermute | solution.py:18
  130.5 1.8 collective-permute-done.35
  133.5 1.4 collective-permute-start.37
  136.6 5.2 %collective-permute-done.37.refs_1_ = bf16[4,208,128]{2,1,0:T(8,128)(2,1)S(1)} collective-permute-done((bf16[4,208,128]{2,1,0:T(8,128)(2,1)S(1)}, bf16[4,208,128]{2,1,0:T(8,128)(2,1)S(1)}, u32[]{:S(2)}, u32[]{:S(2)}) %collective-permute-start.37) | collective-permute-done | bytes 213024 | tf_op jit(solution)/shard_map/ppermute | solution.py:18
  141.7 2.7 collective-permute-done.38.refs_2_
  144.5 2.2 collective-permute-done.39.refs_3_
  146.8 1.4 collective-permute-done.43.refs_7_
  148.2 3.3 %shard_map.113.refs_8_ = bf16[208,128]{1,0:T(8,128)(2,1)S(1)} custom-call(s32[6]{0:T(128)S(1)} %stack.132.place_ref, bf16[4,208,128]{2,1,0:T(8,128)(2,1)S(1)} %pad_maximum_fusion.2.refs_0_, bf16[4,208,128]{2,1,0:T(8,128)(2,1)S(1)} %collective-permute-done.37.refs_1_, bf16[4,208,128]{2,1,0:T(8,128)(2,1)S(1)} %collective-permute-done.38.refs_2_, ...), custom_call_target="tpu_custom_call" | custom-call | tf_op jit(solution)/shard_map/pallas_call | solution.py:188
  151.7 3.3 %collective-permute-start.45 = (bf16[208,128]{1,0:T(8,128)(2,1)S(1)}, bf16[208,128]{1,0:T(8,128)(2,1)S(1)}, u32[]{:S(2)}, u32[]{:S(2)}) collective-permute-start(bf16[208,128]{1,0:T(8,128)(2,1)S(1)} %shard_map.113.refs_8_), channel_id=1, source_target_pairs={{0,4},{2,6},{4,0},{6,2},{1,5},{3,7},{5,1},{7,3},{8,12},{10,14},{12... | collective-permute-start | bytes 159752 | tf_op jit(solution)/shard_map/ppermute | solution.py:18
  155.7 1.7 collective-permute-done.46
  161.3 6.2 %collective-permute-done.47.refs_1_ = bf16[4,208,128]{2,1,0:T(8,128)(2,1)} collective-permute-done((bf16[4,208,128]{2,1,0:T(8,128)(2,1)S(1)}, bf16[4,208,128]{2,1,0:T(8,128)(2,1)}, u32[]{:S(2)}, u32[]{:S(2)}) %collective-permute-start.47) | collective-permute-done | bytes 213024 | tf_op jit(solution)/shard_map/ppermute | solution.py:18
  167.5 2.1 collective-permute-done.48.refs_2_
  169.6 2.3 collective-permute-done.49.refs_3_
  172.0 1.7 collective-permute-done.53.refs_7_
  173.7 3.9 %shard_map.114 = bf16[208,128]{1,0:T(8,128)(2,1)S(1)} custom-call(s32[6]{0:T(128)S(1)} %stack.138.place_ref, bf16[4,208,128]{2,1,0:T(8,128)(2,1)S(1)} %pad_maximum_fusion.3.refs_0_, bf16[4,208,128]{2,1,0:T(8,128)(2,1)} %collective-permute-done.47.refs_1_, bf16[4,208,128]{2,1,0:T(8,128)(2,1)} %collective-permute-done.48.refs_2_, ...), custom_call_target="tpu_custom_call" | custom-call | tf_op jit(solution)/shard_map/pallas_call | solution.py:188
  177.6 2.7 collective-permute-start.55
  181.3 2.3 collective-permute-start.54
  183.6 2.1 collective-permute-done.56
  187.3 3.8 %collective-permute-done.57 = f32[1]{0:T(128)} collective-permute-done((f32[1]{0:T(128)}, f32[1]{0:T(128)}, u32[]{:S(2)}, u32[]{:S(2)}) %collective-permute-start.57) | collective-permute-done | bytes 36 | tf_op jit(solution)/shard_map/ppermute | solution.py:359
  192.3 4.0 %collective-permute-start.58 = (f32[1]{0:T(128)}, f32[1]{0:T(128)}, u32[]{:S(2)}, u32[]{:S(2)}) collective-permute-start(f32[1]{0:T(128)} %add.99), channel_id=1, source_target_pairs={{0,64},{32,96},{64,0},{96,32},{1,65},{33,97},{65,1},{97,33},{2,66}... | collective-permute-start | bytes 20 | tf_op jit(solution)/shard_map/ppermute | solution.py:359
  196.3 1.2 collective-permute-done.58
  198.1 37.2 %all-gather.5.cloned.1.call-done.full_ref = bf16[6656,512]{1,0:T(8,128)(2,1)} async-done(((bf16[208,512]{1,0:T(8,128)(2,1)}), bf16[6656,512]{1,0:T(8,128)(2,1)}) %all-gather.5.cloned.1.call-update) | async-done | bytes 6815760 | tf_op jit(solution)/shard_map/all_gather | solution.py:356
  235.3 14.0 %shard_map.115 = (f32[208,6656]{1,0:T(8,128)}, f32[208,1]{1,0:T(8,128)S(1)}, f32[2,6784]{1,0:T(2,128)S(1)}) custom-call(bf16[208,512]{1,0:T(8,128)(2,1)S(1)} %bitcast.105, bf16[6656,512]{1,0:T(8,128)(2,1)} %all-gather.5.cloned.1.call-done.full_ref, f32[208,1]{1,0:T(8,128)S(1)} %copy.16.row_ref, bf16[208,6656]{1,0:T(8,128)(2,1)S(1)} %bitcast.100), custom_call_target="tpu_custom_call" | custom-call | tf_op jit(solution)/shard_map/pallas_call | solution.py:249
  250.5 1.9 collective-permute-start.61
  252.6 2.1 collective-permute-start.60
  254.7 3.8 %collective-permute-done.62 = f32[2,6784]{1,0:T(2,128)S(1)} collective-permute-done((f32[2,6784]{1,0:T(2,128)S(1)}, f32[2,6784]{1,0:T(2,128)S(1)}, u32[]{:S(2)}, u32[]{:S(2)}) %collective-permute-start.62) | collective-permute-done | bytes 54304 | tf_op jit(solution)/shard_map/ppermute | solution.py:18
  258.6 1.8 collective-permute-start.64
  260.7 2.0 collective-permute-start.63
  262.7 2.3 fusion.2
  266.4 9.4 %shard_map.116 = (bf16[208,6656]{1,0:T(8,128)(2,1)}, f32[1,6656]{1,0:T(1,128)}) custom-call(f32[2,6784]{1,0:T(2,128)S(1)} %add_add_fusion.totals_ref, f32[208,1]{1,0:T(8,128)S(1)} %get-tuple-element.23.row_new_ref, f32[1,6656]{1,0:T(1,128)S(1)} %copy-done.4, f32[208,6656]{1,0:T(8,128)} %get-tuple-element.24.gradient_ref, bf16[208,6656]{1,0:T(8,128)(2,1)S(1)} %bitcast.101), custom_call_target="tpu_custom_call" | custom-call | tf_op jit(solution)/shard_map/pallas_call | solution.py:298
  (125 shorter events, 26.7 us)
Async XLA Ops:
  7.2 114.6 %all-gather.3.cloned.1.call-start = ((), (), s32[]{:S(2)}) async-start(), calls=%async_computation | async-start | bytes 13844480 | tf_op jit(solution)/shard_map/all_gather | solution.py:336
  7.9 227.4 %all-gather.5.cloned.1.call-start = ((), (), s32[]{:S(2)}) async-start(), calls=%async_computation.1 | async-start | bytes 7028736 | tf_op jit(solution)/shard_map/all_gather | solution.py:356
  8.8 6.7 %collective-permute-start.2 = (bf16[208,128]{1,0:T(8,128)(2,1)S(1)}, bf16[208,128]{1,0:T(8,128)(2,1)S(1)}, u32[]{:S(2)}, u32[]{:S(2)}) collective-permute-start(bf16[208,128]{1,0:T(8,128)(2,1)S(1)} %get-tuple-element.46), channel_id=1, source_target_pairs={{0,2},{2,4},{4,6},{6,0},{1,3},{3,5},{5,7},{7,1},{8,10},{10,12},{12... | collective-permute-start | bytes 159752 | tf_op jit(solution)/shard_map/ppermute | solution.py:18
  10.9 6.3 %collective-permute-start.1 = (bf16[208,128]{1,0:T(8,128)(2,1)S(1)}, bf16[208,128]{1,0:T(8,128)(2,1)S(1)}, u32[]{:S(2)}, u32[]{:S(2)}) collective-permute-start(bf16[208,128]{1,0:T(8,128)(2,1)S(1)} %get-tuple-element.46), channel_id=1, source_target_pairs={{0,4},{2,6},{4,0},{6,2},{1,5},{3,7},{5,1},{7,3},{8,12},{10,14},{12... | collective-permute-start | bytes 159752 | tf_op jit(solution)/shard_map/ppermute | solution.py:18
  14.5 4.1 %collective-permute-start = (bf16[208,128]{1,0:T(8,128)(2,1)S(1)}, bf16[208,128]{1,0:T(8,128)(2,1)S(1)}, u32[]{:S(2)}, u32[]{:S(2)}) collective-permute-start(bf16[208,128]{1,0:T(8,128)(2,1)S(1)} %get-tuple-element.46), channel_id=1, source_target_pairs={{0,6},{2,0},{4,2},{6,4},{1,7},{3,1},{5,3},{7,5},{8,14},{10,8},{12,... | collective-permute-start | bytes 159752 | tf_op jit(solution)/shard_map/ppermute | solution.py:18
  18.6 10.7 %collective-permute-start.3 = (bf16[4,208,128]{2,1,0:T(8,128)(2,1)S(1)}, bf16[4,208,128]{2,1,0:T(8,128)(2,1)S(1)}, u32[]{:S(2)}, u32[]{:S(2)}) collective-permute-start(bf16[4,208,128]{2,1,0:T(8,128)(2,1)S(1)} %pad_maximum_fusion.refs_0_), channel_id=1, source_target_pairs={{0,24},{8,0},{16,8},{24,16},{1,25},{9,1},{17,9},{25,17},{2,26},{10... | collective-permute-start | bytes 638984 | tf_op jit(solution)/shard_map/ppermute | solution.py:18
  21.7 9.2 %collective-permute-start.4 = (bf16[4,208,128]{2,1,0:T(8,128)(2,1)S(1)}, bf16[4,208,128]{2,1,0:T(8,128)(2,1)S(1)}, u32[]{:S(2)}, u32[]{:S(2)}) collective-permute-start(bf16[4,208,128]{2,1,0:T(8,128)(2,1)S(1)} %pad_maximum_fusion.refs_0_), channel_id=1, source_target_pairs={{0,16},{8,24},{16,0},{24,8},{1,17},{9,25},{17,1},{25,9},{2,18},{10... | collective-permute-start | bytes 638984 | tf_op jit(solution)/shard_map/ppermute | solution.py:18
  22.3 10.8 %collective-permute-start.5 = (bf16[4,208,128]{2,1,0:T(8,128)(2,1)S(1)}, bf16[4,208,128]{2,1,0:T(8,128)(2,1)S(1)}, u32[]{:S(2)}, u32[]{:S(2)}) collective-permute-start(bf16[4,208,128]{2,1,0:T(8,128)(2,1)S(1)} %pad_maximum_fusion.refs_0_), channel_id=1, source_target_pairs={{0,8},{8,16},{16,24},{24,0},{1,9},{9,17},{17,25},{25,1},{2,10},{10... | collective-permute-start | bytes 638984 | tf_op jit(solution)/shard_map/ppermute | solution.py:18
  23.3 9.9 %collective-permute-start.6 = (bf16[4,208,128]{2,1,0:T(8,128)(2,1)S(1)}, bf16[4,208,128]{2,1,0:T(8,128)(2,1)S(1)}, u32[]{:S(2)}, u32[]{:S(2)}) collective-permute-start(bf16[4,208,128]{2,1,0:T(8,128)(2,1)S(1)} %pad_maximum_fusion.refs_0_), channel_id=1, source_target_pairs={{0,1},{1,0},{2,3},{3,2},{4,5},{5,4},{6,7},{7,6},{8,9},{9,8},{10,11... | collective-permute-start | bytes 638984 | tf_op jit(solution)/shard_map/ppermute | solution.py:36
  29.4 3.9 %collective-permute-start.7 = (bf16[4,208,128]{2,1,0:T(8,128)(2,1)S(1)}, bf16[4,208,128]{2,1,0:T(8,128)(2,1)S(1)}, u32[]{:S(2)}, u32[]{:S(2)}) collective-permute-start(bf16[4,208,128]{2,1,0:T(8,128)(2,1)S(1)} %collective-permute-done.3.refs_1_), channel_id=1, source_target_pairs={{0,1},{1,0},{2,3},{3,2},{4,5},{5,4},{6,7},{7,6},{8,9},{9,8},{10,11... | collective-permute-start | bytes 638984 | tf_op jit(solution)/shard_map/ppermute | solution.py:36
  30.9 2.4 collective-permute-start.8
  33.1 1.5 collective-permute-start.9
  48.7 3.6 %collective-permute-start.12 = (f32[2,128]{1,0:T(2,128)S(1)}, f32[2,128]{1,0:T(2,128)S(1)}, u32[]{:S(2)}, u32[]{:S(2)}) collective-permute-start(f32[2,128]{1,0:T(2,128)S(1)} %add.85), channel_id=1, source_target_pairs={{0,6},{2,0},{4,2},{6,4},{1,7},{3,1},{5,3},{7,5},{8,14},{10,8},{12,... | collective-permute-start | bytes 3080 | tf_op jit(solution)/shard_map/ppermute | solution.py:18
  50.8 4.8 %collective-permute-start.13 = (f32[2,128]{1,0:T(2,128)S(1)}, f32[2,128]{1,0:T(2,128)S(1)}, u32[]{:S(2)}, u32[]{:S(2)}) collective-permute-start(f32[2,128]{1,0:T(2,128)S(1)} %add.85), channel_id=1, source_target_pairs={{0,2},{2,4},{4,6},{6,0},{1,3},{3,5},{5,7},{7,1},{8,10},{10,12},{12... | collective-permute-start | bytes 3080 | tf_op jit(solution)/shard_map/ppermute | solution.py:18
  50.8 5.1 %collective-permute-start.11 = (f32[2,128]{1,0:T(2,128)S(1)}, f32[2,128]{1,0:T(2,128)S(1)}, u32[]{:S(2)}, u32[]{:S(2)}) collective-permute-start(f32[2,128]{1,0:T(2,128)S(1)} %add.85), channel_id=1, source_target_pairs={{0,4},{2,6},{4,0},{6,2},{1,5},{3,7},{5,1},{7,3},{8,12},{10,14},{12... | collective-permute-start | bytes 3080 | tf_op jit(solution)/shard_map/ppermute | solution.py:18
  55.9 13.5 %collective-permute-start.15 = (f32[2,128]{1,0:T(2,128)S(1)}, f32[2,128]{1,0:T(2,128)S(1)}, u32[]{:S(2)}, u32[]{:S(2)}) collective-permute-start(f32[2,128]{1,0:T(2,128)S(1)} %add_add_fusion.3), channel_id=1, source_target_pairs={{0,24},{8,0},{16,8},{24,16},{1,25},{9,1},{17,9},{25,17},{2,26},{10... | collective-permute-start | bytes 3080 | tf_op jit(solution)/shard_map/ppermute | solution.py:18
  56.4 12.9 %collective-permute-start.16 = (f32[2,128]{1,0:T(2,128)S(1)}, f32[2,128]{1,0:T(2,128)S(1)}, u32[]{:S(2)}, u32[]{:S(2)}) collective-permute-start(f32[2,128]{1,0:T(2,128)S(1)} %add_add_fusion.3), channel_id=1, source_target_pairs={{0,8},{8,16},{16,24},{24,0},{1,9},{9,17},{17,25},{25,1},{2,10},{10... | collective-permute-start | bytes 3080 | tf_op jit(solution)/shard_map/ppermute | solution.py:18
  57.9 11.4 %collective-permute-start.14 = (f32[2,128]{1,0:T(2,128)S(1)}, f32[2,128]{1,0:T(2,128)S(1)}, u32[]{:S(2)}, u32[]{:S(2)}) collective-permute-start(f32[2,128]{1,0:T(2,128)S(1)} %add_add_fusion.3), channel_id=1, source_target_pairs={{0,16},{8,24},{16,0},{24,8},{1,17},{9,25},{17,1},{25,9},{2,18},{10... | collective-permute-start | bytes 3080 | tf_op jit(solution)/shard_map/ppermute | solution.py:18
  74.4 2.5 collective-permute-start.17
  77.2 11.6 %collective-permute-start.20 = (bf16[4,208,128]{2,1,0:T(8,128)(2,1)S(1)}, bf16[4,208,128]{2,1,0:T(8,128)(2,1)S(1)}, u32[]{:S(2)}, u32[]{:S(2)}) collective-permute-start(bf16[4,208,128]{2,1,0:T(8,128)(2,1)S(1)} %get-tuple-element.34), channel_id=1, source_target_pairs={{0,24},{8,0},{16,8},{24,16},{1,25},{9,1},{17,9},{25,17},{2,26},{10... | collective-permute-start | bytes 638984 | tf_op jit(solution)/shard_map/ppermute | solution.py:54
  79.3 9.7 %collective-permute-start.19 = (bf16[4,208,128]{2,1,0:T(8,128)(2,1)S(1)}, bf16[4,208,128]{2,1,0:T(8,128)(2,1)S(1)}, u32[]{:S(2)}, u32[]{:S(2)}) collective-permute-start(bf16[4,208,128]{2,1,0:T(8,128)(2,1)S(1)} %get-tuple-element.35), channel_id=1, source_target_pairs={{0,16},{8,24},{16,0},{24,8},{1,17},{9,25},{17,1},{25,9},{2,18},{10... | collective-permute-start | bytes 638984 | tf_op jit(solution)/shard_map/ppermute | solution.py:54
  81.4 11.0 %collective-permute-start.18 = (bf16[4,208,128]{2,1,0:T(8,128)(2,1)S(1)}, bf16[4,208,128]{2,1,0:T(8,128)(2,1)S(1)}, u32[]{:S(2)}, u32[]{:S(2)}) collective-permute-start(bf16[4,208,128]{2,1,0:T(8,128)(2,1)S(1)} %get-tuple-element.33), channel_id=1, source_target_pairs={{0,8},{8,16},{16,24},{24,0},{1,9},{9,17},{17,25},{25,1},{2,10},{10... | collective-permute-start | bytes 638984 | tf_op jit(solution)/shard_map/ppermute | solution.py:54
  92.6 5.8 %collective-permute-start.23 = (bf16[208,128]{1,0:T(8,128)(2,1)S(1)}, bf16[208,128]{1,0:T(8,128)(2,1)S(1)}, u32[]{:S(2)}, u32[]{:S(2)}) collective-permute-start(bf16[208,128]{1,0:T(8,128)(2,1)S(1)} %get-tuple-element.43), channel_id=1, source_target_pairs={{0,6},{2,0},{4,2},{6,4},{1,7},{3,1},{5,3},{7,5},{8,14},{10,8},{12,... | collective-permute-start | bytes 159752 | tf_op jit(solution)/shard_map/ppermute | solution.py:54
  95.9 5.7 %collective-permute-start.22 = (bf16[208,128]{1,0:T(8,128)(2,1)S(1)}, bf16[208,128]{1,0:T(8,128)(2,1)S(1)}, u32[]{:S(2)}, u32[]{:S(2)}) collective-permute-start(bf16[208,128]{1,0:T(8,128)(2,1)S(1)} %get-tuple-element.44), channel_id=1, source_target_pairs={{0,4},{2,6},{4,0},{6,2},{1,5},{3,7},{5,1},{7,3},{8,12},{10,14},{12... | collective-permute-start | bytes 159752 | tf_op jit(solution)/shard_map/ppermute | solution.py:54
  95.9 5.9 %collective-permute-start.21 = (bf16[208,128]{1,0:T(8,128)(2,1)S(1)}, bf16[208,128]{1,0:T(8,128)(2,1)S(1)}, u32[]{:S(2)}, u32[]{:S(2)}) collective-permute-start(bf16[208,128]{1,0:T(8,128)(2,1)S(1)} %get-tuple-element.42), channel_id=1, source_target_pairs={{0,2},{2,4},{4,6},{6,0},{1,3},{3,5},{5,7},{7,1},{8,10},{10,12},{12... | collective-permute-start | bytes 159752 | tf_op jit(solution)/shard_map/ppermute | solution.py:54
  101.8 6.2 %collective-permute-start.26 = (bf16[208,128]{1,0:T(8,128)(2,1)S(1)}, bf16[208,128]{1,0:T(8,128)(2,1)S(1)}, u32[]{:S(2)}, u32[]{:S(2)}) collective-permute-start(bf16[208,128]{1,0:T(8,128)(2,1)S(1)} %fusion.9.refs_8_), channel_id=1, source_target_pairs={{0,2},{2,4},{4,6},{6,0},{1,3},{3,5},{5,7},{7,1},{8,10},{10,12},{12... | collective-permute-start | bytes 159752 | tf_op jit(solution)/shard_map/ppermute | solution.py:18
  102.1 5.9 %collective-permute-start.25 = (bf16[208,128]{1,0:T(8,128)(2,1)S(1)}, bf16[208,128]{1,0:T(8,128)(2,1)S(1)}, u32[]{:S(2)}, u32[]{:S(2)}) collective-permute-start(bf16[208,128]{1,0:T(8,128)(2,1)S(1)} %fusion.9.refs_8_), channel_id=1, source_target_pairs={{0,4},{2,6},{4,0},{6,2},{1,5},{3,7},{5,1},{7,3},{8,12},{10,14},{12... | collective-permute-start | bytes 159752 | tf_op jit(solution)/shard_map/ppermute | solution.py:18
  104.4 4.5 %collective-permute-start.24 = (bf16[208,128]{1,0:T(8,128)(2,1)S(1)}, bf16[208,128]{1,0:T(8,128)(2,1)S(1)}, u32[]{:S(2)}, u32[]{:S(2)}) collective-permute-start(bf16[208,128]{1,0:T(8,128)(2,1)S(1)} %fusion.9.refs_8_), channel_id=1, source_target_pairs={{0,6},{2,0},{4,2},{6,4},{1,7},{3,1},{5,3},{7,5},{8,14},{10,8},{12,... | collective-permute-start | bytes 159752 | tf_op jit(solution)/shard_map/ppermute | solution.py:18
  108.9 7.6 %collective-permute-start.27 = (bf16[4,208,128]{2,1,0:T(8,128)(2,1)S(1)}, bf16[4,208,128]{2,1,0:T(8,128)(2,1)S(1)}, u32[]{:S(2)}, u32[]{:S(2)}) collective-permute-start(bf16[4,208,128]{2,1,0:T(8,128)(2,1)S(1)} %pad_maximum_fusion.1.refs_0_), channel_id=1, source_target_pairs={{0,24},{8,0},{16,8},{24,16},{1,25},{9,1},{17,9},{25,17},{2,26},{10... | collective-permute-start | bytes 638984 | tf_op jit(solution)/shard_map/ppermute | solution.py:18
  109.6 8.6 %collective-permute-start.28 = (bf16[4,208,128]{2,1,0:T(8,128)(2,1)S(1)}, bf16[4,208,128]{2,1,0:T(8,128)(2,1)S(1)}, u32[]{:S(2)}, u32[]{:S(2)}) collective-permute-start(bf16[4,208,128]{2,1,0:T(8,128)(2,1)S(1)} %pad_maximum_fusion.1.refs_0_), channel_id=1, source_target_pairs={{0,16},{8,24},{16,0},{24,8},{1,17},{9,25},{17,1},{25,9},{2,18},{10... | collective-permute-start | bytes 638984 | tf_op jit(solution)/shard_map/ppermute | solution.py:18
  111.6 8.7 %collective-permute-start.29 = (bf16[4,208,128]{2,1,0:T(8,128)(2,1)S(1)}, bf16[4,208,128]{2,1,0:T(8,128)(2,1)S(1)}, u32[]{:S(2)}, u32[]{:S(2)}) collective-permute-start(bf16[4,208,128]{2,1,0:T(8,128)(2,1)S(1)} %pad_maximum_fusion.1.refs_0_), channel_id=1, source_target_pairs={{0,8},{8,16},{16,24},{24,0},{1,9},{9,17},{17,25},{25,1},{2,10},{10... | collective-permute-start | bytes 638984 | tf_op jit(solution)/shard_map/ppermute | solution.py:18
  112.1 8.3 %collective-permute-start.30 = (bf16[4,208,128]{2,1,0:T(8,128)(2,1)S(1)}, bf16[4,208,128]{2,1,0:T(8,128)(2,1)S(1)}, u32[]{:S(2)}, u32[]{:S(2)}) collective-permute-start(bf16[4,208,128]{2,1,0:T(8,128)(2,1)S(1)} %pad_maximum_fusion.1.refs_0_), channel_id=1, source_target_pairs={{0,1},{1,0},{2,3},{3,2},{4,5},{5,4},{6,7},{7,6},{8,9},{9,8},{10,11... | collective-permute-start | bytes 638984 | tf_op jit(solution)/shard_map/ppermute | solution.py:36
  116.4 4.0 %collective-permute-start.31 = (bf16[4,208,128]{2,1,0:T(8,128)(2,1)S(1)}, bf16[4,208,128]{2,1,0:T(8,128)(2,1)S(1)}, u32[]{:S(2)}, u32[]{:S(2)}) collective-permute-start(bf16[4,208,128]{2,1,0:T(8,128)(2,1)S(1)} %collective-permute-done.27.refs_1_), channel_id=1, source_target_pairs={{0,1},{1,0},{2,3},{3,2},{4,5},{5,4},{6,7},{7,6},{8,9},{9,8},{10,11... | collective-permute-start | bytes 638984 | tf_op jit(solution)/shard_map/ppermute | solution.py:36
  118.1 2.3 collective-permute-start.32
  125.1 5.4 %collective-permute-start.36 = (bf16[208,128]{1,0:T(8,128)(2,1)S(1)}, bf16[208,128]{1,0:T(8,128)(2,1)S(1)}, u32[]{:S(2)}, u32[]{:S(2)}) collective-permute-start(bf16[208,128]{1,0:T(8,128)(2,1)S(1)} %shard_map.112.refs_8_), channel_id=1, source_target_pairs={{0,2},{2,4},{4,6},{6,0},{1,3},{3,5},{5,7},{7,1},{8,10},{10,12},{12... | collective-permute-start | bytes 159752 | tf_op jit(solution)/shard_map/ppermute | solution.py:18
  126.4 5.9 %collective-permute-start.35 = (bf16[208,128]{1,0:T(8,128)(2,1)S(1)}, bf16[208,128]{1,0:T(8,128)(2,1)S(1)}, u32[]{:S(2)}, u32[]{:S(2)}) collective-permute-start(bf16[208,128]{1,0:T(8,128)(2,1)S(1)} %shard_map.112.refs_8_), channel_id=1, source_target_pairs={{0,4},{2,6},{4,0},{6,2},{1,5},{3,7},{5,1},{7,3},{8,12},{10,14},{12... | collective-permute-start | bytes 159752 | tf_op jit(solution)/shard_map/ppermute | solution.py:18
  129.3 4.1 %collective-permute-start.34 = (bf16[208,128]{1,0:T(8,128)(2,1)S(1)}, bf16[208,128]{1,0:T(8,128)(2,1)S(1)}, u32[]{:S(2)}, u32[]{:S(2)}) collective-permute-start(bf16[208,128]{1,0:T(8,128)(2,1)S(1)} %shard_map.112.refs_8_), channel_id=1, source_target_pairs={{0,6},{2,0},{4,2},{6,4},{1,7},{3,1},{5,3},{7,5},{8,14},{10,8},{12,... | collective-permute-start | bytes 159752 | tf_op jit(solution)/shard_map/ppermute | solution.py:18
  133.5 8.2 %collective-permute-start.37 = (bf16[4,208,128]{2,1,0:T(8,128)(2,1)S(1)}, bf16[4,208,128]{2,1,0:T(8,128)(2,1)S(1)}, u32[]{:S(2)}, u32[]{:S(2)}) collective-permute-start(bf16[4,208,128]{2,1,0:T(8,128)(2,1)S(1)} %pad_maximum_fusion.2.refs_0_), channel_id=1, source_target_pairs={{0,24},{8,0},{16,8},{24,16},{1,25},{9,1},{17,9},{25,17},{2,26},{10... | collective-permute-start | bytes 638984 | tf_op jit(solution)/shard_map/ppermute | solution.py:18
  134.9 9.5 %collective-permute-start.38 = (bf16[4,208,128]{2,1,0:T(8,128)(2,1)S(1)}, bf16[4,208,128]{2,1,0:T(8,128)(2,1)S(1)}, u32[]{:S(2)}, u32[]{:S(2)}) collective-permute-start(bf16[4,208,128]{2,1,0:T(8,128)(2,1)S(1)} %pad_maximum_fusion.2.refs_0_), channel_id=1, source_target_pairs={{0,16},{8,24},{16,0},{24,8},{1,17},{9,25},{17,1},{25,9},{2,18},{10... | collective-permute-start | bytes 638984 | tf_op jit(solution)/shard_map/ppermute | solution.py:18
  135.8 10.9 %collective-permute-start.39 = (bf16[4,208,128]{2,1,0:T(8,128)(2,1)S(1)}, bf16[4,208,128]{2,1,0:T(8,128)(2,1)S(1)}, u32[]{:S(2)}, u32[]{:S(2)}) collective-permute-start(bf16[4,208,128]{2,1,0:T(8,128)(2,1)S(1)} %pad_maximum_fusion.2.refs_0_), channel_id=1, source_target_pairs={{0,8},{8,16},{16,24},{24,0},{1,9},{9,17},{17,25},{25,1},{2,10},{10... | collective-permute-start | bytes 638984 | tf_op jit(solution)/shard_map/ppermute | solution.py:18
  136.6 10.2 %collective-permute-start.40 = (bf16[4,208,128]{2,1,0:T(8,128)(2,1)S(1)}, bf16[4,208,128]{2,1,0:T(8,128)(2,1)S(1)}, u32[]{:S(2)}, u32[]{:S(2)}) collective-permute-start(bf16[4,208,128]{2,1,0:T(8,128)(2,1)S(1)} %pad_maximum_fusion.2.refs_0_), channel_id=1, source_target_pairs={{0,1},{1,0},{2,3},{3,2},{4,5},{5,4},{6,7},{7,6},{8,9},{9,8},{10,11... | collective-permute-start | bytes 638984 | tf_op jit(solution)/shard_map/ppermute | solution.py:36
  141.7 5.1 %collective-permute-start.41 = (bf16[4,208,128]{2,1,0:T(8,128)(2,1)S(1)}, bf16[4,208,128]{2,1,0:T(8,128)(2,1)S(1)}, u32[]{:S(2)}, u32[]{:S(2)}) collective-permute-start(bf16[4,208,128]{2,1,0:T(8,128)(2,1)S(1)} %collective-permute-done.37.refs_1_), channel_id=1, source_target_pairs={{0,1},{1,0},{2,3},{3,2},{4,5},{5,4},{6,7},{7,6},{8,9},{9,8},{10,11... | collective-permute-start | bytes 638984 | tf_op jit(solution)/shard_map/ppermute | solution.py:36
  144.5 2.3 collective-permute-start.42
  151.5 5.9 %collective-permute-start.46 = (bf16[208,128]{1,0:T(8,128)(2,1)S(1)}, bf16[208,128]{1,0:T(8,128)(2,1)S(1)}, u32[]{:S(2)}, u32[]{:S(2)}) collective-permute-start(bf16[208,128]{1,0:T(8,128)(2,1)S(1)} %shard_map.113.refs_8_), channel_id=1, source_target_pairs={{0,2},{2,4},{4,6},{6,0},{1,3},{3,5},{5,7},{7,1},{8,10},{10,12},{12... | collective-permute-start | bytes 159752 | tf_op jit(solution)/shard_map/ppermute | solution.py:18
  151.7 6.2 %collective-permute-start.45 = (bf16[208,128]{1,0:T(8,128)(2,1)S(1)}, bf16[208,128]{1,0:T(8,128)(2,1)S(1)}, u32[]{:S(2)}, u32[]{:S(2)}) collective-permute-start(bf16[208,128]{1,0:T(8,128)(2,1)S(1)} %shard_map.113.refs_8_), channel_id=1, source_target_pairs={{0,4},{2,6},{4,0},{6,2},{1,5},{3,7},{5,1},{7,3},{8,12},{10,14},{12... | collective-permute-start | bytes 159752 | tf_op jit(solution)/shard_map/ppermute | solution.py:18
  154.9 4.1 %collective-permute-start.44 = (bf16[208,128]{1,0:T(8,128)(2,1)S(1)}, bf16[208,128]{1,0:T(8,128)(2,1)S(1)}, u32[]{:S(2)}, u32[]{:S(2)}) collective-permute-start(bf16[208,128]{1,0:T(8,128)(2,1)S(1)} %shard_map.113.refs_8_), channel_id=1, source_target_pairs={{0,6},{2,0},{4,2},{6,4},{1,7},{3,1},{5,3},{7,5},{8,14},{10,8},{12,... | collective-permute-start | bytes 159752 | tf_op jit(solution)/shard_map/ppermute | solution.py:18
  159.1 8.4 %collective-permute-start.47 = (bf16[4,208,128]{2,1,0:T(8,128)(2,1)S(1)}, bf16[4,208,128]{2,1,0:T(8,128)(2,1)}, u32[]{:S(2)}, u32[]{:S(2)}) collective-permute-start(bf16[4,208,128]{2,1,0:T(8,128)(2,1)S(1)} %pad_maximum_fusion.3.refs_0_), channel_id=1, source_target_pairs={{0,24},{8,0},{16,8},{24,16},{1,25},{9,1},{17,9},{25,17},{2,26},{10... | collective-permute-start | bytes 638984 | tf_op jit(solution)/shard_map/ppermute | solution.py:18
  159.8 9.8 %collective-permute-start.48 = (bf16[4,208,128]{2,1,0:T(8,128)(2,1)S(1)}, bf16[4,208,128]{2,1,0:T(8,128)(2,1)}, u32[]{:S(2)}, u32[]{:S(2)}) collective-permute-start(bf16[4,208,128]{2,1,0:T(8,128)(2,1)S(1)} %pad_maximum_fusion.3.refs_0_), channel_id=1, source_target_pairs={{0,16},{8,24},{16,0},{24,8},{1,17},{9,25},{17,1},{25,9},{2,18},{10... | collective-permute-start | bytes 638984 | tf_op jit(solution)/shard_map/ppermute | solution.py:18
  160.4 11.5 %collective-permute-start.49 = (bf16[4,208,128]{2,1,0:T(8,128)(2,1)S(1)}, bf16[4,208,128]{2,1,0:T(8,128)(2,1)}, u32[]{:S(2)}, u32[]{:S(2)}) collective-permute-start(bf16[4,208,128]{2,1,0:T(8,128)(2,1)S(1)} %pad_maximum_fusion.3.refs_0_), channel_id=1, source_target_pairs={{0,8},{8,16},{16,24},{24,0},{1,9},{9,17},{17,25},{25,1},{2,10},{10... | collective-permute-start | bytes 638984 | tf_op jit(solution)/shard_map/ppermute | solution.py:18
  161.3 10.7 %collective-permute-start.50 = (bf16[4,208,128]{2,1,0:T(8,128)(2,1)S(1)}, bf16[4,208,128]{2,1,0:T(8,128)(2,1)}, u32[]{:S(2)}, u32[]{:S(2)}) collective-permute-start(bf16[4,208,128]{2,1,0:T(8,128)(2,1)S(1)} %pad_maximum_fusion.3.refs_0_), channel_id=1, source_target_pairs={{0,1},{1,0},{2,3},{3,2},{4,5},{5,4},{6,7},{7,6},{8,9},{9,8},{10,11... | collective-permute-start | bytes 638984 | tf_op jit(solution)/shard_map/ppermute | solution.py:36
  167.5 4.5 %collective-permute-start.51 = (bf16[4,208,128]{2,1,0:T(8,128)(2,1)}, bf16[4,208,128]{2,1,0:T(8,128)(2,1)}, u32[]{:S(2)}, u32[]{:S(2)}) collective-permute-start(bf16[4,208,128]{2,1,0:T(8,128)(2,1)} %collective-permute-done.47.refs_1_), channel_id=1, source_target_pairs={{0,1},{1,0},{2,3},{3,2},{4,5},{5,4},{6,7},{7,6},{8,9},{9,8},{10,11... | collective-permute-start | bytes 638984 | tf_op jit(solution)/shard_map/ppermute | solution.py:36
  169.6 2.4 collective-permute-start.52
  171.9 1.8 collective-permute-start.53
  177.6 6.0 %collective-permute-start.55 = (bf16[208,128]{1,0:T(8,128)(2,1)S(1)}, bf16[208,128]{1,0:T(8,128)(2,1)S(1)}, u32[]{:S(2)}, u32[]{:S(2)}) collective-permute-start(bf16[208,128]{1,0:T(8,128)(2,1)S(1)} %get-tuple-element.40), channel_id=1, source_target_pairs={{0,64},{32,96},{64,0},{96,32},{1,65},{33,97},{65,1},{97,33},{2,66}... | collective-permute-start | bytes 159752 | tf_op jit(solution)/shard_map/ppermute | solution.py:68
  180.4 5.3 %collective-permute-start.56 = (bf16[208,128]{1,0:T(8,128)(2,1)S(1)}, bf16[208,128]{1,0:T(8,128)(2,1)S(1)}, u32[]{:S(2)}, u32[]{:S(2)}) collective-permute-start(bf16[208,128]{1,0:T(8,128)(2,1)S(1)} %get-tuple-element.39), channel_id=1, source_target_pairs={{0,32},{32,64},{64,96},{96,0},{1,33},{33,65},{65,97},{97,1},{2,34}... | collective-permute-start | bytes 159752 | tf_op jit(solution)/shard_map/ppermute | solution.py:68
  181.3 4.4 %collective-permute-start.54 = (bf16[208,128]{1,0:T(8,128)(2,1)S(1)}, bf16[208,128]{1,0:T(8,128)(2,1)S(1)}, u32[]{:S(2)}, u32[]{:S(2)}) collective-permute-start(bf16[208,128]{1,0:T(8,128)(2,1)S(1)} %get-tuple-element.41), channel_id=1, source_target_pairs={{0,96},{32,0},{64,32},{96,64},{1,97},{33,1},{65,33},{97,65},{2,98}... | collective-permute-start | bytes 159752 | tf_op jit(solution)/shard_map/ppermute | solution.py:68
  187.3 3.8 %collective-permute-start.57 = (f32[1]{0:T(128)}, f32[1]{0:T(128)}, u32[]{:S(2)}, u32[]{:S(2)}) collective-permute-start(f32[1]{0:T(128)} %bitcast.35), channel_id=1, source_target_pairs={{0,32},{32,0},{64,96},{96,64},{1,33},{33,1},{65,97},{97,65},{2,34}... | collective-permute-start | bytes 20 | tf_op jit(solution)/shard_map/ppermute | solution.py:359
  192.3 5.2 %collective-permute-start.58 = (f32[1]{0:T(128)}, f32[1]{0:T(128)}, u32[]{:S(2)}, u32[]{:S(2)}) collective-permute-start(f32[1]{0:T(128)} %add.99), channel_id=1, source_target_pairs={{0,64},{32,96},{64,0},{96,32},{1,65},{33,97},{65,1},{97,33},{2,66}... | collective-permute-start | bytes 20 | tf_op jit(solution)/shard_map/ppermute | solution.py:359
  250.5 4.2 %collective-permute-start.61 = (f32[2,6784]{1,0:T(2,128)S(1)}, f32[2,6784]{1,0:T(2,128)S(1)}, u32[]{:S(2)}, u32[]{:S(2)}) collective-permute-start(f32[2,6784]{1,0:T(2,128)S(1)} %add.102), channel_id=1, source_target_pairs={{0,6},{2,0},{4,2},{6,4},{1,7},{3,1},{5,3},{7,5},{8,14},{10,8},{12,... | collective-permute-start | bytes 162824 | tf_op jit(solution)/shard_map/ppermute | solution.py:18
  252.5 6.1 %collective-permute-start.62 = (f32[2,6784]{1,0:T(2,128)S(1)}, f32[2,6784]{1,0:T(2,128)S(1)}, u32[]{:S(2)}, u32[]{:S(2)}) collective-permute-start(f32[2,6784]{1,0:T(2,128)S(1)} %add.102), channel_id=1, source_target_pairs={{0,2},{2,4},{4,6},{6,0},{1,3},{3,5},{5,7},{7,1},{8,10},{10,12},{12... | collective-permute-start | bytes 162824 | tf_op jit(solution)/shard_map/ppermute | solution.py:18
  252.6 5.9 %collective-permute-start.60 = (f32[2,6784]{1,0:T(2,128)S(1)}, f32[2,6784]{1,0:T(2,128)S(1)}, u32[]{:S(2)}, u32[]{:S(2)}) collective-permute-start(f32[2,6784]{1,0:T(2,128)S(1)} %add.102), channel_id=1, source_target_pairs={{0,4},{2,6},{4,0},{6,2},{1,5},{3,7},{5,1},{7,3},{8,12},{10,14},{12... | collective-permute-start | bytes 162824 | tf_op jit(solution)/shard_map/ppermute | solution.py:18
  258.6 7.1 %collective-permute-start.64 = (f32[2,6784]{1,0:T(2,128)S(1)}, f32[2,6784]{1,0:T(2,128)S(1)}, u32[]{:S(2)}, u32[]{:S(2)}) collective-permute-start(f32[2,6784]{1,0:T(2,128)S(1)} %add_add_fusion.1), channel_id=1, source_target_pairs={{0,24},{8,0},{16,8},{24,16},{1,25},{9,1},{17,9},{25,17},{2,26},{10... | collective-permute-start | bytes 162824 | tf_op jit(solution)/shard_map/ppermute | solution.py:18
  260.4 5.4 %collective-permute-start.65 = (f32[2,6784]{1,0:T(2,128)S(1)}, f32[2,6784]{1,0:T(2,128)S(1)}, u32[]{:S(2)}, u32[]{:S(2)}) collective-permute-start(f32[2,6784]{1,0:T(2,128)S(1)} %add_add_fusion.1), channel_id=1, source_target_pairs={{0,8},{8,16},{16,24},{24,0},{1,9},{9,17},{17,25},{25,1},{2,10},{10... | collective-permute-start | bytes 162824 | tf_op jit(solution)/shard_map/ppermute | solution.py:18
  260.7 5.6 %collective-permute-start.63 = (f32[2,6784]{1,0:T(2,128)S(1)}, f32[2,6784]{1,0:T(2,128)S(1)}, u32[]{:S(2)}, u32[]{:S(2)}) collective-permute-start(f32[2,6784]{1,0:T(2,128)S(1)} %add_add_fusion.1), channel_id=1, source_target_pairs={{0,16},{8,24},{16,0},{24,8},{1,17},{9,25},{17,1},{25,9},{2,18},{10... | collective-permute-start | bytes 162824 | tf_op jit(solution)/shard_map/ppermute | solution.py:18
  (11 other events, 221.0 us)
Sparse Core Ops, SparseCore 0:
  9.7 108.2 all-gather.2
  186.6 48.5 all-gather.4

commit v2 on v1

--- a/solution.py
+++ b/solution.py
@@ -9,15 +9,8 @@
 learn_rate = 0.3
 tiny_term = 1e-30
 bf16_largest = 3.3895e38
+chips = ("y", "z")
 wide_vmem = 48 * 1024 * 1024
-
-
-def from_ring(block, axis):
-    size = lax.axis_size(axis)
-    return [block] + [
-        lax.ppermute(block, axis, [(i, (i - step) % size) for i in range(size)])
-        for step in range(1, size)
-    ]
 
 
 def rotated(pieces, index, axis=0):
@@ -31,29 +24,26 @@
     return jnp.stack(placed, axis=axis)
 
 
+def other_core(x):
+    return lax.ppermute(x, "c", [(0, 1), (1, 0)])
+
+
+def swapped_chips(blocks):
+    return lax.all_to_all(blocks, chips, 0, 0, tiled=True)
+
+
+def from_chips(block):
+    count = lax.axis_size(chips)
+    return swapped_chips(jnp.broadcast_to(block[None], (count, *block.shape)))
+
+
 def tensor_pieces(block):
-    mine = from_ring(jnp.stack(from_ring(block, "z")), "y")
-    return mine + [lax.ppermute(piece, "c", [(0, 1), (1, 0)]) for piece in mine]
-
-
-def summed(x, axis):
-    pieces = from_ring(x, axis)
-    if len(pieces) == 2:
-        return pieces[0] + pieces[1]
-    return (pieces[0] + pieces[2]) + (pieces[1] + pieces[3])
+    mine = from_chips(block)
+    return [mine, other_core(mine)]
 
 
 def summed_tensor(x):
-    return summed(summed(summed(x, "c"), "z"), "y")
-
-
-def scattered(blocks, axis):
-    size = len(blocks)
-    total = blocks[0].astype(jnp.float32)
-    for step in range(1, size):
-        piece = lax.ppermute(blocks[step], axis, [(i, (i + step) % size) for i in range(size)])
-        total = total + piece.astype(jnp.float32)
-    return total
+    return jnp.sum(from_chips(x + other_core(x)), axis=0)
 
 
 def exchanged(blocks, axis):
@@ -71,19 +61,17 @@
 
 
 def place(pieces, place_ref, full_ref):
-    y, z, c = place_ref[0], place_ref[1], place_ref[2]
-    rows = pieces[0].shape[1]
-    for side in range(2):
-        for step_y in range(4):
-            for step_z in range(4):
-                chip = lax.rem(y + step_y, 4) * 4 + lax.rem(z + step_z, 4)
-                core = c if side == 0 else 1 - c
-                start = pl.multiple_of((chip * 2 + core) * rows, 16)
-                full_ref[pl.ds(start, rows), :] = pieces[side * 4 + step_y][step_z]
+    c = place_ref[2]
+    count, rows = pieces[0].shape[:2]
+    for chip in range(count):
+        for side in range(2):
+            core = c if side == 0 else 1 - c
+            start = pl.multiple_of((chip * 2 + core) * rows, 16)
+            full_ref[pl.ds(start, rows), :] = pieces[side][chip]
 
 
 def logits_kernel(place_ref, *refs):
-    pieces, (labels_ref, weight_ref, both_ref, sums_ref, full_ref, total_ref) = refs[:8], refs[8:]
+    pieces, (labels_ref, weight_ref, both_ref, sums_ref, full_ref, total_ref) = refs[:2], refs[2:]
     step = pl.program_id(0)
     depth = weight_ref.shape[1]
     share = labels_ref.shape[1]
@@ -136,7 +124,7 @@
 def combine_kernel(place_ref, product_ref, sums_ref, keep_ref, send_ref, turned_ref):
     share = sums_ref.shape[1]
     rows = keep_ref.shape[2]
-    z, c = place_ref[1], place_ref[2]
+    c = place_ref[2]
     scale = (1.0 / place_ref[4].astype(jnp.float32)) / sums_ref[0:1, :]
     scale = jnp.broadcast_to(scale, (share, share)).T
     unit = 1.0 / place_ref[4].astype(jnp.float32)
@@ -144,7 +132,7 @@
         block = product_ref[:share, at : at + share] * scale - product_ref[share:, at : at + share] * unit
         turned_ref[at : at + share, :] = block.T
     for step in range(4):
-        chip = lax.rem(z + step, 4) * 2
+        chip = step * 2
         keep_ref[0, step] = turned_ref[pl.ds(pl.multiple_of((chip + c) * rows, 16), rows), :]
         send_ref[0, step] = turned_ref[pl.ds(pl.multiple_of((chip + 1 - c) * rows, 16), rows), :].astype(jnp.bfloat16)
 
@@ -160,7 +148,7 @@
             num_scalar_prefetch=1,
             grid=(4,),
             in_specs=[
-                pl.BlockSpec((width, tile), lambda i, s: (0, lax.rem(s[0] + i, 4))),
+                pl.BlockSpec((width, tile), lambda i, s: (0, i)),
                 pl.BlockSpec(sums.shape, lambda i, s: (0, 0)),
             ],
             out_specs=[out_spec, out_spec],
@@ -175,7 +163,7 @@
 
 
 def layer_kernel(place_ref, *refs):
-    pieces, (carried_ref, weight_ref, out_ref, full_ref) = refs[:8], refs[8:]
+    pieces, (carried_ref, weight_ref, out_ref, full_ref) = refs[:2], refs[2:]
     place(pieces, place_ref, full_ref)
     backward = jnp.dot(weight_ref[0], full_ref[...], preferred_element_type=jnp.float32)
     out_ref[...] = (carried_ref[...].astype(jnp.float32) + backward).astype(jnp.bfloat16)
@@ -203,69 +191,6 @@
     )(where, *pieces, carried, all_weights)
 
 
-def statistics_kernel(saved_ref, full_ref, row_ref, weight_ref, gradient_ref, row_new_ref, totals_ref, rows_ref, weights_ref):
-    step = pl.program_id(0)
-    tile = full_ref.shape[0]
-    width = gradient_ref.shape[1]
-
-    def lanes(x):
-        return sum(x[:, at : at + 128] for at in range(0, x.shape[1], 128))
-
-    @pl.when(step == 0)
-    def _():
-        rows_ref[...] = jnp.zeros_like(rows_ref)
-        weights_ref[...] = jnp.zeros_like(weights_ref)
-
-    gradient = lax.dot_general(
-        saved_ref[...], full_ref[...], (((1,), (1,)), ((), ())), preferred_element_type=jnp.float32
-    )
-    here = pl.ds(pl.multiple_of(step * tile, tile), tile)
-    gradient_ref[:, here] = gradient
-    squares = gradient * gradient + tiny_term
-    totals_ref[0:1, here] = jnp.sum(squares, axis=0, keepdims=True)
-    rows_ref[...] += lanes(squares)
-    weight = weight_ref[...].astype(jnp.float32)
-    weights_ref[...] += lanes(weight * weight)
-
-    @pl.when(step == pl.num_programs(0) - 1)
-    def _():
-        mean = jnp.sum(rows_ref[...], axis=1, keepdims=True) / width
-        row_new = decay_rate * row_ref[...] + (1.0 - decay_rate) * mean
-        row_new_ref[...] = row_new
-        inverse = jnp.broadcast_to(1.0 / row_new, rows_ref.shape)
-        for at in range(0, width, 128):
-            block = gradient_ref[:, at : at + 128]
-            totals_ref[1:2, at : at + 128] = jnp.sum(block * block * inverse, axis=0, keepdims=True)
-        row_total = jnp.sum(row_new, axis=0, keepdims=True)
-        weight_total = jnp.sum(jnp.sum(weights_ref[...], axis=0, keepdims=True), axis=1, keepdims=True)
-        totals_ref[0:1, width:] = jnp.broadcast_to(row_total, (1, 128))
-        totals_ref[1:2, width:] = jnp.broadcast_to(weight_total, (1, 128))
-
-
-def gradient_statistics(saved, full, row_state, weight, tile=512):
-    rows, tokens = saved.shape
-    width = full.shape[0]
-    whole = lambda shape: pl.BlockSpec(shape, lambda i: (0,) * len(shape))
-    return pl.pallas_call(
-        statistics_kernel,
-        grid=(width // tile,),
-        in_specs=[
-            whole(saved.shape),
-            pl.BlockSpec((tile, tokens), lambda i: (i, 0)),
-            whole(row_state.shape),
-            pl.BlockSpec((rows, tile), lambda i: (0, i)),
-        ],
-        out_specs=[whole((rows, width)), whole((rows, 1)), whole((2, width + 128))],
-        out_shape=[
-            jax.ShapeDtypeStruct((rows, width), jnp.float32),
-            jax.ShapeDtypeStruct((rows, 1), jnp.float32),
-            jax.ShapeDtypeStruct((2, width + 128), jnp.float32),
-        ],
-        scratch_shapes=[pltpu.VMEM((rows, 128), jnp.float32), pltpu.VMEM((rows, 128), jnp.float32)],
-        compiler_params=pltpu.CompilerParams(vmem_limit_bytes=wide_vmem),
-    )(saved, full, row_state, weight)
-
-
 def weights_kernel(totals_ref, row_new_ref, col_ref, gradient_ref, weight_ref, out_ref, col_new_ref, rows_ref, cols_ref):
     step = pl.program_id(0)
     tile = weight_ref.shape[1]
@@ -291,7 +216,7 @@
         out_ref[:, at : at + 128] = (weight - change).astype(jnp.bfloat16)
 
 
-def updated_weights(totals, row_new, col_state, gradient, weight, tile=512):
+def updated_weights(totals, row_new, col_state, gradient, weight, tile=1664):
     rows, width = weight.shape
     whole = lambda shape: pl.BlockSpec(shape, lambda i: (0,) * len(shape))
     block = pl.BlockSpec((rows, tile), lambda i: (0, i))
@@ -342,9 +267,8 @@
         both, head_weight, (((0,), (1,)), ((), ())), preferred_element_type=jnp.float32
     )
     keep, send = head_combine(where(0), product, sums, rows_local)
-    part = keep + lax.ppermute(send, "c", [(0, 1), (1, 0)]).astype(jnp.float32)
-    part = scattered([part[0]] + [part[k].astype(jnp.bfloat16) for k in range(1, 4)], "y")
-    part = scattered([part[0]] + [part[k].astype(jnp.bfloat16) for k in range(1, 4)], "z")
+    part = (keep + other_core(send).astype(jnp.float32)).astype(jnp.bfloat16)
+    part = swapped_chips(part.reshape(-1, rows_local, share)).astype(jnp.float32).sum(axis=0)
     carried = part.astype(jnp.bfloat16)
 
     chain = [carried]
@@ -358,9 +282,22 @@
     for distance in (1, 2):
         loss = loss + lax.ppermute(loss, "x", [(i, i ^ distance) for i in range(section_count)])
     loss = loss[0] / all_rows
-    full, loss = lax.optimization_barrier((full, loss))
-    gradient, row_new, totals = gradient_statistics(saved_all.T, full, row_state.T, local_weight)
+    weight_float = local_weight.astype(jnp.float32)
+    weight_part = jnp.broadcast_to(jnp.sum(weight_float * weight_float), (128,))
+    full, loss, weight_part = lax.optimization_barrier((full, loss, weight_part))
+    gradient = lax.dot_general(
+        saved_all, full, (((0,), (1,)), ((), ())), preferred_element_type=jnp.float32
+    )
+    squares = gradient * gradient
+    row_new = decay_rate * row_state[0] + (1.0 - decay_rate) * jnp.mean(squares + tiny_term, axis=1)
+    col_part = jnp.sum(squares + tiny_term, axis=0)
+    scaled_part = jnp.sum(squares * (1.0 / row_new)[:, None], axis=0)
+    row_part = jnp.broadcast_to(jnp.sum(row_new), (128,))
+    totals = jnp.stack(
+        [jnp.concatenate([col_part, row_part]), jnp.concatenate([scaled_part, weight_part])]
+    )
     totals = summed_tensor(totals)
+    row_new = row_new[:, None]
     backward = jnp.dot(local_weight, full, preferred_element_type=jnp.float32)
     outputs = (dy.astype(jnp.float32) + backward).astype(jnp.bfloat16)
     new_weight, col_new = updated_weights(totals, row_new, col_state, gradient, local_weight)

time: 285 us -> 281 us (0.986)
  blocking collectives: 0 us -> 103 us
  waiting for transfers between devices: 130 us -> 71.4 us
  starting transfers between devices: 66.8 us -> 19 us
  Pallas kernels: 51.9 us -> 33.7 us
  matrix products: 13.2 us -> 21.3 us
  other arithmetic: 2.75 us -> 7.94 us
  local copies, waits for them, and re-layouts: 1.45 us -> 6.31 us
    all_to_all x0 -> x5, blocking collectives: none -> 103 us  [swapped_chips(): return lax.all_to_all(blocks, chips, 0, 0, tiled=True)]
    ppermute x61 -> x7, waiting for transfers between devices: 85.5 us -> 13.1 us  [other_core(): return lax.ppermute(x, 'c', [(0, 1), (1, 0)])]
    ppermute x61 -> x7, starting transfers between devices: 56.7 us -> 0.64 us  [other_core(): return lax.ppermute(x, 'c', [(0, 1), (1, 0)])]
    pallas_call x1 -> x0, Pallas kernels: 14 us -> none  [gradient_statistics(): pl.pallas_call(statistics_kernel, grid=(width // tile,), in_specs=[whole(...]
    all_to_all x0 -> x2, waiting for transfers between devices: none -> 10.7 us  [swapped_chips(): return lax.all_to_all(blocks, chips, 0, 0, tiled=True)]
    all_to_all x0 -> x2, starting transfers between devices: none -> 8.22 us  [swapped_chips(): return lax.all_to_all(blocks, chips, 0, 0, tiled=True)]
    reduce_sum x0 -> x6, other arithmetic: none -> 5.62 us  [the longest x1 2.02 us: body(): weight_part = jnp.broadcast_to(jnp.sum(weight_float * weight_float), (128,))]
    dot_general x0 -> x1, matrix products: none -> 5.28 us  [body(): lax.dot_general(saved_all, full, (((0,), (1,)), ((), ())), preferred_elem...]
  transfers between devices with their start and end apart: 68 -> 16, of which waited for: 43 -> 13; matrix products, arithmetic and copies ran while one was open for 6% -> 8% of each run, Pallas kernels for 6% -> 6%
where the time goes in v2:
time: 281 us; the launch traced here: 280 us
  blocking collectives  103 us (37%)
  waiting for transfers between devices  71.4 us (25%)
  Pallas kernels  33.7 us (12%)
  matrix products  21.3 us (8%)
  starting transfers between devices  19 us (7%)
  between operations  17.3 us (6%)
  other arithmetic  7.94 us (3%)
  local copies, waits for them, and re-layouts  6.31 us (2%)
    all_to_all x5, blocking collectives, swapped_chips(): return lax.all_to_all(blocks, chips, 0, 0, tiled=True)  103 us
    all_gather x1, waiting for transfers between devices, body(): full = lax.all_gather(dy, ('y', 'z', 'c'), axis=0, tiled=True)  35.3 us
    ppermute x7, waiting for transfers between devices, other_core(): return lax.ppermute(x, 'c', [(0, 1), (1, 0)])  13.1 us
    pallas_call x1, Pallas kernels, head_logits(): pl.pallas_call(logits_kernel, grid_spec=pltpu.PrefetchScalarGridSpec(num_...  12.8 us
    dot_general x1, matrix products, body(): lax.dot_general(both, head_weight, (((0,), (1,)), ((), ())), preferred_el...  10.8 us
    all_to_all x2, waiting for transfers between devices, swapped_chips(): return lax.all_to_all(blocks, chips, 0, 0, tiled=True)  10.7 us
    pallas_call x3, Pallas kernels, layer_back(): pl.pallas_call(layer_kernel, grid_spec=pltpu.PrefetchScalarGridSpec(num_s...  10.5 us
    all_to_all x2, starting transfers between devices, swapped_chips(): return lax.all_to_all(blocks, chips, 0, 0, tiled=True)  8.22 us
  transfers between devices with their start and end apart: 16, of which 13 were waited for; matrix products, arithmetic and copies ran while one was open for 8% of the time, Pallas kernels for 6%

profile of v2, /device:TPU:0, one launch (start us, length us, event | category | flops | bytes accessed | tf_op | source)
XLA Modules:
  0.0 279.6 jit_solution(1631505158342878315)
XLA Ops:
  7.2 0.7 all-gather.3.cloned.1.call-update
  7.9 0.8 dynamic-slice_bitcast_fusion
  8.7 0.1 broadcast_in_dim.22
  8.9 22.7 %all_to_all.35.refs_0_ = bf16[16,208,128]{2,1,0:T(8,128)(2,1)S(1)} all-to-all(bf16[16,208,128]{2,1,0:T(8,128)(2,1)S(1)} %broadcast_in_dim.22), channel_id=1, replica_groups=mesh['x'=4,'y'=4,'z'=4,'c'=2] {'y','z'}, dimensions={0} | all-to-all | bytes 1703936 | tf_op jit(solution)/shard_map/all_to_all | solution.py:32
  31.6 0.1 stack.70.place_ref
  31.7 0.8 dynamic-slice_bitcast_fusion.1.refs_2_
  32.4 1.5 collective-permute-done.refs_1_
  33.9 12.8 %shard_map.110 = (bf16[1000,256]{1,0:T(8,128)(2,1)S(1)}, f32[2,128]{1,0:T(2,128)S(1)}) custom-call(s32[6]{0:T(128)S(1)} %stack.70.place_ref, bf16[16,208,128]{2,1,0:T(8,128)(2,1)S(1)} %all_to_all.35.refs_0_, bf16[16,208,128]{2,1,0:T(8,128)(2,1)S(1)} %collective-permute-done.refs_1_, s32[1,128]{1,0:T(1,128)S(1)} %dynamic-slice_bitcast_fusion.1.refs_2_, ...), custom_call_target="tpu_custom_call" | custom-call | tf_op jit(solution)/shard_map/pallas_call | solution.py:103
  46.8 0.2 collective-permute-start.1
  47.0 1.0 collective-permute-done.1
  48.0 0.6 broadcast_in_dim.24
  48.6 3.7 %all-to-all-start.1 = ((f32[16,2,128]{2,1,0:T(2,128)}), f32[16,2,128]{2,1,0:T(2,128)S(1)}, u32[]{:S(2)}, u32[]{:S(2)}) async-start(f32[16,2,128]{2,1,0:T(2,128)} %broadcast_in_dim.24), calls=%async_computation.1 | async-start | bytes 32768 | tf_op jit(solution)/shard_map/all_to_all | solution.py:32
  52.3 0.0 all-gather.5.cloned.1.call-start
  52.4 10.8 %fusion.7.product_ref = f32[256,6656]{1,0:T(8,128)} fusion(bf16[1000,256]{1,0:T(8,128)(2,1)S(1)} %get-tuple-element.14, bf16[6656,1000]{0,1:T(8,128)(2,1)} %param.9), kind=kOutput, calls=%fused_computation.34 | convolution fusion | flops 3407872000 | bytes 20639744 | tf_op jit(solution)/shard_map/dot_general | solution.py:266
  63.2 5.1 %shard_map.111 = (f32[4,4,208,128]{3,2,1,0:T(8,128)S(1)}, bf16[4,4,208,128]{3,2,1,0:T(8,128)(2,1)S(1)}) custom-call(s32[6]{0:T(128)S(1)} %stack.70.place_ref, f32[256,6656]{1,0:T(8,128)} %fusion.7.product_ref, f32[2,128]{1,0:T(2,128)S(1)} %reduce_sum.84.sums_ref), custom_call_target="tpu_custom_call" | custom-call | tf_op jit(solution)/shard_map/pallas_call | solution.py:145
  68.3 0.1 collective-permute-start.2
  68.4 2.4 collective-permute-done.2
  70.8 0.2 add_convert_fusion
  70.9 22.1 %all_to_all.36 = bf16[16,208,128]{2,1,0:T(8,128)(2,1)S(1)} all-to-all(bf16[16,208,128]{2,1,0:T(8,128)(2,1)S(1)} %bitcast.63), channel_id=1, replica_groups=mesh['x'=4,'y'=4,'z'=4,'c'=2] {'y','z'}, dimensions={0} | all-to-all | bytes 1703936 | tf_op jit(solution)/shard_map/all_to_all | solution.py:32
  93.1 0.1 reduce_sum.85.refs_2_
  93.2 0.1 broadcast_in_dim.25
  93.3 17.5 %all_to_all.37.refs_0_ = bf16[16,208,128]{2,1,0:T(8,128)(2,1)S(1)} all-to-all(bf16[16,208,128]{2,1,0:T(8,128)(2,1)S(1)} %broadcast_in_dim.25), channel_id=1, replica_groups=mesh['x'=4,'y'=4,'z'=4,'c'=2] {'y','z'}, dimensions={0} | all-to-all | bytes 1703936 | tf_op jit(solution)/shard_map/all_to_all | solution.py:32
  110.8 0.1 stack.69.place_ref
  110.9 2.3 collective-permute-done.3.refs_1_
  113.2 4.8 %all-gather.3.cloned.1.call-done.refs_3_ = bf16[4,208,6656]{2,1,0:T(8,128)(2,1)} async-done(((bf16[1,208,6656]{2,1,0:T(8,128)(2,1)}), bf16[4,208,6656]{2,1,0:T(8,128)(2,1)}) %all-gather.3.cloned.1.call-update) | async-done | bytes 11075600 | tf_op jit(solution)/shard_map/all_gather | solution.py:261
  118.0 3.3 %shard_map.112.refs_2_ = bf16[208,128]{1,0:T(8,128)(2,1)S(1)} custom-call(s32[6]{0:T(128)S(1)} %stack.69.place_ref, bf16[16,208,128]{2,1,0:T(8,128)(2,1)S(1)} %all_to_all.37.refs_0_, bf16[16,208,128]{2,1,0:T(8,128)(2,1)S(1)} %collective-permute-done.3.refs_1_, bf16[208,128]{1,0:T(8,128)(2,1)S(1)} %reduce_sum.85.refs_2_, ...), custom_call_target="tpu_custom_call" | custom-call | tf_op jit(solution)/shard_map/pallas_call | solution.py:176
  121.3 0.1 broadcast_in_dim.26
  121.5 21.6 %all_to_all.38.refs_0_ = bf16[16,208,128]{2,1,0:T(8,128)(2,1)S(1)} all-to-all(bf16[16,208,128]{2,1,0:T(8,128)(2,1)S(1)} %broadcast_in_dim.26), channel_id=1, replica_groups=mesh['x'=4,'y'=4,'z'=4,'c'=2] {'y','z'}, dimensions={0} | all-to-all | bytes 1703936 | tf_op jit(solution)/shard_map/all_to_all | solution.py:32
  143.0 0.1 stack.71.place_ref
  143.1 2.3 collective-permute-done.4.refs_1_
  145.4 3.3 %shard_map.113.refs_2_ = bf16[208,128]{1,0:T(8,128)(2,1)S(1)} custom-call(s32[6]{0:T(128)S(1)} %stack.71.place_ref, bf16[16,208,128]{2,1,0:T(8,128)(2,1)S(1)} %all_to_all.38.refs_0_, bf16[16,208,128]{2,1,0:T(8,128)(2,1)S(1)} %collective-permute-done.4.refs_1_, bf16[208,128]{1,0:T(8,128)(2,1)S(1)} %shard_map.112.refs_2_, ...), custom_call_target="tpu_custom_call" | custom-call | tf_op jit(solution)/shard_map/pallas_call | solution.py:176
  148.7 0.1 broadcast_in_dim.27
  148.8 18.7 %all_to_all.39.refs_0_ = bf16[16,208,128]{2,1,0:T(8,128)(2,1)} all-to-all(bf16[16,208,128]{2,1,0:T(8,128)(2,1)S(1)} %broadcast_in_dim.27), channel_id=1, replica_groups=mesh['x'=4,'y'=4,'z'=4,'c'=2] {'y','z'}, dimensions={0} | all-to-all | bytes 1703936 | tf_op jit(solution)/shard_map/all_to_all | solution.py:32
  167.5 0.1 stack.72.place_ref
  167.6 2.6 collective-permute-done.5.refs_1_
  170.3 3.8 %shard_map.114 = bf16[208,128]{1,0:T(8,128)(2,1)S(1)} custom-call(s32[6]{0:T(128)S(1)} %stack.72.place_ref, bf16[16,208,128]{2,1,0:T(8,128)(2,1)} %all_to_all.39.refs_0_, bf16[16,208,128]{2,1,0:T(8,128)(2,1)} %collective-permute-done.5.refs_1_, bf16[208,128]{1,0:T(8,128)(2,1)S(1)} %shard_map.113.refs_2_, ...), custom_call_target="tpu_custom_call" | custom-call | tf_op jit(solution)/shard_map/pallas_call | solution.py:176
  174.1 2.8 collective-permute-start.7
  176.9 3.2 %collective-permute-start.6 = (bf16[208,128]{1,0:T(8,128)(2,1)S(1)}, bf16[208,128]{1,0:T(8,128)(2,1)S(1)}, u32[]{:S(2)}, u32[]{:S(2)}) collective-permute-start(bf16[208,128]{1,0:T(8,128)(2,1)S(1)} %get-tuple-element.32), channel_id=1, source_target_pairs={{0,96},{32,0},{64,32},{96,64},{1,97},{33,1},{65,33},{97,65},{2,98}... | collective-permute-start | bytes 159752 | tf_op jit(solution)/shard_map/ppermute | solution.py:58
  180.1 2.1 collective-permute-done.8
  182.3 0.7 copy_bitcast_fusion
  183.0 2.0 multiply_reduce_fusion.1
  185.1 0.6 subtract_reduce_fusion
  185.7 3.6 %collective-permute-done.9 = f32[1]{0:T(128)} collective-permute-done((f32[1]{0:T(128)}, f32[1]{0:T(128)}, u32[]{:S(2)}, u32[]{:S(2)}) %collective-permute-start.9) | collective-permute-done | bytes 36 | tf_op jit(solution)/shard_map/ppermute | solution.py:283
  190.6 4.0 %collective-permute-start.10 = (f32[1]{0:T(128)}, f32[1]{0:T(128)}, u32[]{:S(2)}, u32[]{:S(2)}) collective-permute-start(f32[1]{0:T(128)} %add.57), channel_id=1, source_target_pairs={{0,64},{32,96},{64,0},{96,32},{1,65},{33,97},{65,1},{97,33},{2,66}... | collective-permute-start | bytes 20 | tf_op jit(solution)/shard_map/ppermute | solution.py:283
  194.6 1.0 collective-permute-done.10
  196.3 35.3 %all-gather.5.cloned.1.call-done = bf16[6656,512]{1,0:T(8,128)(2,1)} async-done(((bf16[208,512]{1,0:T(8,128)(2,1)}), bf16[6656,512]{1,0:T(8,128)(2,1)}) %all-gather.5.cloned.1.call-update) | async-done | bytes 6815760 | tf_op jit(solution)/shard_map/all_gather | solution.py:280
  231.6 0.6 broadcast_in_dim.29
  232.3 5.3 %add_reduce_fusion = (f32[208]{0:T(256)S(1)}, f32[208,6656]{1,0:T(8,128)S(1)}) fusion(bf16[6656,512]{1,0:T(8,128)(2,1)} %all-gather.5.cloned.1.call-done, bf16[1,512,208]{1,2,0:T(8,128)(2,1)S(1)} %copy-done), kind=kOutput, calls=%fused_computation.3 | convolution fusion | flops 1421827840 | bytes 12567360 | tf_op jit(solution)/shard_map/dot_general | solution.py:288
  237.6 0.6 fusion.5
  238.2 1.0 add_reduce_fusion.2
  239.2 0.7 copy-done.3
  239.9 1.0 add_reduce_fusion.1
  241.0 0.7 concatenate.6
  241.7 0.1 pad_maximum_fusion
  241.7 0.3 collective-permute-start.11
  242.1 1.0 collective-permute-done.11
  243.1 0.1 fusion.6
  243.1 1.1 broadcast_in_dim.31
  244.3 4.5 %all-to-all-start.6 = ((f32[16,2,6784]{2,1,0:T(2,128)}), f32[16,2,6784]{2,1,0:T(2,128)}, u32[]{:S(2)}, u32[]{:S(2)}) async-start(f32[16,2,6784]{2,1,0:T(2,128)} %broadcast_in_dim.31), calls=%async_computation.6 | async-start | bytes 1736704 | tf_op jit(solution)/shard_map/all_to_all | solution.py:32
  248.8 0.1 copy.29.row_new_ref
  249.0 5.2 %fusion.2 = bf16[1,512,208]{1,2,0:T(8,128)(2,1)} fusion(bf16[6656,512]{1,0:T(8,128)(2,1)} %all-gather.5.cloned.1.call-done, bf16[1,208,6656]{2,1,0:T(8,128)(2,1)S(1)} %copy-done.1, bf16[208,1,128]{2,0,1:T(8,128)(2,1)S(1)} %get-tuple-element.28, bf16[208,1,128]{2,0,1:T(8,128)(2,1)S(1)} %get-tuple-element.29, bf16[208,1,128]{2,0,1:T(8,128)(2,1)S(1)} %get-tuple-element.27, ...), kind=kOutput, calls=%fused_computation.9 | convolution fusion | flops 1418313728 | bytes 10010624 | tf_op jit(solution)/shard_map/dot_general | solution.py:301
  254.2 10.7 %all-to-all-done.6 = f32[16,2,6784]{2,1,0:T(2,128)} async-done(((f32[16,2,6784]{2,1,0:T(2,128)}), f32[16,2,6784]{2,1,0:T(2,128)}, u32[]{:S(2)}, u32[]{:S(2)}) %all-to-all-start.6) | async-done | bytes 868384 | tf_op jit(solution)/shard_map/all_to_all | solution.py:32
  264.9 1.4 reduce_sum.92.totals_ref
  266.4 5.3 %shard_map.115 = (bf16[208,6656]{1,0:T(8,128)(2,1)}, f32[1,6656]{1,0:T(1,128)}) custom-call(f32[2,6784]{1,0:T(2,128)S(1)} %reduce_sum.92.totals_ref, f32[208,1]{1,0:T(8,128)S(1)} %copy.29.row_new_ref, f32[1,6656]{1,0:T(1,128)S(1)} %copy-done.2, f32[208,6656]{1,0:T(8,128)} %copy-done.3, bf16[208,6656]{1,0:T(8,128)(2,1)S(1)} %bitcast.61), custom_call_target="tpu_custom_call" | custom-call | tf_op jit(solution)/shard_map/pallas_call | solution.py:223
  (30 shorter events, 0.3 us)
Async XLA Ops:
  7.2 225.1 %copy-start = (bf16[1,512,208]{1,2,0:T(8,128)(2,1)S(1)}, bf16[1,512,208]{1,2,0:T(8,128)(2,1)}, u32[]{:S(2)}) copy-start(bf16[1,512,208]{1,2,0:T(8,128)(2,1)} %param.10) | copy-start | bytes 638980
  7.2 110.8 %all-gather.3.cloned.1.call-start = ((), (), s32[]{:S(2)}) async-start(), calls=%async_computation.7 | async-start | bytes 13844480 | tf_op jit(solution)/shard_map/all_gather | solution.py:261
  31.6 2.4 collective-permute-start
  46.8 1.2 collective-permute-start.1
  48.6 14.6 %all-to-all-start.1 = ((f32[16,2,128]{2,1,0:T(2,128)}), f32[16,2,128]{2,1,0:T(2,128)S(1)}, u32[]{:S(2)}, u32[]{:S(2)}) async-start(f32[16,2,128]{2,1,0:T(2,128)} %broadcast_in_dim.24), calls=%async_computation.1 | async-start | bytes 32768 | tf_op jit(solution)/shard_map/all_to_all | solution.py:32
  52.3 179.2 %all-gather.5.cloned.1.call-start = ((), (), s32[]{:S(2)}) async-start(), calls=%async_computation.8 | async-start | bytes 7028736 | tf_op jit(solution)/shard_map/all_gather | solution.py:280
  68.3 2.5 collective-permute-start.2
  110.8 2.4 collective-permute-start.3
  143.0 2.4 collective-permute-start.4
  167.5 2.7 collective-permute-start.5
  167.6 15.4 %copy-start.1 = (bf16[1,208,6656]{2,1,0:T(8,128)(2,1)S(1)}, bf16[1,208,6656]{2,1,0:T(8,128)(2,1)}, u32[]{:S(2)}) copy-start(bf16[1,208,6656]{2,1,0:T(8,128)(2,1)} %param.11) | copy-start | bytes 8306692
  174.1 6.0 %collective-permute-start.7 = (bf16[208,128]{1,0:T(8,128)(2,1)S(1)}, bf16[208,128]{1,0:T(8,128)(2,1)S(1)}, u32[]{:S(2)}, u32[]{:S(2)}) collective-permute-start(bf16[208,128]{1,0:T(8,128)(2,1)S(1)} %get-tuple-element.31), channel_id=1, source_target_pairs={{0,64},{32,96},{64,0},{96,32},{1,65},{33,97},{65,1},{97,33},{2,66}... | collective-permute-start | bytes 159752 | tf_op jit(solution)/shard_map/ppermute | solution.py:58
  176.9 5.3 %collective-permute-start.8 = (bf16[208,128]{1,0:T(8,128)(2,1)S(1)}, bf16[208,128]{1,0:T(8,128)(2,1)S(1)}, u32[]{:S(2)}, u32[]{:S(2)}) collective-permute-start(bf16[208,128]{1,0:T(8,128)(2,1)S(1)} %get-tuple-element.30), channel_id=1, source_target_pairs={{0,32},{32,64},{64,96},{96,0},{1,33},{33,65},{65,97},{97,1},{2,34}... | collective-permute-start | bytes 159752 | tf_op jit(solution)/shard_map/ppermute | solution.py:58
  176.9 5.3 %collective-permute-start.6 = (bf16[208,128]{1,0:T(8,128)(2,1)S(1)}, bf16[208,128]{1,0:T(8,128)(2,1)S(1)}, u32[]{:S(2)}, u32[]{:S(2)}) collective-permute-start(bf16[208,128]{1,0:T(8,128)(2,1)S(1)} %get-tuple-element.32), channel_id=1, source_target_pairs={{0,96},{32,0},{64,32},{96,64},{1,97},{33,1},{65,33},{97,65},{2,98}... | collective-permute-start | bytes 159752 | tf_op jit(solution)/shard_map/ppermute | solution.py:58
  185.7 3.6 %collective-permute-start.9 = (f32[1]{0:T(128)}, f32[1]{0:T(128)}, u32[]{:S(2)}, u32[]{:S(2)}) collective-permute-start(f32[1]{0:T(128)} %bitcast.12), channel_id=1, source_target_pairs={{0,32},{32,0},{64,96},{96,64},{1,33},{33,1},{65,97},{97,65},{2,34}... | collective-permute-start | bytes 20 | tf_op jit(solution)/shard_map/ppermute | solution.py:283
  190.6 5.1 %collective-permute-start.10 = (f32[1]{0:T(128)}, f32[1]{0:T(128)}, u32[]{:S(2)}, u32[]{:S(2)}) collective-permute-start(f32[1]{0:T(128)} %add.57), channel_id=1, source_target_pairs={{0,64},{32,96},{64,0},{96,32},{1,65},{33,97},{65,1},{97,33},{2,66}... | collective-permute-start | bytes 20 | tf_op jit(solution)/shard_map/ppermute | solution.py:283
  232.3 5.3 %copy-start.4 = (f32[1,208]{1,0:T(1,128)S(1)}, f32[1,208]{1,0:T(1,128)}, u32[]{:S(2)}) copy-start(f32[1,208]{1,0:T(1,128)} %param.12) | copy-start | bytes 2500
  237.5 2.4 copy-start.3
  241.7 1.3 collective-permute-start.11
  244.3 20.7 %all-to-all-start.6 = ((f32[16,2,6784]{2,1,0:T(2,128)}), f32[16,2,6784]{2,1,0:T(2,128)}, u32[]{:S(2)}, u32[]{:S(2)}) async-start(f32[16,2,6784]{2,1,0:T(2,128)} %broadcast_in_dim.31), calls=%async_computation.6 | async-start | bytes 1736704 | tf_op jit(solution)/shard_map/all_to_all | solution.py:32
  248.9 17.4 %copy-start.2 = (f32[1,6656]{1,0:T(1,128)S(1)}, f32[1,6656]{1,0:T(1,128)}, u32[]{:S(2)}) copy-start(f32[1,6656]{1,0:T(1,128)} %col_ref.1) | copy-start | bytes 79876
Sparse Core Ops, SparseCore 0:
  9.7 108.2 all-gather.2
  183.2 48.3 all-gather.4

commit v3 on v2

--- a/solution.py
+++ b/solution.py
@@ -44,6 +44,13 @@
 
 def summed_tensor(x):
     return jnp.sum(from_chips(x + other_core(x)), axis=0)
+
+
+def summed_ring(x, axis):
+    one, two, three = (
+        lax.ppermute(x, axis, [(i, (i - step) % 4) for i in range(4)]) for step in (1, 2, 3)
+    )
+    return (x + two) + (one + three)
 
 
 def exchanged(blocks, axis):
@@ -70,55 +77,24 @@
             full_ref[pl.ds(start, rows), :] = pieces[side][chip]
 
 
-def logits_kernel(place_ref, *refs):
-    pieces, (labels_ref, weight_ref, both_ref, sums_ref, full_ref, total_ref) = refs[:2], refs[2:]
-    step = pl.program_id(0)
-    depth = weight_ref.shape[1]
-    share = labels_ref.shape[1]
-
-    @pl.when(step == 0)
-    def _():
-        place(pieces, place_ref, full_ref)
-        total_ref[...] = jnp.zeros_like(total_ref)
-
-    rows = full_ref[pl.ds(pl.multiple_of(step * depth, depth), depth), :]
-    total_ref[...] += jnp.dot(weight_ref[...], rows, preferred_element_type=jnp.float32)
-
-    @pl.when(step == pl.num_programs(0) - 1)
-    def _():
-        logits = total_ref[...]
-        exponent = jnp.exp(logits)
-        columns = place_ref[3] + lax.broadcasted_iota(jnp.int32, logits.shape, 0)
-        label_hit = columns == labels_ref[...]
-        sums_ref[0:1, :] = jnp.sum(exponent, axis=0, keepdims=True)
-        sums_ref[1:2, :] = jnp.sum(jnp.where(label_hit, logits, 0.0), axis=0, keepdims=True)
-        both_ref[:, :share] = jnp.minimum(exponent, bf16_largest).astype(jnp.bfloat16)
-        both_ref[:, share:] = jnp.where(label_hit, 1.0, 0.0).astype(jnp.bfloat16)
-
-
-def head_logits(where, pieces, labels, weight, tile=512):
-    vocab_local, model_width = weight.shape
-    share = labels.shape[1]
+def order_kernel(place_ref, *refs):
+    place(refs[:2], place_ref, refs[2])
+
+
+def in_order(where, pieces):
+    count, rows, tokens = pieces[0].shape
     whole = lambda shape: pl.BlockSpec(shape, lambda i, s: (0,) * len(shape))
     return pl.pallas_call(
-        logits_kernel,
+        order_kernel,
         grid_spec=pltpu.PrefetchScalarGridSpec(
             num_scalar_prefetch=1,
-            grid=(model_width // tile,),
-            in_specs=[whole(p.shape) for p in pieces]
-            + [whole(labels.shape), pl.BlockSpec((vocab_local, tile), lambda i, s: (0, i))],
-            out_specs=[whole((vocab_local, 2 * share)), whole((2, share))],
-            scratch_shapes=[
-                pltpu.VMEM((model_width, share), jnp.bfloat16),
-                pltpu.VMEM((vocab_local, share), jnp.float32),
-            ],
-        ),
-        out_shape=[
-            jax.ShapeDtypeStruct((vocab_local, 2 * share), jnp.bfloat16),
-            jax.ShapeDtypeStruct((2, share), jnp.float32),
-        ],
+            grid=(1,),
+            in_specs=[whole(p.shape) for p in pieces],
+            out_specs=whole((2 * count * rows, tokens)),
+        ),
+        out_shape=jax.ShapeDtypeStruct((2 * count * rows, tokens), jnp.bfloat16),
         compiler_params=pltpu.CompilerParams(vmem_limit_bytes=wide_vmem),
-    )(where, *pieces, labels, weight)
+    )(where, *pieces)
 
 
 def combine_kernel(place_ref, product_ref, sums_ref, keep_ref, send_ref, turned_ref):
@@ -260,9 +236,24 @@
 
     all_weights = lax.all_gather(local_weight, "x", axis=0)
     hidden_rows = lax.dynamic_slice_in_dim(hidden_last, row_start, share, 0).T
-    labels_here = lax.dynamic_slice_in_dim(labels, row_start, share, 0)[None, :]
-    both, sums = head_logits(where(0), tensor_pieces(hidden_rows), labels_here, head_weight.T)
+    labels_here = lax.dynamic_slice_in_dim(labels, row_start, share, 0)
+    hidden_all = in_order(where(0), tensor_pieces(hidden_rows))
+    logits = lax.dot_general(
+        head_weight, hidden_all, (((0,), (0,)), ((), ())), preferred_element_type=jnp.float32
+    )
+    exponent = jnp.exp(logits)
+    columns = tensor_index * vocab_local + lax.iota(jnp.int32, vocab_local)
+    label_hit = labels_here[None, :] == columns[:, None]
+    sums = jnp.stack(
+        [
+            jnp.sum(exponent, axis=0),
+            jnp.sum(jnp.where(label_hit, logits, jnp.zeros_like(logits)), axis=0),
+        ]
+    )
     sums = summed_tensor(sums)
+    both = jnp.concatenate(
+        [jnp.minimum(exponent, bf16_largest).astype(jnp.bfloat16), label_hit.astype(jnp.bfloat16)], axis=1
+    )
     product = lax.dot_general(
         both, head_weight, (((0,), (1,)), ((), ())), preferred_element_type=jnp.float32
     )
@@ -296,7 +287,8 @@
     totals = jnp.stack(
         [jnp.concatenate([col_part, row_part]), jnp.concatenate([scaled_part, weight_part])]
     )
-    totals = summed_tensor(totals)
+    totals = totals + other_core(totals)
+    totals = summed_ring(summed_ring(totals, "z"), "y")
     row_new = row_new[:, None]
     backward = jnp.dot(local_weight, full, preferred_element_type=jnp.float32)
     outputs = (dy.astype(jnp.float32) + backward).astype(jnp.bfloat16)

time: 281 us -> 273 us (0.972)
  Pallas kernels: 33.7 us -> 21.6 us
  matrix products: 21.3 us -> 27.4 us
  starting transfers between devices: 19 us -> 22.7 us
    pallas_call x1, Pallas kernels: 12.8 us -> 0.67 us  [in_order(): pl.pallas_call(order_kernel, grid_spec=pltpu.PrefetchScalarGridSpec(num_s...]
    all_to_all x2 -> x1, waiting for transfers between devices: 10.7 us -> 0.01 us  [swapped_chips(): return lax.all_to_all(blocks, chips, 0, 0, tiled=True)]
    dot_general x0 -> x1, matrix products: none -> 8.54 us  [body(): lax.dot_general(head_weight, hidden_all, (((0,), (0,)), ((), ())), prefer...]
    ppermute x0 -> x6, starting transfers between devices: none -> 8.22 us  [summed_ring(): lax.ppermute(x, axis, [(i, (i - step) % 4) for i in range(4)])]
    ppermute x0 -> x6, waiting for transfers between devices: none -> 5.1 us  [summed_ring(): lax.ppermute(x, axis, [(i, (i - step) % 4) for i in range(4)])]
    all_to_all x2 -> x1, starting transfers between devices: 8.22 us -> 3.59 us  [swapped_chips(): return lax.all_to_all(blocks, chips, 0, 0, tiled=True)]
    all_gather x1, waiting for transfers between devices: 4.83 us -> 8.49 us  [body(): all_weights = lax.all_gather(local_weight, 'x', axis=0)]
    dot_general x1, matrix products: 5.23 us -> 2.32 us  [body(): backward = jnp.dot(local_weight, full, preferred_element_type=jnp.float32)]
  transfers between devices with their start and end apart: 16 -> 21, of which waited for: 13 -> 15; matrix products, arithmetic and copies ran while one was open for 8% -> 10% of each run, Pallas kernels for 6% -> 2%
where the time goes in v3:
time: 273 us; the launch traced here: 272 us
  blocking collectives  103 us (38%)
  waiting for transfers between devices  69.1 us (25%)
  matrix products  27.4 us (10%)
  starting transfers between devices  22.7 us (8%)
  Pallas kernels  21.6 us (8%)
  between operations  17.4 us (6%)
  other arithmetic  6.92 us (3%)
  local copies, waits for them, and re-layouts  4.61 us (2%)
    all_to_all x5, blocking collectives, swapped_chips(): return lax.all_to_all(blocks, chips, 0, 0, tiled=True)  103 us
    all_gather x1, waiting for transfers between devices, body(): full = lax.all_gather(dy, ('y', 'z', 'c'), axis=0, tiled=True)  35 us
    ppermute x7, waiting for transfers between devices, other_core(): return lax.ppermute(x, 'c', [(0, 1), (1, 0)])  12.7 us
    dot_general x1, matrix products, body(): lax.dot_general(both, head_weight, (((0,), (1,)), ((), ())), preferred_el...  10.8 us
    pallas_call x3, Pallas kernels, layer_back(): pl.pallas_call(layer_kernel, grid_spec=pltpu.PrefetchScalarGridSpec(num_s...  10.5 us
    dot_general x1, matrix products, body(): lax.dot_general(head_weight, hidden_all, (((0,), (0,)), ((), ())), prefer...  8.54 us
    all_gather x1, waiting for transfers between devices, body(): all_weights = lax.all_gather(local_weight, 'x', axis=0)  8.49 us
    ppermute x6, starting transfers between devices, summed_ring(): lax.ppermute(x, axis, [(i, (i - step) % 4) for i in range(4)])  8.22 us
  transfers between devices with their start and end apart: 21, of which 15 were waited for; matrix products, arithmetic and copies ran while one was open for 10% of the time, Pallas kernels for 2%

profile of v3, /device:TPU:0, one launch (start us, length us, event | category | flops | bytes accessed | tf_op | source)
XLA Modules:
  0.0 272.2 jit_solution(5502569609015354104)
XLA Ops:
  7.2 0.7 all-gather.3.cloned.1.call-update
  7.9 0.8 dynamic-slice_bitcast_fusion
  8.7 0.1 broadcast_in_dim.20
  8.9 22.7 %all_to_all.30.refs_0_ = bf16[16,208,128]{2,1,0:T(8,128)(2,1)S(1)} all-to-all(bf16[16,208,128]{2,1,0:T(8,128)(2,1)S(1)} %broadcast_in_dim.20), channel_id=1, replica_groups=mesh['x'=4,'y'=4,'z'=4,'c'=2] {'y','z'}, dimensions={0} | all-to-all | bytes 1703936 | tf_op jit(solution)/shard_map/all_to_all | solution.py:32
  31.6 0.8 dynamic_slice.7
  32.4 1.5 collective-permute-done.refs_1_
  33.9 0.7 shard_map.110
  34.6 8.5 %exponential_reduce_fusion = (f32[128]{0:T(128)S(1)}, f32[128]{0:T(128)S(1)}, bf16[1000,128]{1,0:T(8,128)(2,1)S(1)}) fusion(s32[1000]{0:T(1024)S(1)} %iota_add_fusion, s32[128]{0:T(128)S(1)} %dynamic_slice.7, bf16[6656,128]{1,0:T(8,128)(2,1)S(1)} %shard_map.110, bf16[6656,1000]{0,1:T(8,128)(2,1)} %param.9), kind=kOutput, calls=%fused_computation.19 | convolution fusion | flops 1704703744 | bytes 15277472 | tf_op jit(solution)/shard_map/dot_general | solution.py:241
  43.2 0.3 collective-permute-start.1
  43.4 0.2 compare_convert_fusion
  43.6 0.8 collective-permute-done.1
  44.4 0.6 broadcast_in_dim.22
  45.0 3.6 %all-to-all-start.1 = ((f32[16,2,128]{2,1,0:T(2,128)}), f32[16,2,128]{2,1,0:T(2,128)S(1)}, u32[]{:S(2)}, u32[]{:S(2)}) async-start(f32[16,2,128]{2,1,0:T(2,128)} %broadcast_in_dim.22), calls=%async_computation.1 | async-start | bytes 32768 | tf_op jit(solution)/shard_map/all_to_all | solution.py:32
  48.7 10.8 %fusion.4.product_ref = f32[256,6656]{1,0:T(8,128)} fusion(bf16[6656,1000]{0,1:T(8,128)(2,1)} %param.9, bf16[1000,128]{1,0:T(8,128)(2,1)S(1)} %compare_convert_fusion, bf16[1000,128]{1,0:T(8,128)(2,1)S(1)} %get-tuple-element.25), kind=kOutput, calls=%fused_computation.14 | convolution fusion | flops 3408896000 | bytes 20639744 | tf_op jit(solution)/shard_map/dot_general | solution.py:257
  59.5 5.1 %shard_map.111 = (f32[4,4,208,128]{3,2,1,0:T(8,128)S(1)}, bf16[4,4,208,128]{3,2,1,0:T(8,128)(2,1)S(1)}) custom-call(s32[6]{0:T(128)S(1)} %stack.79.place_ref, f32[256,6656]{1,0:T(8,128)} %fusion.4.product_ref, f32[2,128]{1,0:T(2,128)S(1)} %reduce_sum.95.sums_ref), custom_call_target="tpu_custom_call" | custom-call | tf_op jit(solution)/shard_map/pallas_call | solution.py:121
  64.6 0.2 collective-permute-start.2
  64.8 2.2 collective-permute-done.2
  67.1 0.2 add_convert_fusion
  67.3 22.1 %all_to_all.31 = bf16[16,208,128]{2,1,0:T(8,128)(2,1)S(1)} all-to-all(bf16[16,208,128]{2,1,0:T(8,128)(2,1)S(1)} %bitcast.64), channel_id=1, replica_groups=mesh['x'=4,'y'=4,'z'=4,'c'=2] {'y','z'}, dimensions={0} | all-to-all | bytes 1703936 | tf_op jit(solution)/shard_map/all_to_all | solution.py:32
  89.4 0.1 reduce_sum.96.refs_2_
  89.5 0.1 broadcast_in_dim.23
  89.6 17.5 %all_to_all.32.refs_0_ = bf16[16,208,128]{2,1,0:T(8,128)(2,1)S(1)} all-to-all(bf16[16,208,128]{2,1,0:T(8,128)(2,1)S(1)} %broadcast_in_dim.23), channel_id=1, replica_groups=mesh['x'=4,'y'=4,'z'=4,'c'=2] {'y','z'}, dimensions={0} | all-to-all | bytes 1703936 | tf_op jit(solution)/shard_map/all_to_all | solution.py:32
  107.2 2.3 collective-permute-done.3.refs_1_
  109.5 8.5 %all-gather.3.cloned.1.call-done.refs_3_ = bf16[4,208,6656]{2,1,0:T(8,128)(2,1)} async-done(((bf16[1,208,6656]{2,1,0:T(8,128)(2,1)}), bf16[4,208,6656]{2,1,0:T(8,128)(2,1)}) %all-gather.3.cloned.1.call-update) | async-done | bytes 11075600 | tf_op jit(solution)/shard_map/all_gather | solution.py:237
  118.0 3.3 %shard_map.112.refs_2_ = bf16[208,128]{1,0:T(8,128)(2,1)S(1)} custom-call(s32[6]{0:T(128)S(1)} %stack.78.place_ref, bf16[16,208,128]{2,1,0:T(8,128)(2,1)S(1)} %all_to_all.32.refs_0_, bf16[16,208,128]{2,1,0:T(8,128)(2,1)S(1)} %collective-permute-done.3.refs_1_, bf16[208,128]{1,0:T(8,128)(2,1)S(1)} %reduce_sum.96.refs_2_, ...), custom_call_target="tpu_custom_call" | custom-call | tf_op jit(solution)/shard_map/pallas_call | solution.py:152
  121.3 0.1 broadcast_in_dim.24
  121.5 21.6 %all_to_all.33.refs_0_ = bf16[16,208,128]{2,1,0:T(8,128)(2,1)S(1)} all-to-all(bf16[16,208,128]{2,1,0:T(8,128)(2,1)S(1)} %broadcast_in_dim.24), channel_id=1, replica_groups=mesh['x'=4,'y'=4,'z'=4,'c'=2] {'y','z'}, dimensions={0} | all-to-all | bytes 1703936 | tf_op jit(solution)/shard_map/all_to_all | solution.py:32
  143.1 2.3 collective-permute-done.4.refs_1_
  145.4 3.3 %shard_map.113.refs_2_ = bf16[208,128]{1,0:T(8,128)(2,1)S(1)} custom-call(s32[6]{0:T(128)S(1)} %stack.83.place_ref, bf16[16,208,128]{2,1,0:T(8,128)(2,1)S(1)} %all_to_all.33.refs_0_, bf16[16,208,128]{2,1,0:T(8,128)(2,1)S(1)} %collective-permute-done.4.refs_1_, bf16[208,128]{1,0:T(8,128)(2,1)S(1)} %shard_map.112.refs_2_, ...), custom_call_target="tpu_custom_call" | custom-call | tf_op jit(solution)/shard_map/pallas_call | solution.py:152
  148.7 0.1 broadcast_in_dim.25
  148.8 18.7 %all_to_all.34.refs_0_ = bf16[16,208,128]{2,1,0:T(8,128)(2,1)} all-to-all(bf16[16,208,128]{2,1,0:T(8,128)(2,1)S(1)} %broadcast_in_dim.25), channel_id=1, replica_groups=mesh['x'=4,'y'=4,'z'=4,'c'=2] {'y','z'}, dimensions={0} | all-to-all | bytes 1703936 | tf_op jit(solution)/shard_map/all_to_all | solution.py:32
  167.6 2.6 collective-permute-done.5.refs_1_
  170.3 3.8 %shard_map.114 = bf16[208,128]{1,0:T(8,128)(2,1)S(1)} custom-call(s32[6]{0:T(128)S(1)} %stack.84.place_ref, bf16[16,208,128]{2,1,0:T(8,128)(2,1)} %all_to_all.34.refs_0_, bf16[16,208,128]{2,1,0:T(8,128)(2,1)} %collective-permute-done.5.refs_1_, bf16[208,128]{1,0:T(8,128)(2,1)S(1)} %shard_map.113.refs_2_, ...), custom_call_target="tpu_custom_call" | custom-call | tf_op jit(solution)/shard_map/pallas_call | solution.py:152
  174.1 2.8 %collective-permute-start.7 = (bf16[208,128]{1,0:T(8,128)(2,1)S(1)}, bf16[208,128]{1,0:T(8,128)(2,1)S(1)}, u32[]{:S(2)}, u32[]{:S(2)}) collective-permute-start(bf16[208,128]{1,0:T(8,128)(2,1)S(1)} %get-tuple-element.30), channel_id=1, source_target_pairs={{0,64},{32,96},{64,0},{96,32},{1,65},{33,97},{65,1},{97,33},{2,66}... | collective-permute-start | bytes 159752 | tf_op jit(solution)/shard_map/ppermute | solution.py:65
  176.9 3.2 %collective-permute-start.6 = (bf16[208,128]{1,0:T(8,128)(2,1)S(1)}, bf16[208,128]{1,0:T(8,128)(2,1)S(1)}, u32[]{:S(2)}, u32[]{:S(2)}) collective-permute-start(bf16[208,128]{1,0:T(8,128)(2,1)S(1)} %get-tuple-element.31), channel_id=1, source_target_pairs={{0,96},{32,0},{64,32},{96,64},{1,97},{33,1},{65,33},{97,65},{2,98}... | collective-permute-start | bytes 159752 | tf_op jit(solution)/shard_map/ppermute | solution.py:65
  180.1 2.1 collective-permute-done.8
  182.3 0.7 copy_bitcast_fusion
  183.1 2.0 multiply_reduce_fusion.1
  185.1 0.6 subtract_reduce_fusion
  185.7 3.8 %collective-permute-done.9 = f32[1]{0:T(128)} collective-permute-done((f32[1]{0:T(128)}, f32[1]{0:T(128)}, u32[]{:S(2)}, u32[]{:S(2)}) %collective-permute-start.9) | collective-permute-done | bytes 36 | tf_op jit(solution)/shard_map/ppermute | solution.py:274
  190.7 4.0 %collective-permute-start.10 = (f32[1]{0:T(128)}, f32[1]{0:T(128)}, u32[]{:S(2)}, u32[]{:S(2)}) collective-permute-start(f32[1]{0:T(128)} %add.87), channel_id=1, source_target_pairs={{0,64},{32,96},{64,0},{96,32},{1,65},{33,97},{65,1},{97,33},{2,66}... | collective-permute-start | bytes 20 | tf_op jit(solution)/shard_map/ppermute | solution.py:274
  194.8 1.2 collective-permute-done.10
  196.6 35.0 %all-gather.5.cloned.1.call-done = bf16[6656,512]{1,0:T(8,128)(2,1)} async-done(((bf16[208,512]{1,0:T(8,128)(2,1)}), bf16[6656,512]{1,0:T(8,128)(2,1)}) %all-gather.5.cloned.1.call-update) | async-done | bytes 6815760 | tf_op jit(solution)/shard_map/all_gather | solution.py:271
  231.6 0.8 broadcast_in_dim.27
  232.4 5.7 %add_reduce_fusion = (f32[208]{0:T(256)S(1)}, f32[208,6656]{1,0:T(8,128)S(1)}) fusion(bf16[6656,512]{1,0:T(8,128)(2,1)} %all-gather.5.cloned.1.call-done, bf16[1,512,208]{1,2,0:T(8,128)(2,1)S(1)} %copy-done), kind=kOutput, calls=%fused_computation.3 | convolution fusion | flops 1421827840 | bytes 12567360 | tf_op jit(solution)/shard_map/dot_general | solution.py:279
  238.2 0.6 fusion.12
  238.8 1.0 add_reduce_fusion.2
  239.8 1.0 add_reduce_fusion.1
  240.9 0.7 concatenate.10
  241.6 0.3 collective-permute-start.11
  241.9 1.0 collective-permute-done.11
  243.0 1.9 collective-permute-start.13
  245.0 0.1 collective-permute-start.14
  245.1 2.1 collective-permute-start.12
  247.2 2.3 fusion.2
  249.5 1.5 collective-permute-done.14
  251.1 0.1 add_add_fusion.1
  251.2 1.8 collective-permute-start.16
  252.9 0.3 collective-permute-start.17
  253.3 2.0 collective-permute-start.15
  255.2 0.1 copy.27.row_new_ref
  255.4 2.9 %collective-permute-done.17 = f32[2,6784]{1,0:T(2,128)S(1)} collective-permute-done((f32[2,6784]{1,0:T(2,128)S(1)}, f32[2,6784]{1,0:T(2,128)S(1)}, u32[]{:S(2)}, u32[]{:S(2)}) %collective-permute-start.17) | collective-permute-done | bytes 54304 | tf_op jit(solution)/shard_map/ppermute | solution.py:51
  258.3 0.6 collective-permute-done.15
  259.0 5.3 %shard_map.115 = (bf16[208,6656]{1,0:T(8,128)(2,1)}, f32[1,6656]{1,0:T(1,128)}) custom-call(f32[2,6784]{1,0:T(2,128)S(1)} %add_add_fusion.totals_ref, f32[208,1]{1,0:T(8,128)S(1)} %copy.27.row_new_ref, f32[1,6656]{1,0:T(1,128)S(1)} %copy-done.2, f32[208,6656]{1,0:T(8,128)} %copy-done.3, bf16[208,6656]{1,0:T(8,128)(2,1)S(1)} %bitcast.63), custom_call_target="tpu_custom_call" | custom-call | tf_op jit(solution)/shard_map/pallas_call | solution.py:199
  (49 shorter events, 0.9 us)
Async XLA Ops:
  7.2 225.2 %copy-start = (bf16[1,512,208]{1,2,0:T(8,128)(2,1)S(1)}, bf16[1,512,208]{1,2,0:T(8,128)(2,1)}, u32[]{:S(2)}) copy-start(bf16[1,512,208]{1,2,0:T(8,128)(2,1)} %param.10) | copy-start | bytes 638980
  7.2 110.8 %all-gather.3.cloned.1.call-start = ((), (), s32[]{:S(2)}) async-start(), calls=%async_computation.6 | async-start | bytes 13844480 | tf_op jit(solution)/shard_map/all_gather | solution.py:237
  31.6 2.4 collective-permute-start
  43.2 1.2 collective-permute-start.1
  45.0 14.4 %all-to-all-start.1 = ((f32[16,2,128]{2,1,0:T(2,128)}), f32[16,2,128]{2,1,0:T(2,128)S(1)}, u32[]{:S(2)}, u32[]{:S(2)}) async-start(f32[16,2,128]{2,1,0:T(2,128)} %broadcast_in_dim.22), calls=%async_computation.1 | async-start | bytes 32768 | tf_op jit(solution)/shard_map/all_to_all | solution.py:32
  48.6 183.0 %all-gather.5.cloned.1.call-start = ((), (), s32[]{:S(2)}) async-start(), calls=%async_computation.7 | async-start | bytes 7028736 | tf_op jit(solution)/shard_map/all_gather | solution.py:271
  64.6 2.5 collective-permute-start.2
  107.1 2.4 collective-permute-start.3
  143.0 2.4 collective-permute-start.4
  167.5 2.7 collective-permute-start.5
  167.6 15.4 %copy-start.1 = (bf16[1,208,6656]{2,1,0:T(8,128)(2,1)S(1)}, bf16[1,208,6656]{2,1,0:T(8,128)(2,1)}, u32[]{:S(2)}) copy-start(bf16[1,208,6656]{2,1,0:T(8,128)(2,1)} %param.11) | copy-start | bytes 8306692
  174.1 6.0 %collective-permute-start.7 = (bf16[208,128]{1,0:T(8,128)(2,1)S(1)}, bf16[208,128]{1,0:T(8,128)(2,1)S(1)}, u32[]{:S(2)}, u32[]{:S(2)}) collective-permute-start(bf16[208,128]{1,0:T(8,128)(2,1)S(1)} %get-tuple-element.30), channel_id=1, source_target_pairs={{0,64},{32,96},{64,0},{96,32},{1,65},{33,97},{65,1},{97,33},{2,66}... | collective-permute-start | bytes 159752 | tf_op jit(solution)/shard_map/ppermute | solution.py:65
  176.9 5.3 %collective-permute-start.8 = (bf16[208,128]{1,0:T(8,128)(2,1)S(1)}, bf16[208,128]{1,0:T(8,128)(2,1)S(1)}, u32[]{:S(2)}, u32[]{:S(2)}) collective-permute-start(bf16[208,128]{1,0:T(8,128)(2,1)S(1)} %get-tuple-element.29), channel_id=1, source_target_pairs={{0,32},{32,64},{64,96},{96,0},{1,33},{33,65},{65,97},{97,1},{2,34}... | collective-permute-start | bytes 159752 | tf_op jit(solution)/shard_map/ppermute | solution.py:65
  176.9 5.3 %collective-permute-start.6 = (bf16[208,128]{1,0:T(8,128)(2,1)S(1)}, bf16[208,128]{1,0:T(8,128)(2,1)S(1)}, u32[]{:S(2)}, u32[]{:S(2)}) collective-permute-start(bf16[208,128]{1,0:T(8,128)(2,1)S(1)} %get-tuple-element.31), channel_id=1, source_target_pairs={{0,96},{32,0},{64,32},{96,64},{1,97},{33,1},{65,33},{97,65},{2,98}... | collective-permute-start | bytes 159752 | tf_op jit(solution)/shard_map/ppermute | solution.py:65
  185.7 3.8 %collective-permute-start.9 = (f32[1]{0:T(128)}, f32[1]{0:T(128)}, u32[]{:S(2)}, u32[]{:S(2)}) collective-permute-start(f32[1]{0:T(128)} %bitcast.13), channel_id=1, source_target_pairs={{0,32},{32,0},{64,96},{96,64},{1,33},{33,1},{65,97},{97,65},{2,34}... | collective-permute-start | bytes 20 | tf_op jit(solution)/shard_map/ppermute | solution.py:274
  190.7 5.2 %collective-permute-start.10 = (f32[1]{0:T(128)}, f32[1]{0:T(128)}, u32[]{:S(2)}, u32[]{:S(2)}) collective-permute-start(f32[1]{0:T(128)} %add.87), channel_id=1, source_target_pairs={{0,64},{32,96},{64,0},{96,32},{1,65},{33,97},{65,1},{97,33},{2,66}... | collective-permute-start | bytes 20 | tf_op jit(solution)/shard_map/ppermute | solution.py:274
  231.6 15.6 %slice-start = ((s8[6815744]{0:T(1024)(128)(4,1)}), s8[4194304]{0:T(1024)(128)(4,1)S(1)}, s32[]{:S(2)}) async-start(s8[6815744]{0:T(1024)(128)(4,1)} %bitcast.72), calls=%async_computation.8 | async-start | bytes 8388608
  232.4 5.8 %copy-start.4 = (f32[1,208]{1,0:T(1,128)S(1)}, f32[1,208]{1,0:T(1,128)}, u32[]{:S(2)}) copy-start(f32[1,208]{1,0:T(1,128)} %param.12) | copy-start | bytes 2500
  232.4 14.8 %slice-start.1 = ((s8[6815744]{0:T(1024)(128)(4,1)}), s8[2621440]{0:T(1024)(128)(4,1)S(1)}, s32[]{:S(2)}) async-start(s8[6815744]{0:T(1024)(128)(4,1)} %bitcast.72), calls=%async_computation.9 | async-start | bytes 5242880
  238.1 11.4 %copy-start.3 = (f32[208,6656]{1,0:T(8,128)}, f32[208,6656]{1,0:T(8,128)S(1)}, u32[]{:S(2)}) copy-start(f32[208,6656]{1,0:T(8,128)S(1)} %get-tuple-element.37.gradient_ref) | copy-start | bytes 16613380
  241.6 1.3 collective-permute-start.11
  243.0 16.0 %copy-start.2 = (f32[1,6656]{1,0:T(1,128)S(1)}, f32[1,6656]{1,0:T(1,128)}, u32[]{:S(2)}) copy-start(f32[1,6656]{1,0:T(1,128)} %col_ref.1) | copy-start | bytes 79876
  243.0 6.5 %collective-permute-start.13 = (f32[2,6784]{1,0:T(2,128)S(1)}, f32[2,6784]{1,0:T(2,128)S(1)}, u32[]{:S(2)}, u32[]{:S(2)}) collective-permute-start(f32[2,6784]{1,0:T(2,128)S(1)} %fusion.13), channel_id=1, source_target_pairs={{0,6},{2,0},{4,2},{6,4},{1,7},{3,1},{5,3},{7,5},{8,14},{10,8},{12,... | collective-permute-start | bytes 162824 | tf_op jit(solution)/shard_map/ppermute | solution.py:51
  245.0 6.1 %collective-permute-start.14 = (f32[2,6784]{1,0:T(2,128)S(1)}, f32[2,6784]{1,0:T(2,128)S(1)}, u32[]{:S(2)}, u32[]{:S(2)}) collective-permute-start(f32[2,6784]{1,0:T(2,128)S(1)} %fusion.13), channel_id=1, source_target_pairs={{0,2},{2,4},{4,6},{6,0},{1,3},{3,5},{5,7},{7,1},{8,10},{10,12},{12... | collective-permute-start | bytes 162824 | tf_op jit(solution)/shard_map/ppermute | solution.py:51
  245.1 6.0 %collective-permute-start.12 = (f32[2,6784]{1,0:T(2,128)S(1)}, f32[2,6784]{1,0:T(2,128)S(1)}, u32[]{:S(2)}, u32[]{:S(2)}) collective-permute-start(f32[2,6784]{1,0:T(2,128)S(1)} %fusion.13), channel_id=1, source_target_pairs={{0,4},{2,6},{4,0},{6,2},{1,5},{3,7},{5,1},{7,3},{8,12},{10,14},{12... | collective-permute-start | bytes 162824 | tf_op jit(solution)/shard_map/ppermute | solution.py:51
  251.2 4.2 %collective-permute-start.16 = (f32[2,6784]{1,0:T(2,128)S(1)}, f32[2,6784]{1,0:T(2,128)S(1)}, u32[]{:S(2)}, u32[]{:S(2)}) collective-permute-start(f32[2,6784]{1,0:T(2,128)S(1)} %add_add_fusion.1), channel_id=1, source_target_pairs={{0,24},{8,0},{16,8},{24,16},{1,25},{9,1},{17,9},{25,17},{2,26},{10... | collective-permute-start | bytes 162824 | tf_op jit(solution)/shard_map/ppermute | solution.py:51
  252.9 5.4 %collective-permute-start.17 = (f32[2,6784]{1,0:T(2,128)S(1)}, f32[2,6784]{1,0:T(2,128)S(1)}, u32[]{:S(2)}, u32[]{:S(2)}) collective-permute-start(f32[2,6784]{1,0:T(2,128)S(1)} %add_add_fusion.1), channel_id=1, source_target_pairs={{0,8},{8,16},{16,24},{24,0},{1,9},{9,17},{17,25},{25,1},{2,10},{10... | collective-permute-start | bytes 162824 | tf_op jit(solution)/shard_map/ppermute | solution.py:51
  253.3 5.6 %collective-permute-start.15 = (f32[2,6784]{1,0:T(2,128)S(1)}, f32[2,6784]{1,0:T(2,128)S(1)}, u32[]{:S(2)}, u32[]{:S(2)}) collective-permute-start(f32[2,6784]{1,0:T(2,128)S(1)} %add_add_fusion.1), channel_id=1, source_target_pairs={{0,16},{8,24},{16,0},{24,8},{1,17},{9,25},{17,1},{25,9},{2,18},{10... | collective-permute-start | bytes 162824 | tf_op jit(solution)/shard_map/ppermute | solution.py:51
Sparse Core Ops, SparseCore 0:
  9.7 108.2 all-gather.2
  183.2 48.3 all-gather.4

commit v4 on v3

--- a/solution.py
+++ b/solution.py
@@ -141,30 +141,30 @@
 def layer_kernel(place_ref, *refs):
     pieces, (carried_ref, weight_ref, out_ref, full_ref) = refs[:2], refs[2:]
     place(pieces, place_ref, full_ref)
-    backward = jnp.dot(weight_ref[0], full_ref[...], preferred_element_type=jnp.float32)
-    out_ref[...] = (carried_ref[...].astype(jnp.float32) + backward).astype(jnp.bfloat16)
-
-
-def layer_back(where, carried, all_weights):
+    total = carried_ref[...].astype(jnp.float32)
+    quarter = weight_ref.shape[2]
+    for part in range(weight_ref.shape[0]):
+        rows = full_ref[part * quarter : (part + 1) * quarter, :]
+        total = total + jnp.dot(weight_ref[part], rows, preferred_element_type=jnp.float32)
+    out_ref[...] = total.astype(jnp.bfloat16)
+
+
+def layer_back(where, carried, weight):
     pieces = tensor_pieces(carried)
-    rows_local, model_width = all_weights.shape[1:]
+    width = weight.shape[0] * weight.shape[2]
     whole = lambda shape: pl.BlockSpec(shape, lambda i, s: (0,) * len(shape))
     return pl.pallas_call(
         layer_kernel,
         grid_spec=pltpu.PrefetchScalarGridSpec(
             num_scalar_prefetch=1,
             grid=(1,),
-            in_specs=[whole(p.shape) for p in pieces]
-            + [
-                whole(carried.shape),
-                pl.BlockSpec((1, rows_local, model_width), lambda i, s: (s[5], 0, 0)),
-            ],
+            in_specs=[whole(p.shape) for p in pieces] + [whole(carried.shape), whole(weight.shape)],
             out_specs=whole(carried.shape),
-            scratch_shapes=[pltpu.VMEM((model_width, carried.shape[1]), jnp.bfloat16)],
+            scratch_shapes=[pltpu.VMEM((width, carried.shape[1]), jnp.bfloat16)],
         ),
         out_shape=jax.ShapeDtypeStruct(carried.shape, jnp.bfloat16),
         compiler_params=pltpu.CompilerParams(vmem_limit_bytes=wide_vmem),
-    )(where, *pieces, carried, all_weights)
+    )(where, *pieces, carried, weight)
 
 
 def weights_kernel(totals_ref, row_new_ref, col_ref, gradient_ref, weight_ref, out_ref, col_new_ref, rows_ref, cols_ref):
@@ -234,10 +234,22 @@
             ]
         )
 
-    all_weights = lax.all_gather(local_weight, "x", axis=0)
+    quarter = model_width // section_count
+    last = section_count - 1
+    own_last = local_weight[:, last * quarter :]
+    parts_last = []
+    for step in range(1, section_count):
+        target = (last + step) % section_count
+        part = local_weight[:, target * quarter : (target + 1) * quarter]
+        parts_last.append(lax.ppermute(part, "x", [(last, target)]))
     hidden_rows = lax.dynamic_slice_in_dim(hidden_last, row_start, share, 0).T
     labels_here = lax.dynamic_slice_in_dim(labels, row_start, share, 0)
-    hidden_all = in_order(where(0), tensor_pieces(hidden_rows))
+    hidden_chips, parts_last = lax.optimization_barrier((from_chips(hidden_rows), parts_last))
+    part = own_last
+    for target in range(last):
+        part = jnp.where(section_index == target, parts_last[target], part)
+    all_weights = {last: lax.all_gather(part, "x", axis=0)}
+    hidden_all = in_order(where(0), [hidden_chips, other_core(hidden_chips)])
     logits = lax.dot_general(
         head_weight, hidden_all, (((0,), (0,)), ((), ())), preferred_element_type=jnp.float32
     )
@@ -262,9 +274,23 @@
     part = swapped_chips(part.reshape(-1, rows_local, share)).astype(jnp.float32).sum(axis=0)
     carried = part.astype(jnp.bfloat16)
 
+    held = []
+    for step in range(section_count):
+        start = (section_index + step) % section_count * quarter
+        part = lax.dynamic_slice_in_dim(local_weight, start, quarter, 1)
+        if step:
+            part = lax.ppermute(part, "x", [(i, (i + step) % section_count) for i in range(1, last)])
+        held.append(part)
+    held, carried = lax.optimization_barrier((held, carried))
+    for layer in reversed(range(1, last)):
+        part = held[0]
+        for step in range(1, section_count):
+            part = jnp.where(section_index == (layer + step) % section_count, held[step], part)
+        all_weights[layer] = lax.all_gather(part, "x", axis=0)
+
     chain = [carried]
     for layer in reversed(range(1, section_count)):
-        carried = layer_back(where(layer), carried, all_weights)
+        carried = layer_back(where(layer), carried, all_weights[layer])
         chain.insert(0, carried)
 
     dy = exchanged(chain, "x").reshape(rows_local, all_rows)

time: 273 us -> 331 us (1.21)
  waiting for transfers between devices: 69.1 us -> 125 us
  blocking collectives: 103 us -> 58.1 us
  starting transfers between devices: 22.7 us -> 48 us
  local copies, waits for them, and re-layouts: 4.61 us -> 15.5 us
  other arithmetic: 6.92 us -> 15.8 us
    ppermute x0 -> x6, waiting for transfers between devices: none -> 53.5 us  [the longest x3 37.7 us: body(): lax.ppermute(part, 'x', [(i, (i + step) % section_count) for i in range(1...]
    all_to_all x5 -> x3, blocking collectives: 103 us -> 58.1 us  [swapped_chips(): return lax.all_to_all(blocks, chips, 0, 0, tiled=True)]
    all_to_all x1 -> x3, starting transfers between devices: 3.59 us -> 22.4 us  [swapped_chips(): return lax.all_to_all(blocks, chips, 0, 0, tiled=True)]
    all_to_all x1 -> x3, waiting for transfers between devices: 0.01 us -> 10 us  [swapped_chips(): return lax.all_to_all(blocks, chips, 0, 0, tiled=True)]
    ppermute x0 -> x6, starting transfers between devices: none -> 8.4 us  [the longest x3 4.33 us: body(): parts_last.append(lax.ppermute(part, 'x', [(last, target)]))]
    all_gather x1 -> x3, waiting for transfers between devices: 8.49 us -> 0.44 us  [the longest x2 0.44 us: body(): all_weights[layer] = lax.all_gather(part, 'x', axis=0)]
    unnamed x14 -> x22, local copies, waits for them, and re-layouts: 0.04 us -> 6.58 us
    select_n x0 -> x2, other arithmetic: none -> 5.15 us  [the longest x1 3.03 us: body(): jnp.where(section_index == (layer + step) % section_count, held[step], part)]
  transfers between devices with their start and end apart: 21 -> 31, of which waited for: 15 -> 19; matrix products, arithmetic and copies ran while one was open for 10% -> 12% of each run, Pallas kernels for 2% -> 4%
where the time goes in v4:
time: 331 us; the launch traced here: 329 us
  waiting for transfers between devices  125 us (38%)
  blocking collectives  58.1 us (18%)
  starting transfers between devices  48 us (15%)
  matrix products  27.2 us (8%)
  Pallas kernels  22.4 us (7%)
  between operations  17.2 us (5%)
  other arithmetic  15.8 us (5%)
  local copies, waits for them, and re-layouts  15.5 us (5%)
    all_to_all x3, blocking collectives, swapped_chips(): return lax.all_to_all(blocks, chips, 0, 0, tiled=True)  58.1 us
    ppermute x3, waiting for transfers between devices, body(): lax.ppermute(part, 'x', [(i, (i + step) % section_count) for i in range(1...  37.7 us
    all_gather x1, waiting for transfers between devices, body(): full = lax.all_gather(dy, ('y', 'z', 'c'), axis=0, tiled=True)  37.3 us
    all_to_all x3, starting transfers between devices, swapped_chips(): return lax.all_to_all(blocks, chips, 0, 0, tiled=True)  22.4 us
    ppermute x3, waiting for transfers between devices, body(): parts_last.append(lax.ppermute(part, 'x', [(last, target)]))  15.9 us
    ppermute x7, waiting for transfers between devices, other_core(): return lax.ppermute(x, 'c', [(0, 1), (1, 0)])  11.7 us
    dot_general x1, matrix products, body(): lax.dot_general(both, head_weight, (((0,), (1,)), ((), ())), preferred_el...  10.7 us
    all_to_all x3, waiting for transfers between devices, swapped_chips(): return lax.all_to_all(blocks, chips, 0, 0, tiled=True)  10 us
  transfers between devices with their start and end apart: 31, of which 19 were waited for; matrix products, arithmetic and copies ran while one was open for 12% of the time, Pallas kernels for 4%

profile of v4, /device:TPU:0, one launch (start us, length us, event | category | flops | bytes accessed | tf_op | source)
XLA Modules:
  0.0 329.5 jit_solution(5497401039830420306)
XLA Ops:
  7.2 1.0 dynamic-slice_bitcast_fusion.4
  8.2 1.0 broadcast_in_dim.20
  9.2 8.2 %all-to-all-start = ((bf16[16,208,128]{2,1,0:T(8,128)(2,1)}), bf16[16,208,128]{2,1,0:T(8,128)(2,1)}, u32[]{:S(2)}, u32[]{:S(2)}) async-start(bf16[16,208,128]{2,1,0:T(8,128)(2,1)} %broadcast_in_dim.20), calls=%async_computation | async-start | bytes 1703936 | tf_op jit(solution)/shard_map/all_to_all | solution.py:32
  17.4 1.7 fusion.16
  19.1 1.3 collective-permute-start.3
  20.4 1.5 collective-permute-start.4
  21.9 1.5 collective-permute-start.5
  23.4 15.9 %collective-permute-done.3 = bf16[208,1664]{1,0:T(8,128)(2,1)} collective-permute-done((bf16[208,1664]{1,0:T(8,128)(2,1)S(1)}, bf16[208,1664]{1,0:T(8,128)(2,1)}, u32[]{:S(2)}, u32[]{:S(2)}) %collective-permute-start.3) | collective-permute-done | bytes 692256 | tf_op jit(solution)/shard_map/ppermute | solution.py:244
  39.4 0.8 dynamic_slice.35
  40.3 2.1 fusion.4
  42.4 2.1 shard_map.110
  44.5 8.4 %exponential_reduce_fusion = (f32[128]{0:T(128)S(1)}, f32[128]{0:T(128)S(1)}, bf16[1000,128]{1,0:T(8,128)(2,1)S(1)}) fusion(s32[1000]{0:T(1024)S(1)} %iota_add_fusion, s32[128]{0:T(128)S(1)} %dynamic_slice.35, bf16[6656,128]{1,0:T(8,128)(2,1)S(1)} %shard_map.110, bf16[6656,1000]{0,1:T(8,128)(2,1)} %param.9), kind=kOutput, calls=%fused_computation.28 | convolution fusion | flops 1704703744 | bytes 15277472 | tf_op jit(solution)/shard_map/dot_general | solution.py:253
  54.9 6.9 %all-to-all-start.1 = ((f32[16,2,128]{2,1,0:T(2,128)}), f32[16,2,128]{2,1,0:T(2,128)S(1)}, u32[]{:S(2)}, u32[]{:S(2)}) async-start(f32[16,2,128]{2,1,0:T(2,128)} %broadcast_in_dim.22), calls=%async_computation.1 | async-start | bytes 32768 | tf_op jit(solution)/shard_map/all_to_all | solution.py:32
  61.8 10.7 %fusion.6.product_ref = f32[256,6656]{1,0:T(8,128)} fusion(bf16[6656,1000]{0,1:T(8,128)(2,1)} %param.9, bf16[1000,128]{1,0:T(8,128)(2,1)S(1)} %compare_convert_fusion, bf16[1000,128]{1,0:T(8,128)(2,1)S(1)} %get-tuple-element.52), kind=kOutput, calls=%fused_computation.23 | convolution fusion | flops 3408896000 | bytes 20639744 | tf_op jit(solution)/shard_map/dot_general | solution.py:269
  72.6 5.9 %shard_map.111 = (f32[4,4,208,128]{3,2,1,0:T(8,128)S(1)}, bf16[4,4,208,128]{3,2,1,0:T(8,128)(2,1)}) custom-call(s32[6]{0:T(128)S(1)} %stack.79.place_ref, f32[256,6656]{1,0:T(8,128)} %fusion.6.product_ref, f32[2,128]{1,0:T(2,128)S(1)} %reduce_sum.95.sums_ref), custom_call_target="tpu_custom_call" | custom-call | tf_op jit(solution)/shard_map/pallas_call | solution.py:121
  78.5 1.2 copy-done.5
  79.7 2.7 collective-permute-done.8
  82.4 2.8 add_convert_fusion
  85.2 7.3 %all-to-all-start.2 = ((bf16[16,208,128]{2,1,0:T(8,128)(2,1)}), bf16[16,208,128]{2,1,0:T(8,128)(2,1)}, u32[]{:S(2)}, u32[]{:S(2)}) async-start(bf16[16,208,128]{2,1,0:T(8,128)(2,1)} %bitcast.80), calls=%async_computation.2 | async-start | bytes 1703936 | tf_op jit(solution)/shard_map/all_to_all | solution.py:32
  92.5 1.6 dynamic-slice_bitcast_fusion
  94.1 1.5 collective-permute-start
  95.6 1.3 collective-permute-start.1
  96.9 1.3 collective-permute-start.2
  98.2 10.0 %all-to-all-done.2 = bf16[16,208,128]{2,1,0:T(8,128)(2,1)} async-done(((bf16[16,208,128]{2,1,0:T(8,128)(2,1)}), bf16[16,208,128]{2,1,0:T(8,128)(2,1)}, u32[]{:S(2)}, u32[]{:S(2)}) %all-to-all-start.2) | async-done | bytes 852000 | tf_op jit(solution)/shard_map/all_to_all | solution.py:32
  108.3 1.3 reduce_sum.96.refs_2_
  109.6 35.9 %collective-permute-done.1 = bf16[208,1664]{1,0:T(8,128)(2,1)} collective-permute-done((bf16[208,1664]{1,0:T(8,128)(2,1)}, bf16[208,1664]{1,0:T(8,128)(2,1)}, u32[]{:S(2)}, u32[]{:S(2)}) %collective-permute-start.1) | collective-permute-done | bytes 692256 | tf_op jit(solution)/shard_map/ppermute | solution.py:282
  145.4 1.8 collective-permute-done.2
  147.2 3.0 select_select_fusion
  150.4 20.4 %all_to_all.30.refs_0_ = bf16[16,208,128]{2,1,0:T(8,128)(2,1)} all-to-all(bf16[16,208,128]{2,1,0:T(8,128)(2,1)S(1)} %broadcast_in_dim.23), channel_id=1, replica_groups=mesh['x'=4,'y'=4,'z'=4,'c'=2] {'y','z'}, dimensions={0} | all-to-all | bytes 1703936 | tf_op jit(solution)/shard_map/all_to_all | solution.py:32
  171.0 2.6 collective-permute-done.9.refs_1_
  173.6 1.8 copy-done.2
  175.4 3.0 shard_map.112.refs_2_
  178.5 18.7 %all_to_all.31.refs_0_ = bf16[16,208,128]{2,1,0:T(8,128)(2,1)} all-to-all(bf16[16,208,128]{2,1,0:T(8,128)(2,1)S(1)} %broadcast_in_dim.24), channel_id=1, replica_groups=mesh['x'=4,'y'=4,'z'=4,'c'=2] {'y','z'}, dimensions={0} | all-to-all | bytes 1703936 | tf_op jit(solution)/shard_map/all_to_all | solution.py:32
  197.3 2.6 collective-permute-done.10.refs_1_
  200.0 1.8 copy-done.4
  201.7 3.0 shard_map.113.refs_2_
  204.9 19.0 %all_to_all.32.refs_0_ = bf16[16,208,128]{2,1,0:T(8,128)(2,1)} all-to-all(bf16[16,208,128]{2,1,0:T(8,128)(2,1)S(1)} %broadcast_in_dim.25), channel_id=1, replica_groups=mesh['x'=4,'y'=4,'z'=4,'c'=2] {'y','z'}, dimensions={0} | all-to-all | bytes 1703936 | tf_op jit(solution)/shard_map/all_to_all | solution.py:32
  224.4 2.2 collective-permute-done.11.refs_1_
  226.6 1.8 copy-done.3
  228.4 3.0 shard_map.114
  231.6 3.2 collective-permute-start.12
  234.8 2.7 collective-permute-done.13
  237.9 0.7 copy_bitcast_fusion
  238.6 2.0 multiply_reduce_fusion.1
  241.2 1.3 collective-permute-start.15
  242.5 2.3 collective-permute-done.15
  246.1 3.2 collective-permute-start.16
  249.3 1.9 collective-permute-done.16
  251.8 37.3 %all-gather.8.cloned.1.call-done = bf16[6656,512]{1,0:T(8,128)(2,1)} async-done(((bf16[208,512]{1,0:T(8,128)(2,1)}), bf16[6656,512]{1,0:T(8,128)(2,1)}) %all-gather.8.cloned.1.call-update) | async-done | bytes 6815760 | tf_op jit(solution)/shard_map/all_gather | solution.py:297
  289.2 0.8 broadcast_in_dim.27
  290.0 5.7 %add_reduce_fusion = (f32[208]{0:T(256)S(1)}, f32[208,6656]{1,0:T(8,128)S(1)}) fusion(bf16[6656,512]{1,0:T(8,128)(2,1)} %all-gather.8.cloned.1.call-done, bf16[1,512,208]{1,2,0:T(8,128)(2,1)S(1)} %copy-done), kind=kOutput, calls=%fused_computation.3 | convolution fusion | flops 1421827840 | bytes 12567360 | tf_op jit(solution)/shard_map/dot_general | solution.py:305
  296.4 1.0 add_reduce_fusion.2
  297.4 1.0 add_reduce_fusion.1
  298.4 0.7 concatenate.10
  299.5 1.0 collective-permute-done.17
  300.6 1.9 collective-permute-start.19
  302.7 2.1 collective-permute-start.18
  304.8 2.3 fusion.2
  307.0 1.6 collective-permute-done.20
  308.7 1.8 collective-permute-start.22
  310.8 2.0 collective-permute-start.21
  312.9 2.9 collective-permute-done.23
  315.8 0.6 collective-permute-done.21
  316.5 5.3 %shard_map.115 = (bf16[208,6656]{1,0:T(8,128)(2,1)}, f32[1,6656]{1,0:T(1,128)}) custom-call(f32[2,6784]{1,0:T(2,128)S(1)} %add_add_fusion.totals_ref, f32[208,1]{1,0:T(8,128)S(1)} %copy.24.row_new_ref, f32[1,6656]{1,0:T(1,128)S(1)} %copy-done.6, f32[208,6656]{1,0:T(8,128)} %copy-done.7, bf16[208,6656]{1,0:T(8,128)(2,1)S(1)} %bitcast.76), custom_call_target="tpu_custom_call" | custom-call | tf_op jit(solution)/shard_map/pallas_call | solution.py:199
  (81 shorter events, 6.7 us)
Async XLA Ops:
  7.2 282.8 %copy-start = (bf16[1,512,208]{1,2,0:T(8,128)(2,1)S(1)}, bf16[1,512,208]{1,2,0:T(8,128)(2,1)}, u32[]{:S(2)}) copy-start(bf16[1,512,208]{1,2,0:T(8,128)(2,1)} %param.10) | copy-start | bytes 638980
  7.2 33.1 %copy-start.1 = (bf16[1,208,6656]{2,1,0:T(8,128)(2,1)S(1)}, bf16[1,208,6656]{2,1,0:T(8,128)(2,1)}, u32[]{:S(2)}) copy-start(bf16[1,208,6656]{2,1,0:T(8,128)(2,1)} %param.11) | copy-start | bytes 8306692
  9.2 30.1 %all-to-all-start = ((bf16[16,208,128]{2,1,0:T(8,128)(2,1)}), bf16[16,208,128]{2,1,0:T(8,128)(2,1)}, u32[]{:S(2)}, u32[]{:S(2)}) async-start(bf16[16,208,128]{2,1,0:T(8,128)(2,1)} %broadcast_in_dim.20), calls=%async_computation | async-start | bytes 1703936 | tf_op jit(solution)/shard_map/all_to_all | solution.py:32
  17.4 153.6 %all-gather.10.cloned.1.call-start = ((), (), s32[]{:S(2)}) async-start(), calls=%async_computation.7 | async-start | bytes 3461120 | tf_op jit(solution)/shard_map/all_gather | solution.py:251
  19.1 20.2 %collective-permute-start.3 = (bf16[208,1664]{1,0:T(8,128)(2,1)S(1)}, bf16[208,1664]{1,0:T(8,128)(2,1)}, u32[]{:S(2)}, u32[]{:S(2)}) collective-permute-start(bf16[208,1664]{1,0:T(8,128)(2,1)S(1)} %get-tuple-element.47), channel_id=1, source_target_pairs={{96,0},{97,1},{98,2},{99,3},{100,4},{101,5},{102,6},{103,7},{104,8... | collective-permute-start | bytes 2076680 | tf_op jit(solution)/shard_map/ppermute | solution.py:244
  20.4 18.9 %collective-permute-start.4 = (bf16[208,1664]{1,0:T(8,128)(2,1)S(1)}, bf16[208,1664]{1,0:T(8,128)(2,1)}, u32[]{:S(2)}, u32[]{:S(2)}) collective-permute-start(bf16[208,1664]{1,0:T(8,128)(2,1)S(1)} %get-tuple-element.46), channel_id=1, source_target_pairs={{96,32},{97,33},{98,34},{99,35},{100,36},{101,37},{102,38},{103,39... | collective-permute-start | bytes 2076680 | tf_op jit(solution)/shard_map/ppermute | solution.py:244
  21.9 17.4 %collective-permute-start.5 = (bf16[208,1664]{1,0:T(8,128)(2,1)S(1)}, bf16[208,1664]{1,0:T(8,128)(2,1)}, u32[]{:S(2)}, u32[]{:S(2)}) collective-permute-start(bf16[208,1664]{1,0:T(8,128)(2,1)S(1)} %get-tuple-element.45), channel_id=1, source_target_pairs={{96,64},{97,65},{98,66},{99,67},{100,68},{101,69},{102,70},{103,71... | collective-permute-start | bytes 2076680 | tf_op jit(solution)/shard_map/ppermute | solution.py:244
  39.3 3.1 collective-permute-start.6
  52.9 1.4 collective-permute-start.7
  54.9 17.6 %all-to-all-start.1 = ((f32[16,2,128]{2,1,0:T(2,128)}), f32[16,2,128]{2,1,0:T(2,128)S(1)}, u32[]{:S(2)}, u32[]{:S(2)}) async-start(f32[16,2,128]{2,1,0:T(2,128)} %broadcast_in_dim.22), calls=%async_computation.1 | async-start | bytes 32768 | tf_op jit(solution)/shard_map/all_to_all | solution.py:32
  78.5 1.2 copy-start.5
  79.7 2.7 collective-permute-start.8
  85.2 23.1 %all-to-all-start.2 = ((bf16[16,208,128]{2,1,0:T(8,128)(2,1)}), bf16[16,208,128]{2,1,0:T(8,128)(2,1)}, u32[]{:S(2)}, u32[]{:S(2)}) async-start(bf16[16,208,128]{2,1,0:T(8,128)(2,1)} %bitcast.80), calls=%async_computation.2 | async-start | bytes 1703936 | tf_op jit(solution)/shard_map/all_to_all | solution.py:32
  92.5 107.5 %all-gather.12.cloned.1.call-start = ((), (), s32[]{:S(2)}) async-start(), calls=%async_computation.8 | async-start | bytes 3461120 | tf_op jit(solution)/shard_map/all_gather | solution.py:289
  94.1 15.4 %collective-permute-start = (bf16[208,1664]{1,0:T(8,128)(2,1)}, bf16[208,1664]{1,0:T(8,128)(2,1)}, u32[]{:S(2)}, u32[]{:S(2)}) collective-permute-start(bf16[208,1664]{1,0:T(8,128)(2,1)} %get-tuple-element.50), channel_id=1, source_target_pairs={{32,64},{64,96},{33,65},{65,97},{34,66},{66,98},{35,67},{67,99},{3... | collective-permute-start | bytes 2076680 | tf_op jit(solution)/shard_map/ppermute | solution.py:282
  95.6 49.8 %collective-permute-start.1 = (bf16[208,1664]{1,0:T(8,128)(2,1)}, bf16[208,1664]{1,0:T(8,128)(2,1)}, u32[]{:S(2)}, u32[]{:S(2)}) collective-permute-start(bf16[208,1664]{1,0:T(8,128)(2,1)} %get-tuple-element.49), channel_id=1, source_target_pairs={{32,96},{64,0},{33,97},{65,1},{34,98},{66,2},{35,99},{67,3},{36,10... | collective-permute-start | bytes 2076680 | tf_op jit(solution)/shard_map/ppermute | solution.py:282
  96.9 50.3 %collective-permute-start.2 = (bf16[208,1664]{1,0:T(8,128)(2,1)}, bf16[208,1664]{1,0:T(8,128)(2,1)}, u32[]{:S(2)}, u32[]{:S(2)}) collective-permute-start(bf16[208,1664]{1,0:T(8,128)(2,1)} %get-tuple-element.48), channel_id=1, source_target_pairs={{32,0},{64,32},{33,1},{65,33},{34,2},{66,34},{35,3},{67,35},{36,4}... | collective-permute-start | bytes 2076680 | tf_op jit(solution)/shard_map/ppermute | solution.py:282
  150.3 74.1 %all-gather.14.cloned.1.call-start = ((), (), s32[]{:S(2)}) async-start(), calls=%async_computation.9 | async-start | bytes 3461120 | tf_op jit(solution)/shard_map/all_gather | solution.py:289
  170.8 2.7 collective-permute-start.9
  170.9 118.3 %all-gather.8.cloned.1.call-start = ((), (), s32[]{:S(2)}) async-start(), calls=%async_computation.6 | async-start | bytes 7028736 | tf_op jit(solution)/shard_map/all_gather | solution.py:297
  173.6 1.8 copy-start.2
  197.2 2.7 collective-permute-start.10
  200.0 1.8 copy-start.4
  223.8 2.7 collective-permute-start.11
  226.6 1.8 copy-start.3
  231.4 6.1 %collective-permute-start.13 = (bf16[208,128]{1,0:T(8,128)(2,1)S(1)}, bf16[208,128]{1,0:T(8,128)(2,1)S(1)}, u32[]{:S(2)}, u32[]{:S(2)}) collective-permute-start(bf16[208,128]{1,0:T(8,128)(2,1)S(1)} %get-tuple-element.57), channel_id=1, source_target_pairs={{0,64},{32,96},{64,0},{96,32},{1,65},{33,97},{65,1},{97,33},{2,66}... | collective-permute-start | bytes 159752 | tf_op jit(solution)/shard_map/ppermute | solution.py:65
  231.5 6.3 %collective-permute-start.14 = (bf16[208,128]{1,0:T(8,128)(2,1)S(1)}, bf16[208,128]{1,0:T(8,128)(2,1)S(1)}, u32[]{:S(2)}, u32[]{:S(2)}) collective-permute-start(bf16[208,128]{1,0:T(8,128)(2,1)S(1)} %get-tuple-element.56), channel_id=1, source_target_pairs={{0,32},{32,64},{64,96},{96,0},{1,33},{33,65},{65,97},{97,1},{2,34}... | collective-permute-start | bytes 159752 | tf_op jit(solution)/shard_map/ppermute | solution.py:65
  231.6 6.2 %collective-permute-start.12 = (bf16[208,128]{1,0:T(8,128)(2,1)S(1)}, bf16[208,128]{1,0:T(8,128)(2,1)S(1)}, u32[]{:S(2)}, u32[]{:S(2)}) collective-permute-start(bf16[208,128]{1,0:T(8,128)(2,1)S(1)} %get-tuple-element.58), channel_id=1, source_target_pairs={{0,96},{32,0},{64,32},{96,64},{1,97},{33,1},{65,33},{97,65},{2,98}... | collective-permute-start | bytes 159752 | tf_op jit(solution)/shard_map/ppermute | solution.py:65
  241.2 3.6 %collective-permute-start.15 = (f32[1]{0:T(128)}, f32[1]{0:T(128)}, u32[]{:S(2)}, u32[]{:S(2)}) collective-permute-start(f32[1]{0:T(128)} %bitcast.21), channel_id=1, source_target_pairs={{0,32},{32,0},{64,96},{96,64},{1,33},{33,1},{65,97},{97,65},{2,34}... | collective-permute-start | bytes 20 | tf_op jit(solution)/shard_map/ppermute | solution.py:300
  246.1 5.1 %collective-permute-start.16 = (f32[1]{0:T(128)}, f32[1]{0:T(128)}, u32[]{:S(2)}, u32[]{:S(2)}) collective-permute-start(f32[1]{0:T(128)} %add.132), channel_id=1, source_target_pairs={{0,64},{32,96},{64,0},{96,32},{1,65},{33,97},{65,1},{97,33},{2,66}... | collective-permute-start | bytes 20 | tf_op jit(solution)/shard_map/ppermute | solution.py:300
  289.2 15.6 %slice-start = ((s8[6815744]{0:T(1024)(128)(4,1)}), s8[4194304]{0:T(1024)(128)(4,1)S(1)}, s32[]{:S(2)}) async-start(s8[6815744]{0:T(1024)(128)(4,1)} %bitcast.88), calls=%async_computation.10 | async-start | bytes 8388608
  290.0 5.8 %copy-start.8 = (f32[1,208]{1,0:T(1,128)S(1)}, f32[1,208]{1,0:T(1,128)}, u32[]{:S(2)}) copy-start(f32[1,208]{1,0:T(1,128)} %param.12) | copy-start | bytes 2500
  290.0 14.8 %slice-start.1 = ((s8[6815744]{0:T(1024)(128)(4,1)}), s8[2621440]{0:T(1024)(128)(4,1)S(1)}, s32[]{:S(2)}) async-start(s8[6815744]{0:T(1024)(128)(4,1)} %bitcast.88), calls=%async_computation.11 | async-start | bytes 5242880
  295.7 11.3 %copy-start.7 = (f32[208,6656]{1,0:T(8,128)}, f32[208,6656]{1,0:T(8,128)S(1)}, u32[]{:S(2)}) copy-start(f32[208,6656]{1,0:T(8,128)S(1)} %get-tuple-element.64.gradient_ref) | copy-start | bytes 16613380
  299.2 1.3 collective-permute-start.17
  300.6 16.0 %copy-start.6 = (f32[1,6656]{1,0:T(1,128)S(1)}, f32[1,6656]{1,0:T(1,128)}, u32[]{:S(2)}) copy-start(f32[1,6656]{1,0:T(1,128)} %col_ref.1) | copy-start | bytes 79876
  300.6 6.5 %collective-permute-start.19 = (f32[2,6784]{1,0:T(2,128)S(1)}, f32[2,6784]{1,0:T(2,128)S(1)}, u32[]{:S(2)}, u32[]{:S(2)}) collective-permute-start(f32[2,6784]{1,0:T(2,128)S(1)} %fusion.15), channel_id=1, source_target_pairs={{0,6},{2,0},{4,2},{6,4},{1,7},{3,1},{5,3},{7,5},{8,14},{10,8},{12,... | collective-permute-start | bytes 162824 | tf_op jit(solution)/shard_map/ppermute | solution.py:51
  302.5 6.1 %collective-permute-start.20 = (f32[2,6784]{1,0:T(2,128)S(1)}, f32[2,6784]{1,0:T(2,128)S(1)}, u32[]{:S(2)}, u32[]{:S(2)}) collective-permute-start(f32[2,6784]{1,0:T(2,128)S(1)} %fusion.15), channel_id=1, source_target_pairs={{0,2},{2,4},{4,6},{6,0},{1,3},{3,5},{5,7},{7,1},{8,10},{10,12},{12... | collective-permute-start | bytes 162824 | tf_op jit(solution)/shard_map/ppermute | solution.py:51
  302.7 5.9 %collective-permute-start.18 = (f32[2,6784]{1,0:T(2,128)S(1)}, f32[2,6784]{1,0:T(2,128)S(1)}, u32[]{:S(2)}, u32[]{:S(2)}) collective-permute-start(f32[2,6784]{1,0:T(2,128)S(1)} %fusion.15), channel_id=1, source_target_pairs={{0,4},{2,6},{4,0},{6,2},{1,5},{3,7},{5,1},{7,3},{8,12},{10,14},{12... | collective-permute-start | bytes 162824 | tf_op jit(solution)/shard_map/ppermute | solution.py:51
  308.7 4.2 %collective-permute-start.22 = (f32[2,6784]{1,0:T(2,128)S(1)}, f32[2,6784]{1,0:T(2,128)S(1)}, u32[]{:S(2)}, u32[]{:S(2)}) collective-permute-start(f32[2,6784]{1,0:T(2,128)S(1)} %add_add_fusion.1), channel_id=1, source_target_pairs={{0,24},{8,0},{16,8},{24,16},{1,25},{9,1},{17,9},{25,17},{2,26},{10... | collective-permute-start | bytes 162824 | tf_op jit(solution)/shard_map/ppermute | solution.py:51
  310.5 5.4 %collective-permute-start.23 = (f32[2,6784]{1,0:T(2,128)S(1)}, f32[2,6784]{1,0:T(2,128)S(1)}, u32[]{:S(2)}, u32[]{:S(2)}) collective-permute-start(f32[2,6784]{1,0:T(2,128)S(1)} %add_add_fusion.1), channel_id=1, source_target_pairs={{0,8},{8,16},{16,24},{24,0},{1,9},{9,17},{17,25},{25,1},{2,10},{10... | collective-permute-start | bytes 162824 | tf_op jit(solution)/shard_map/ppermute | solution.py:51
  310.8 5.6 %collective-permute-start.21 = (f32[2,6784]{1,0:T(2,128)S(1)}, f32[2,6784]{1,0:T(2,128)S(1)}, u32[]{:S(2)}, u32[]{:S(2)}) collective-permute-start(f32[2,6784]{1,0:T(2,128)S(1)} %add_add_fusion.1), channel_id=1, source_target_pairs={{0,16},{8,24},{16,0},{24,8},{1,17},{9,25},{17,1},{25,9},{2,18},{10... | collective-permute-start | bytes 162824 | tf_op jit(solution)/shard_map/ppermute | solution.py:51
Sparse Core Ops, SparseCore 0:
  42.5 53.3 all-gather.9
  150.4 35.1 all-gather.11
  187.8 36.5 all-gather.13
  238.7 50.3 all-gather.7

commit v5 on v3

--- a/solution.py
+++ b/solution.py
@@ -187,7 +187,7 @@
 
     for at in range(0, tile, 128):
         here = pl.ds(pl.multiple_of(step * tile + at, 128), 128)
-        change = gradient_ref[:, at : at + 128] * rows_ref[...] * cols_ref[:, here]
+        change = gradient_ref[:, at : at + 128].astype(jnp.float32) * rows_ref[...] * cols_ref[:, here]
         weight = weight_ref[:, at : at + 128].astype(jnp.float32)
         out_ref[:, at : at + 128] = (weight - change).astype(jnp.bfloat16)
 
@@ -206,7 +206,7 @@
             jax.ShapeDtypeStruct(col_state.shape, jnp.float32),
         ],
         scratch_shapes=[pltpu.VMEM((rows, 128), jnp.float32), pltpu.VMEM((1, width), jnp.float32)],
-        compiler_params=pltpu.CompilerParams(vmem_limit_bytes=wide_vmem),
+        compiler_params=pltpu.CompilerParams(vmem_limit_bytes=60 * 1024 * 1024),
     )(totals, row_new, col_state, gradient, weight)
 
 
@@ -274,19 +274,19 @@
         loss = loss + lax.ppermute(loss, "x", [(i, i ^ distance) for i in range(section_count)])
     loss = loss[0] / all_rows
     weight_float = local_weight.astype(jnp.float32)
-    weight_part = jnp.broadcast_to(jnp.sum(weight_float * weight_float), (128,))
+    weight_part = jnp.sum(weight_float * weight_float)
     full, loss, weight_part = lax.optimization_barrier((full, loss, weight_part))
     gradient = lax.dot_general(
         saved_all, full, (((0,), (1,)), ((), ())), preferred_element_type=jnp.float32
     )
-    squares = gradient * gradient
-    row_new = decay_rate * row_state[0] + (1.0 - decay_rate) * jnp.mean(squares + tiny_term, axis=1)
+    row_mean = jnp.mean(gradient * gradient + tiny_term, axis=1)
+    gradient = gradient.astype(jnp.bfloat16)
+    squares = jnp.square(gradient.astype(jnp.float32))
+    row_new = decay_rate * row_state[0] + (1.0 - decay_rate) * row_mean
     col_part = jnp.sum(squares + tiny_term, axis=0)
     scaled_part = jnp.sum(squares * (1.0 / row_new)[:, None], axis=0)
-    row_part = jnp.broadcast_to(jnp.sum(row_new), (128,))
-    totals = jnp.stack(
-        [jnp.concatenate([col_part, row_part]), jnp.concatenate([scaled_part, weight_part])]
-    )
+    room = [(0, 128, 0)]
+    totals = jnp.stack([lax.pad(col_part, jnp.sum(row_new), room), lax.pad(scaled_part, weight_part, room)])
     totals = totals + other_core(totals)
     totals = summed_ring(summed_ring(totals, "z"), "y")
     row_new = row_new[:, None]

time: 273 us -> 273 us (level)
  starting transfers between devices: 22.7 us -> 19.1 us
  other arithmetic: 6.92 us -> 10.5 us
    all_gather x1, waiting for transfers between devices: 35 us -> 31.2 us  [body(): full = lax.all_gather(dy, ('y', 'z', 'c'), axis=0, tiled=True)]
  transfers between devices with their start and end apart: 21 -> 21, of which waited for: 15 -> 17; matrix products, arithmetic and copies ran while one was open for 10% -> 11% of each run, Pallas kernels for 2% -> 2%
where the time goes in v5:
time: 273 us; the launch traced here: 272 us
  blocking collectives  102 us (37%)
  waiting for transfers between devices  69.8 us (26%)
  matrix products  27.1 us (10%)
  Pallas kernels  21.1 us (8%)
  starting transfers between devices  19.1 us (7%)
  between operations  17.3 us (6%)
  other arithmetic  10.5 us (4%)
  local copies, waits for them, and re-layouts  5.1 us (2%)
    all_to_all x5, blocking collectives, swapped_chips(): return lax.all_to_all(blocks, chips, 0, 0, tiled=True)  102 us
    all_gather x1, waiting for transfers between devices, body(): full = lax.all_gather(dy, ('y', 'z', 'c'), axis=0, tiled=True)  31.2 us
    ppermute x7, waiting for transfers between devices, other_core(): return lax.ppermute(x, 'c', [(0, 1), (1, 0)])  12.4 us
    dot_general x1, matrix products, body(): lax.dot_general(both, head_weight, (((0,), (1,)), ((), ())), preferred_el...  10.8 us
    pallas_call x3, Pallas kernels, layer_back(): pl.pallas_call(layer_kernel, grid_spec=pltpu.PrefetchScalarGridSpec(num_s...  9.96 us
    dot_general x1, matrix products, body(): lax.dot_general(head_weight, hidden_all, (((0,), (0,)), ((), ())), prefer...  8.54 us
    all_gather x1, waiting for transfers between devices, body(): all_weights = lax.all_gather(local_weight, 'x', axis=0)  8.52 us
    ppermute x6, starting transfers between devices, summed_ring(): lax.ppermute(x, axis, [(i, (i - step) % 4) for i in range(4)])  8.19 us
  transfers between devices with their start and end apart: 21, of which 17 were waited for; matrix products, arithmetic and copies ran while one was open for 11% of the time, Pallas kernels for 2%

profile of v5, /device:TPU:0, one launch (start us, length us, event | category | flops | bytes accessed | tf_op | source)
XLA Modules:
  0.0 272.5 jit_solution(15772328407724306235)
XLA Ops:
  7.2 0.7 all-gather.3.cloned.1.call-update
  7.9 0.8 dynamic-slice_bitcast_fusion
  8.9 22.7 %all_to_all.30.refs_0_ = bf16[16,208,128]{2,1,0:T(8,128)(2,1)S(1)} all-to-all(bf16[16,208,128]{2,1,0:T(8,128)(2,1)S(1)} %broadcast_in_dim.18), channel_id=1, replica_groups=mesh['x'=4,'y'=4,'z'=4,'c'=2] {'y','z'}, dimensions={0} | all-to-all | bytes 1703936 | tf_op jit(solution)/shard_map/all_to_all | solution.py:32
  31.6 0.8 dynamic_slice.7
  32.4 1.5 collective-permute-done.refs_1_
  33.9 0.7 shard_map.110
  34.6 8.5 %exponential_reduce_fusion = (f32[128]{0:T(128)S(1)}, f32[128]{0:T(128)S(1)}, bf16[1000,128]{1,0:T(8,128)(2,1)S(1)}) fusion(s32[1000]{0:T(1024)S(1)} %iota_add_fusion, s32[128]{0:T(128)S(1)} %dynamic_slice.7, bf16[6656,128]{1,0:T(8,128)(2,1)S(1)} %shard_map.110, bf16[6656,1000]{0,1:T(8,128)(2,1)} %param.9), kind=kOutput, calls=%fused_computation.20 | convolution fusion | flops 1704703744 | bytes 15277472 | tf_op jit(solution)/shard_map/dot_general | solution.py:241
  43.2 0.3 collective-permute-start.1
  43.4 0.2 compare_convert_fusion
  43.6 0.8 collective-permute-done.1
  44.4 0.6 broadcast_in_dim.20
  45.0 3.6 %all-to-all-start.1 = ((f32[16,2,128]{2,1,0:T(2,128)}), f32[16,2,128]{2,1,0:T(2,128)S(1)}, u32[]{:S(2)}, u32[]{:S(2)}) async-start(f32[16,2,128]{2,1,0:T(2,128)} %broadcast_in_dim.20), calls=%async_computation.1 | async-start | bytes 32768 | tf_op jit(solution)/shard_map/all_to_all | solution.py:32
  48.7 10.8 %fusion.4.product_ref = f32[256,6656]{1,0:T(8,128)} fusion(bf16[6656,1000]{0,1:T(8,128)(2,1)} %param.9, bf16[1000,128]{1,0:T(8,128)(2,1)S(1)} %compare_convert_fusion, bf16[1000,128]{1,0:T(8,128)(2,1)S(1)} %get-tuple-element.26), kind=kOutput, calls=%fused_computation.15 | convolution fusion | flops 3408896000 | bytes 20639744 | tf_op jit(solution)/shard_map/dot_general | solution.py:257
  59.5 5.1 %shard_map.111 = (f32[4,4,208,128]{3,2,1,0:T(8,128)S(1)}, bf16[4,4,208,128]{3,2,1,0:T(8,128)(2,1)S(1)}) custom-call(s32[6]{0:T(128)S(1)} %stack.79.place_ref, f32[256,6656]{1,0:T(8,128)} %fusion.4.product_ref, f32[2,128]{1,0:T(2,128)S(1)} %reduce_sum.95.sums_ref), custom_call_target="tpu_custom_call" | custom-call | tf_op jit(solution)/shard_map/pallas_call | solution.py:121
  64.6 0.2 collective-permute-start.2
  64.8 2.2 collective-permute-done.2
  67.1 0.2 add_convert_fusion
  67.2 22.1 %all_to_all.31 = bf16[16,208,128]{2,1,0:T(8,128)(2,1)S(1)} all-to-all(bf16[16,208,128]{2,1,0:T(8,128)(2,1)S(1)} %bitcast.65), channel_id=1, replica_groups=mesh['x'=4,'y'=4,'z'=4,'c'=2] {'y','z'}, dimensions={0} | all-to-all | bytes 1703936 | tf_op jit(solution)/shard_map/all_to_all | solution.py:32
  89.4 0.1 reduce_sum.96.refs_2_
  89.5 0.1 broadcast_in_dim.21
  89.6 17.5 %all_to_all.32.refs_0_ = bf16[16,208,128]{2,1,0:T(8,128)(2,1)S(1)} all-to-all(bf16[16,208,128]{2,1,0:T(8,128)(2,1)S(1)} %broadcast_in_dim.21), channel_id=1, replica_groups=mesh['x'=4,'y'=4,'z'=4,'c'=2] {'y','z'}, dimensions={0} | all-to-all | bytes 1703936 | tf_op jit(solution)/shard_map/all_to_all | solution.py:32
  107.2 2.3 collective-permute-done.3.refs_1_
  109.5 8.5 %all-gather.3.cloned.1.call-done.refs_3_ = bf16[4,208,6656]{2,1,0:T(8,128)(2,1)} async-done(((bf16[1,208,6656]{2,1,0:T(8,128)(2,1)}), bf16[4,208,6656]{2,1,0:T(8,128)(2,1)}) %all-gather.3.cloned.1.call-update) | async-done | bytes 11075600 | tf_op jit(solution)/shard_map/all_gather | solution.py:237
  118.0 3.3 %shard_map.112.refs_2_ = bf16[208,128]{1,0:T(8,128)(2,1)S(1)} custom-call(s32[6]{0:T(128)S(1)} %stack.78.place_ref, bf16[16,208,128]{2,1,0:T(8,128)(2,1)S(1)} %all_to_all.32.refs_0_, bf16[16,208,128]{2,1,0:T(8,128)(2,1)S(1)} %collective-permute-done.3.refs_1_, bf16[208,128]{1,0:T(8,128)(2,1)S(1)} %reduce_sum.96.refs_2_, ...), custom_call_target="tpu_custom_call" | custom-call | tf_op jit(solution)/shard_map/pallas_call | solution.py:152
  121.5 21.6 %all_to_all.33.refs_0_ = bf16[16,208,128]{2,1,0:T(8,128)(2,1)S(1)} all-to-all(bf16[16,208,128]{2,1,0:T(8,128)(2,1)S(1)} %broadcast_in_dim.22), channel_id=1, replica_groups=mesh['x'=4,'y'=4,'z'=4,'c'=2] {'y','z'}, dimensions={0} | all-to-all | bytes 1703936 | tf_op jit(solution)/shard_map/all_to_all | solution.py:32
  143.1 2.3 collective-permute-done.4.refs_1_
  145.4 3.3 %shard_map.113.refs_2_ = bf16[208,128]{1,0:T(8,128)(2,1)S(1)} custom-call(s32[6]{0:T(128)S(1)} %stack.83.place_ref, bf16[16,208,128]{2,1,0:T(8,128)(2,1)S(1)} %all_to_all.33.refs_0_, bf16[16,208,128]{2,1,0:T(8,128)(2,1)S(1)} %collective-permute-done.4.refs_1_, bf16[208,128]{1,0:T(8,128)(2,1)S(1)} %shard_map.112.refs_2_, ...), custom_call_target="tpu_custom_call" | custom-call | tf_op jit(solution)/shard_map/pallas_call | solution.py:152
  148.8 18.6 %all_to_all.34.refs_0_ = bf16[16,208,128]{2,1,0:T(8,128)(2,1)S(1)} all-to-all(bf16[16,208,128]{2,1,0:T(8,128)(2,1)S(1)} %broadcast_in_dim.23), channel_id=1, replica_groups=mesh['x'=4,'y'=4,'z'=4,'c'=2] {'y','z'}, dimensions={0} | all-to-all | bytes 1703936 | tf_op jit(solution)/shard_map/all_to_all | solution.py:32
  167.5 2.3 collective-permute-done.5.refs_1_
  169.8 3.3 %shard_map.114 = bf16[208,128]{1,0:T(8,128)(2,1)S(1)} custom-call(s32[6]{0:T(128)S(1)} %stack.84.place_ref, bf16[16,208,128]{2,1,0:T(8,128)(2,1)S(1)} %all_to_all.34.refs_0_, bf16[16,208,128]{2,1,0:T(8,128)(2,1)S(1)} %collective-permute-done.5.refs_1_, bf16[208,128]{1,0:T(8,128)(2,1)S(1)} %shard_map.113.refs_2_, ...), custom_call_target="tpu_custom_call" | custom-call | tf_op jit(solution)/shard_map/pallas_call | solution.py:152
  173.2 1.8 collective-permute-start.6
  175.0 1.8 collective-permute-start.7
  176.8 0.6 collective-permute-start.8
  177.4 3.4 %collective-permute-done.7 = bf16[208,128]{1,0:T(8,128)(2,1)S(1)} collective-permute-done((bf16[208,128]{1,0:T(8,128)(2,1)S(1)}, bf16[208,128]{1,0:T(8,128)(2,1)S(1)}, u32[]{:S(2)}, u32[]{:S(2)}) %collective-permute-start.7) | collective-permute-done | bytes 53280 | tf_op jit(solution)/shard_map/ppermute | solution.py:65
  180.8 1.3 collective-permute-done.8
  182.2 0.7 copy_bitcast_fusion
  182.9 3.8 %multiply_reduce_fusion.1 = f32[]{:T(128)} fusion(bf16[1,208,6656]{2,1,0:T(8,128)(2,1)} %param.11), kind=kLoop, calls=%fused_computation.4 | loop fusion | flops 4153343 | bytes 2768900 | tf_op jit(solution)/shard_map/reduce_sum | solution.py:277
  186.7 0.6 subtract_reduce_fusion
  187.3 3.6 %collective-permute-done.9 = f32[1]{0:T(128)} collective-permute-done((f32[1]{0:T(128)}, f32[1]{0:T(128)}, u32[]{:S(2)}, u32[]{:S(2)}) %collective-permute-start.9) | collective-permute-done | bytes 36 | tf_op jit(solution)/shard_map/ppermute | solution.py:274
  192.2 2.3 collective-permute-start.10
  194.5 2.8 %collective-permute-done.10 = f32[1]{0:T(128)} collective-permute-done((f32[1]{0:T(128)}, f32[1]{0:T(128)}, u32[]{:S(2)}, u32[]{:S(2)}) %collective-permute-start.10) | collective-permute-done | bytes 36 | tf_op jit(solution)/shard_map/ppermute | solution.py:274
  197.9 31.2 %all-gather.5.cloned.1.call-done = bf16[6656,512]{1,0:T(8,128)(2,1)} async-done(((bf16[208,512]{1,0:T(8,128)(2,1)}), bf16[6656,512]{1,0:T(8,128)(2,1)}) %all-gather.5.cloned.1.call-update) | async-done | bytes 6815760 | tf_op jit(solution)/shard_map/all_gather | solution.py:271
  229.1 5.4 %add_reduce_fusion = (f32[208]{0:T(256)S(1)}, bf16[6656,208]{0,1:T(8,128)(2,1)S(1)}) fusion(bf16[6656,512]{1,0:T(8,128)(2,1)} %all-gather.5.cloned.1.call-done, bf16[1,512,208]{1,2,0:T(8,128)(2,1)S(1)} %copy-done), kind=kOutput, calls=%fused_computation.1 | convolution fusion | flops 1423212288 | bytes 9798464 | tf_op jit(solution)/shard_map/dot_general | solution.py:279
  234.6 0.6 fusion.13
  235.2 0.6 add_reduce_fusion.2
  235.8 2.7 %add_reduce_fusion.1 = (f32[6656]{0:T(1024)S(1)}, f32[6656]{0:T(1024)S(1)}, bf16[208,6656]{1,0:T(8,128)(2,1)}) fusion(f32[208]{0:T(256)S(1)} %get-tuple-element.34, bf16[6656,208]{0,1:T(8,128)(2,1)S(1)} %get-tuple-element.38), kind=kLoop, calls=%fused_computation.2 | loop fusion | flops 8293376 | bytes 5591872 | tf_op jit(solution)/shard_map/reduce_sum | solution.py:286
  238.5 0.6 pad.6
  239.2 0.7 pad.7
  239.9 0.3 collective-permute-start.11
  240.3 1.0 collective-permute-done.11
  241.3 2.1 collective-permute-start.12
  243.5 1.1 collective-permute-start.13
  244.6 0.9 collective-permute-start.14
  245.5 2.3 fusion.2
  247.8 2.1 collective-permute-done.14
  250.0 2.0 collective-permute-start.15
  252.0 1.2 collective-permute-start.16
  253.2 0.9 collective-permute-start.17
  254.0 0.8 copy.27.row_new_ref
  254.8 1.0 collective-permute-done.15
  255.8 0.3 collective-permute-done.16
  256.1 2.4 collective-permute-done.17
  258.5 0.7 add_add_fusion.totals_ref
  259.2 5.3 %shard_map.115 = (bf16[208,6656]{1,0:T(8,128)(2,1)}, f32[1,6656]{1,0:T(1,128)}) custom-call(f32[2,6784]{1,0:T(2,128)} %add_add_fusion.totals_ref, f32[208,1]{1,0:T(8,128)} %copy.27.row_new_ref, f32[1,6656]{1,0:T(1,128)} %col_ref.1, bf16[208,6656]{1,0:T(8,128)(2,1)} %get-tuple-element.23.gradient_ref, bf16[208,6656]{1,0:T(8,128)(2,1)} %bitcast.64), custom_call_target="tpu_custom_call" | custom-call | tf_op jit(solution)/shard_map/pallas_call | solution.py:199
  (44 shorter events, 1.2 us)
Async XLA Ops:
  7.2 222.0 %copy-start = (bf16[1,512,208]{1,2,0:T(8,128)(2,1)S(1)}, bf16[1,512,208]{1,2,0:T(8,128)(2,1)}, u32[]{:S(2)}) copy-start(bf16[1,512,208]{1,2,0:T(8,128)(2,1)} %param.10) | copy-start | bytes 638980
  7.2 110.8 %all-gather.3.cloned.1.call-start = ((), (), s32[]{:S(2)}) async-start(), calls=%async_computation.6 | async-start | bytes 13844480 | tf_op jit(solution)/shard_map/all_gather | solution.py:237
  31.6 2.4 collective-permute-start
  43.2 1.2 collective-permute-start.1
  45.0 14.5 %all-to-all-start.1 = ((f32[16,2,128]{2,1,0:T(2,128)}), f32[16,2,128]{2,1,0:T(2,128)S(1)}, u32[]{:S(2)}, u32[]{:S(2)}) async-start(f32[16,2,128]{2,1,0:T(2,128)} %broadcast_in_dim.20), calls=%async_computation.1 | async-start | bytes 32768 | tf_op jit(solution)/shard_map/all_to_all | solution.py:32
  48.6 180.5 %all-gather.5.cloned.1.call-start = ((), (), s32[]{:S(2)}) async-start(), calls=%async_computation.7 | async-start | bytes 7028736 | tf_op jit(solution)/shard_map/all_gather | solution.py:271
  64.6 2.5 collective-permute-start.2
  107.1 2.4 collective-permute-start.3
  143.0 2.4 collective-permute-start.4
  167.4 2.4 collective-permute-start.5
  173.2 4.2 %collective-permute-start.6 = (bf16[208,128]{1,0:T(8,128)(2,1)S(1)}, bf16[208,128]{1,0:T(8,128)(2,1)S(1)}, u32[]{:S(2)}, u32[]{:S(2)}) collective-permute-start(bf16[208,128]{1,0:T(8,128)(2,1)S(1)} %get-tuple-element.32), channel_id=1, source_target_pairs={{0,96},{32,0},{64,32},{96,64},{1,97},{33,1},{65,33},{97,65},{2,98}... | collective-permute-start | bytes 159752 | tf_op jit(solution)/shard_map/ppermute | solution.py:65
  175.0 5.8 %collective-permute-start.7 = (bf16[208,128]{1,0:T(8,128)(2,1)S(1)}, bf16[208,128]{1,0:T(8,128)(2,1)S(1)}, u32[]{:S(2)}, u32[]{:S(2)}) collective-permute-start(bf16[208,128]{1,0:T(8,128)(2,1)S(1)} %get-tuple-element.31), channel_id=1, source_target_pairs={{0,64},{32,96},{64,0},{96,32},{1,65},{33,97},{65,1},{97,33},{2,66}... | collective-permute-start | bytes 159752 | tf_op jit(solution)/shard_map/ppermute | solution.py:65
  176.8 5.3 %collective-permute-start.8 = (bf16[208,128]{1,0:T(8,128)(2,1)S(1)}, bf16[208,128]{1,0:T(8,128)(2,1)S(1)}, u32[]{:S(2)}, u32[]{:S(2)}) collective-permute-start(bf16[208,128]{1,0:T(8,128)(2,1)S(1)} %get-tuple-element.30), channel_id=1, source_target_pairs={{0,32},{32,64},{64,96},{96,0},{1,33},{33,65},{65,97},{97,1},{2,34}... | collective-permute-start | bytes 159752 | tf_op jit(solution)/shard_map/ppermute | solution.py:65
  187.3 3.6 %collective-permute-start.9 = (f32[1]{0:T(128)}, f32[1]{0:T(128)}, u32[]{:S(2)}, u32[]{:S(2)}) collective-permute-start(f32[1]{0:T(128)} %bitcast.13), channel_id=1, source_target_pairs={{0,32},{32,0},{64,96},{96,64},{1,33},{33,1},{65,97},{97,65},{2,34}... | collective-permute-start | bytes 20 | tf_op jit(solution)/shard_map/ppermute | solution.py:274
  192.2 5.1 %collective-permute-start.10 = (f32[1]{0:T(128)}, f32[1]{0:T(128)}, u32[]{:S(2)}, u32[]{:S(2)}) collective-permute-start(f32[1]{0:T(128)} %add.92), channel_id=1, source_target_pairs={{0,64},{32,96},{64,0},{96,32},{1,65},{33,97},{65,1},{97,33},{2,66}... | collective-permute-start | bytes 20 | tf_op jit(solution)/shard_map/ppermute | solution.py:274
  229.1 16.4 %slice-start = ((s8[6815744]{0:T(1024)(128)(4,1)}), s8[4194304]{0:T(1024)(128)(4,1)S(1)}, s32[]{:S(2)}) async-start(s8[6815744]{0:T(1024)(128)(4,1)} %bitcast.73), calls=%async_computation.8 | async-start | bytes 8388608
  229.1 5.5 %copy-start.2 = (f32[1,208]{1,0:T(1,128)S(1)}, f32[1,208]{1,0:T(1,128)}, u32[]{:S(2)}) copy-start(f32[1,208]{1,0:T(1,128)} %param.12) | copy-start | bytes 2500
  229.1 16.4 %slice-start.1 = ((s8[6815744]{0:T(1024)(128)(4,1)}), s8[2621440]{0:T(1024)(128)(4,1)S(1)}, s32[]{:S(2)}) async-start(s8[6815744]{0:T(1024)(128)(4,1)} %bitcast.73), calls=%async_computation.9 | async-start | bytes 5242880
  234.6 10.9 %copy-start.1 = (bf16[1,208,6656]{2,1,0:T(8,128)(2,1)S(1)}, bf16[1,208,6656]{2,1,0:T(8,128)(2,1)}, u32[]{:S(2)}) copy-start(bf16[1,208,6656]{2,1,0:T(8,128)(2,1)} %param.11) | copy-start | bytes 8306692
  239.9 1.3 collective-permute-start.11
  241.3 6.5 %collective-permute-start.12 = (f32[2,6784]{1,0:T(2,128)S(1)}, f32[2,6784]{1,0:T(2,128)S(1)}, u32[]{:S(2)}, u32[]{:S(2)}) collective-permute-start(f32[2,6784]{1,0:T(2,128)S(1)} %fusion.14), channel_id=1, source_target_pairs={{0,4},{2,6},{4,0},{6,2},{1,5},{3,7},{5,1},{7,3},{8,12},{10,14},{12... | collective-permute-start | bytes 162824 | tf_op jit(solution)/shard_map/ppermute | solution.py:51
  243.5 4.4 %collective-permute-start.13 = (f32[2,6784]{1,0:T(2,128)S(1)}, f32[2,6784]{1,0:T(2,128)S(1)}, u32[]{:S(2)}, u32[]{:S(2)}) collective-permute-start(f32[2,6784]{1,0:T(2,128)S(1)} %fusion.14), channel_id=1, source_target_pairs={{0,6},{2,0},{4,2},{6,4},{1,7},{3,1},{5,3},{7,5},{8,14},{10,8},{12,... | collective-permute-start | bytes 162824 | tf_op jit(solution)/shard_map/ppermute | solution.py:51
  244.6 5.4 %collective-permute-start.14 = (f32[2,6784]{1,0:T(2,128)S(1)}, f32[2,6784]{1,0:T(2,128)S(1)}, u32[]{:S(2)}, u32[]{:S(2)}) collective-permute-start(f32[2,6784]{1,0:T(2,128)S(1)} %fusion.14), channel_id=1, source_target_pairs={{0,2},{2,4},{4,6},{6,0},{1,3},{3,5},{5,7},{7,1},{8,10},{10,12},{12... | collective-permute-start | bytes 162824 | tf_op jit(solution)/shard_map/ppermute | solution.py:51
  250.0 5.8 %collective-permute-start.15 = (f32[2,6784]{1,0:T(2,128)S(1)}, f32[2,6784]{1,0:T(2,128)S(1)}, u32[]{:S(2)}, u32[]{:S(2)}) collective-permute-start(f32[2,6784]{1,0:T(2,128)S(1)} %add_add_fusion.1), channel_id=1, source_target_pairs={{0,16},{8,24},{16,0},{24,8},{1,17},{9,25},{17,1},{25,9},{2,18},{10... | collective-permute-start | bytes 162824 | tf_op jit(solution)/shard_map/ppermute | solution.py:51
  252.0 4.1 %collective-permute-start.16 = (f32[2,6784]{1,0:T(2,128)S(1)}, f32[2,6784]{1,0:T(2,128)S(1)}, u32[]{:S(2)}, u32[]{:S(2)}) collective-permute-start(f32[2,6784]{1,0:T(2,128)S(1)} %add_add_fusion.1), channel_id=1, source_target_pairs={{0,24},{8,0},{16,8},{24,16},{1,25},{9,1},{17,9},{25,17},{2,26},{10... | collective-permute-start | bytes 162824 | tf_op jit(solution)/shard_map/ppermute | solution.py:51
  253.2 5.4 %collective-permute-start.17 = (f32[2,6784]{1,0:T(2,128)S(1)}, f32[2,6784]{1,0:T(2,128)S(1)}, u32[]{:S(2)}, u32[]{:S(2)}) collective-permute-start(f32[2,6784]{1,0:T(2,128)S(1)} %add_add_fusion.1), channel_id=1, source_target_pairs={{0,8},{8,16},{16,24},{24,0},{1,9},{9,17},{17,25},{25,1},{2,10},{10... | collective-permute-start | bytes 162824 | tf_op jit(solution)/shard_map/ppermute | solution.py:51
Sparse Core Ops, SparseCore 0:
  9.7 108.2 all-gather.2
  183.0 46.0 all-gather.4

commit v6 on v3

--- a/solution.py
+++ b/solution.py
@@ -139,10 +139,21 @@
 
 
 def layer_kernel(place_ref, *refs):
-    pieces, (carried_ref, weight_ref, out_ref, full_ref) = refs[:2], refs[2:]
-    place(pieces, place_ref, full_ref)
-    backward = jnp.dot(weight_ref[0], full_ref[...], preferred_element_type=jnp.float32)
-    out_ref[...] = (carried_ref[...].astype(jnp.float32) + backward).astype(jnp.bfloat16)
+    pieces, (carried_ref, weight_ref, out_ref, full_ref, total_ref) = refs[:2], refs[2:]
+    step = pl.program_id(0)
+    depth = weight_ref.shape[2]
+
+    @pl.when(step == 0)
+    def _():
+        place(pieces, place_ref, full_ref)
+        total_ref[...] = carried_ref[...].astype(jnp.float32)
+
+    rows = full_ref[pl.ds(pl.multiple_of(step * depth, depth), depth), :]
+    total_ref[...] += jnp.dot(weight_ref[0], rows, preferred_element_type=jnp.float32)
+
+    @pl.when(step == pl.num_programs(0) - 1)
+    def _():
+        out_ref[...] = total_ref[...].astype(jnp.bfloat16)
 
 
 def layer_back(where, carried, all_weights):
@@ -153,14 +164,17 @@
         layer_kernel,
         grid_spec=pltpu.PrefetchScalarGridSpec(
             num_scalar_prefetch=1,
-            grid=(1,),
+            grid=(2,),
             in_specs=[whole(p.shape) for p in pieces]
             + [
                 whole(carried.shape),
-                pl.BlockSpec((1, rows_local, model_width), lambda i, s: (s[5], 0, 0)),
+                pl.BlockSpec((1, rows_local, model_width // 2), lambda i, s: (s[5], 0, i)),
             ],
             out_specs=whole(carried.shape),
-            scratch_shapes=[pltpu.VMEM((model_width, carried.shape[1]), jnp.bfloat16)],
+            scratch_shapes=[
+                pltpu.VMEM((model_width, carried.shape[1]), jnp.bfloat16),
+                pltpu.VMEM(carried.shape, jnp.float32),
+            ],
         ),
         out_shape=jax.ShapeDtypeStruct(carried.shape, jnp.bfloat16),
         compiler_params=pltpu.CompilerParams(vmem_limit_bytes=wide_vmem),
@@ -274,7 +288,7 @@
         loss = loss + lax.ppermute(loss, "x", [(i, i ^ distance) for i in range(section_count)])
     loss = loss[0] / all_rows
     weight_float = local_weight.astype(jnp.float32)
-    weight_part = jnp.broadcast_to(jnp.sum(weight_float * weight_float), (128,))
+    weight_part = jnp.sum(weight_float * weight_float)
     full, loss, weight_part = lax.optimization_barrier((full, loss, weight_part))
     gradient = lax.dot_general(
         saved_all, full, (((0,), (1,)), ((), ())), preferred_element_type=jnp.float32
@@ -283,10 +297,8 @@
     row_new = decay_rate * row_state[0] + (1.0 - decay_rate) * jnp.mean(squares + tiny_term, axis=1)
     col_part = jnp.sum(squares + tiny_term, axis=0)
     scaled_part = jnp.sum(squares * (1.0 / row_new)[:, None], axis=0)
-    row_part = jnp.broadcast_to(jnp.sum(row_new), (128,))
-    totals = jnp.stack(
-        [jnp.concatenate([col_part, row_part]), jnp.concatenate([scaled_part, weight_part])]
-    )
+    room = [(0, 128, 0)]
+    totals = jnp.stack([lax.pad(col_part, jnp.sum(row_new), room), lax.pad(scaled_part, weight_part, room)])
     totals = totals + other_core(totals)
     totals = summed_ring(summed_ring(totals, "z"), "y")
     row_new = row_new[:, None]

time: 273 us -> 272 us (level)
  no operation moved by 1% of the time
where the time goes in v6:
time: 272 us; the launch traced here: 271 us
  blocking collectives  103 us (38%)
  waiting for transfers between devices  69.1 us (25%)
  matrix products  27.1 us (10%)
  starting transfers between devices  22.9 us (8%)
  Pallas kernels  20.9 us (8%)
  between operations  17.4 us (6%)
  other arithmetic  6.91 us (3%)
  local copies, waits for them, and re-layouts  4.46 us (2%)
    all_to_all x5, blocking collectives, swapped_chips(): return lax.all_to_all(blocks, chips, 0, 0, tiled=True)  103 us
    all_gather x1, waiting for transfers between devices, body(): full = lax.all_gather(dy, ('y', 'z', 'c'), axis=0, tiled=True)  35 us
    ppermute x7, waiting for transfers between devices, other_core(): return lax.ppermute(x, 'c', [(0, 1), (1, 0)])  12.8 us
    dot_general x1, matrix products, body(): lax.dot_general(both, head_weight, (((0,), (1,)), ((), ())), preferred_el...  10.8 us
    pallas_call x3, Pallas kernels, layer_back(): pl.pallas_call(layer_kernel, grid_spec=pltpu.PrefetchScalarGridSpec(num_s...  9.81 us
    dot_general x1, matrix products, body(): lax.dot_general(head_weight, hidden_all, (((0,), (0,)), ((), ())), prefer...  8.54 us
    all_gather x1, waiting for transfers between devices, body(): all_weights = lax.all_gather(local_weight, 'x', axis=0)  8.49 us
    ppermute x6, starting transfers between devices, summed_ring(): lax.ppermute(x, axis, [(i, (i - step) % 4) for i in range(4)])  8.22 us
  transfers between devices with their start and end apart: 21, of which 15 were waited for; matrix products, arithmetic and copies ran while one was open for 10% of the time, Pallas kernels for 2%

profile of v6, /device:TPU:0, one launch (start us, length us, event | category | flops | bytes accessed | tf_op | source)
XLA Modules:
  0.0 271.3 jit_solution(2807185367068608617)
XLA Ops:
  7.2 0.7 all-gather.3.cloned.1.call-update
  7.9 0.8 dynamic-slice_bitcast_fusion
  8.7 0.1 broadcast_in_dim.18
  8.9 22.7 %all_to_all.30.refs_0_ = bf16[16,208,128]{2,1,0:T(8,128)(2,1)S(1)} all-to-all(bf16[16,208,128]{2,1,0:T(8,128)(2,1)S(1)} %broadcast_in_dim.18), channel_id=1, replica_groups=mesh['x'=4,'y'=4,'z'=4,'c'=2] {'y','z'}, dimensions={0} | all-to-all | bytes 1703936 | tf_op jit(solution)/shard_map/all_to_all | solution.py:32
  31.6 0.8 dynamic_slice.7
  32.4 1.5 collective-permute-done.refs_1_
  33.9 0.7 shard_map.110
  34.6 8.5 %exponential_reduce_fusion = (f32[128]{0:T(128)S(1)}, f32[128]{0:T(128)S(1)}, bf16[1000,128]{1,0:T(8,128)(2,1)S(1)}) fusion(s32[1000]{0:T(1024)S(1)} %iota_add_fusion, s32[128]{0:T(128)S(1)} %dynamic_slice.7, bf16[6656,128]{1,0:T(8,128)(2,1)S(1)} %shard_map.110, bf16[6656,1000]{0,1:T(8,128)(2,1)} %param.9), kind=kOutput, calls=%fused_computation.19 | convolution fusion | flops 1704703744 | bytes 15277472 | tf_op jit(solution)/shard_map/dot_general | solution.py:255
  43.2 0.3 collective-permute-start.1
  43.4 0.2 compare_convert_fusion
  43.6 0.8 collective-permute-done.1
  44.4 0.6 broadcast_in_dim.20
  45.0 3.6 %all-to-all-start.1 = ((f32[16,2,128]{2,1,0:T(2,128)}), f32[16,2,128]{2,1,0:T(2,128)S(1)}, u32[]{:S(2)}, u32[]{:S(2)}) async-start(f32[16,2,128]{2,1,0:T(2,128)} %broadcast_in_dim.20), calls=%async_computation.1 | async-start | bytes 32768 | tf_op jit(solution)/shard_map/all_to_all | solution.py:32
  48.7 10.8 %fusion.4.product_ref = f32[256,6656]{1,0:T(8,128)} fusion(bf16[6656,1000]{0,1:T(8,128)(2,1)} %param.9, bf16[1000,128]{1,0:T(8,128)(2,1)S(1)} %compare_convert_fusion, bf16[1000,128]{1,0:T(8,128)(2,1)S(1)} %get-tuple-element.25), kind=kOutput, calls=%fused_computation.14 | convolution fusion | flops 3408896000 | bytes 20639744 | tf_op jit(solution)/shard_map/dot_general | solution.py:271
  59.5 5.1 %shard_map.111 = (f32[4,4,208,128]{3,2,1,0:T(8,128)S(1)}, bf16[4,4,208,128]{3,2,1,0:T(8,128)(2,1)S(1)}) custom-call(s32[6]{0:T(128)S(1)} %stack.79.place_ref, f32[256,6656]{1,0:T(8,128)} %fusion.4.product_ref, f32[2,128]{1,0:T(2,128)S(1)} %reduce_sum.95.sums_ref), custom_call_target="tpu_custom_call" | custom-call | tf_op jit(solution)/shard_map/pallas_call | solution.py:121
  64.6 0.2 collective-permute-start.2
  64.8 2.2 collective-permute-done.2
  67.1 0.2 add_convert_fusion
  67.3 22.1 %all_to_all.31 = bf16[16,208,128]{2,1,0:T(8,128)(2,1)S(1)} all-to-all(bf16[16,208,128]{2,1,0:T(8,128)(2,1)S(1)} %bitcast.64), channel_id=1, replica_groups=mesh['x'=4,'y'=4,'z'=4,'c'=2] {'y','z'}, dimensions={0} | all-to-all | bytes 1703936 | tf_op jit(solution)/shard_map/all_to_all | solution.py:32
  89.4 0.1 reduce_sum.96.refs_2_
  89.5 0.1 broadcast_in_dim.21
  89.6 17.5 %all_to_all.32.refs_0_ = bf16[16,208,128]{2,1,0:T(8,128)(2,1)S(1)} all-to-all(bf16[16,208,128]{2,1,0:T(8,128)(2,1)S(1)} %broadcast_in_dim.21), channel_id=1, replica_groups=mesh['x'=4,'y'=4,'z'=4,'c'=2] {'y','z'}, dimensions={0} | all-to-all | bytes 1703936 | tf_op jit(solution)/shard_map/all_to_all | solution.py:32
  107.2 2.3 collective-permute-done.3.refs_1_
  109.5 8.5 %all-gather.3.cloned.1.call-done.refs_3_ = bf16[4,208,6656]{2,1,0:T(8,128)(2,1)} async-done(((bf16[1,208,6656]{2,1,0:T(8,128)(2,1)}), bf16[4,208,6656]{2,1,0:T(8,128)(2,1)}) %all-gather.3.cloned.1.call-update) | async-done | bytes 11075600 | tf_op jit(solution)/shard_map/all_gather | solution.py:251
  118.0 3.1 %shard_map.112.refs_2_ = bf16[208,128]{1,0:T(8,128)(2,1)S(1)} custom-call(s32[6]{0:T(128)S(1)} %stack.78.place_ref, bf16[16,208,128]{2,1,0:T(8,128)(2,1)S(1)} %all_to_all.32.refs_0_, bf16[16,208,128]{2,1,0:T(8,128)(2,1)S(1)} %collective-permute-done.3.refs_1_, bf16[208,128]{1,0:T(8,128)(2,1)S(1)} %reduce_sum.96.refs_2_, ...), custom_call_target="tpu_custom_call" | custom-call | tf_op jit(solution)/shard_map/pallas_call | solution.py:163
  121.1 0.1 broadcast_in_dim.22
  121.2 21.6 %all_to_all.33.refs_0_ = bf16[16,208,128]{2,1,0:T(8,128)(2,1)S(1)} all-to-all(bf16[16,208,128]{2,1,0:T(8,128)(2,1)S(1)} %broadcast_in_dim.22), channel_id=1, replica_groups=mesh['x'=4,'y'=4,'z'=4,'c'=2] {'y','z'}, dimensions={0} | all-to-all | bytes 1703936 | tf_op jit(solution)/shard_map/all_to_all | solution.py:32
  142.9 2.3 collective-permute-done.4.refs_1_
  145.2 3.1 %shard_map.113.refs_2_ = bf16[208,128]{1,0:T(8,128)(2,1)S(1)} custom-call(s32[6]{0:T(128)S(1)} %stack.83.place_ref, bf16[16,208,128]{2,1,0:T(8,128)(2,1)S(1)} %all_to_all.33.refs_0_, bf16[16,208,128]{2,1,0:T(8,128)(2,1)S(1)} %collective-permute-done.4.refs_1_, bf16[208,128]{1,0:T(8,128)(2,1)S(1)} %shard_map.112.refs_2_, ...), custom_call_target="tpu_custom_call" | custom-call | tf_op jit(solution)/shard_map/pallas_call | solution.py:163
  148.3 0.1 broadcast_in_dim.23
  148.4 18.7 %all_to_all.34.refs_0_ = bf16[16,208,128]{2,1,0:T(8,128)(2,1)} all-to-all(bf16[16,208,128]{2,1,0:T(8,128)(2,1)S(1)} %broadcast_in_dim.23), channel_id=1, replica_groups=mesh['x'=4,'y'=4,'z'=4,'c'=2] {'y','z'}, dimensions={0} | all-to-all | bytes 1703936 | tf_op jit(solution)/shard_map/all_to_all | solution.py:32
  167.2 2.6 collective-permute-done.5.refs_1_
  169.8 3.6 %shard_map.114 = bf16[208,128]{1,0:T(8,128)(2,1)S(1)} custom-call(s32[6]{0:T(128)S(1)} %stack.84.place_ref, bf16[16,208,128]{2,1,0:T(8,128)(2,1)} %all_to_all.34.refs_0_, bf16[16,208,128]{2,1,0:T(8,128)(2,1)} %collective-permute-done.5.refs_1_, bf16[208,128]{1,0:T(8,128)(2,1)S(1)} %shard_map.113.refs_2_, ...), custom_call_target="tpu_custom_call" | custom-call | tf_op jit(solution)/shard_map/pallas_call | solution.py:163
  173.5 2.9 %collective-permute-start.7 = (bf16[208,128]{1,0:T(8,128)(2,1)S(1)}, bf16[208,128]{1,0:T(8,128)(2,1)S(1)}, u32[]{:S(2)}, u32[]{:S(2)}) collective-permute-start(bf16[208,128]{1,0:T(8,128)(2,1)S(1)} %get-tuple-element.30), channel_id=1, source_target_pairs={{0,64},{32,96},{64,0},{96,32},{1,65},{33,97},{65,1},{97,33},{2,66}... | collective-permute-start | bytes 159752 | tf_op jit(solution)/shard_map/ppermute | solution.py:65
  176.4 3.2 %collective-permute-start.6 = (bf16[208,128]{1,0:T(8,128)(2,1)S(1)}, bf16[208,128]{1,0:T(8,128)(2,1)S(1)}, u32[]{:S(2)}, u32[]{:S(2)}) collective-permute-start(bf16[208,128]{1,0:T(8,128)(2,1)S(1)} %get-tuple-element.31), channel_id=1, source_target_pairs={{0,96},{32,0},{64,32},{96,64},{1,97},{33,1},{65,33},{97,65},{2,98}... | collective-permute-start | bytes 159752 | tf_op jit(solution)/shard_map/ppermute | solution.py:65
  179.7 2.1 collective-permute-done.8
  181.8 0.7 copy_bitcast_fusion
  182.6 2.0 multiply_reduce_fusion.1
  184.6 0.6 subtract_reduce_fusion
  185.2 3.8 %collective-permute-done.9 = f32[1]{0:T(128)} collective-permute-done((f32[1]{0:T(128)}, f32[1]{0:T(128)}, u32[]{:S(2)}, u32[]{:S(2)}) %collective-permute-start.9) | collective-permute-done | bytes 36 | tf_op jit(solution)/shard_map/ppermute | solution.py:288
  190.3 4.0 %collective-permute-start.10 = (f32[1]{0:T(128)}, f32[1]{0:T(128)}, u32[]{:S(2)}, u32[]{:S(2)}) collective-permute-start(f32[1]{0:T(128)} %add.89), channel_id=1, source_target_pairs={{0,64},{32,96},{64,0},{96,32},{1,65},{33,97},{65,1},{97,33},{2,66}... | collective-permute-start | bytes 20 | tf_op jit(solution)/shard_map/ppermute | solution.py:288
  194.3 1.2 collective-permute-done.10
  196.1 35.0 %all-gather.5.cloned.1.call-done = bf16[6656,512]{1,0:T(8,128)(2,1)} async-done(((bf16[208,512]{1,0:T(8,128)(2,1)}), bf16[6656,512]{1,0:T(8,128)(2,1)}) %all-gather.5.cloned.1.call-update) | async-done | bytes 6815760 | tf_op jit(solution)/shard_map/all_gather | solution.py:285
  231.1 5.4 %add_reduce_fusion = (f32[208]{0:T(256)S(1)}, f32[208,6656]{1,0:T(8,128)S(1)}) fusion(bf16[6656,512]{1,0:T(8,128)(2,1)} %all-gather.5.cloned.1.call-done, bf16[1,512,208]{1,2,0:T(8,128)(2,1)S(1)} %copy-done), kind=kOutput, calls=%fused_computation.3 | convolution fusion | flops 1421827840 | bytes 12567360 | tf_op jit(solution)/shard_map/dot_general | solution.py:293
  236.6 0.6 fusion.12
  237.2 1.0 add_reduce_fusion.2
  238.2 1.0 add_reduce_fusion.1
  239.2 0.7 pad.7
  239.9 0.7 pad.6
  240.7 0.3 collective-permute-start.11
  241.0 1.0 collective-permute-done.11
  242.1 1.9 collective-permute-start.13
  244.0 0.2 collective-permute-start.14
  244.2 2.1 collective-permute-start.12
  246.2 2.3 fusion.2
  248.5 1.6 collective-permute-done.14
  250.1 0.1 add_add_fusion.1
  250.2 1.8 collective-permute-start.16
  252.0 0.3 collective-permute-start.17
  252.3 2.0 collective-permute-start.15
  254.3 0.1 copy.27.row_new_ref
  254.4 2.9 %collective-permute-done.17 = f32[2,6784]{1,0:T(2,128)S(1)} collective-permute-done((f32[2,6784]{1,0:T(2,128)S(1)}, f32[2,6784]{1,0:T(2,128)S(1)}, u32[]{:S(2)}, u32[]{:S(2)}) %collective-permute-start.17) | collective-permute-done | bytes 54304 | tf_op jit(solution)/shard_map/ppermute | solution.py:51
  257.3 0.6 collective-permute-done.15
  258.0 5.3 %shard_map.115 = (bf16[208,6656]{1,0:T(8,128)(2,1)}, f32[1,6656]{1,0:T(1,128)}) custom-call(f32[2,6784]{1,0:T(2,128)S(1)} %add_add_fusion.totals_ref, f32[208,1]{1,0:T(8,128)S(1)} %copy.27.row_new_ref, f32[1,6656]{1,0:T(1,128)S(1)} %copy-done.2, f32[208,6656]{1,0:T(8,128)} %copy-done.3, bf16[208,6656]{1,0:T(8,128)(2,1)S(1)} %bitcast.63), custom_call_target="tpu_custom_call" | custom-call | tf_op jit(solution)/shard_map/pallas_call | solution.py:213
  (48 shorter events, 0.9 us)
Async XLA Ops:
  7.2 224.0 %copy-start = (bf16[1,512,208]{1,2,0:T(8,128)(2,1)S(1)}, bf16[1,512,208]{1,2,0:T(8,128)(2,1)}, u32[]{:S(2)}) copy-start(bf16[1,512,208]{1,2,0:T(8,128)(2,1)} %param.10) | copy-start | bytes 638980
  7.2 110.8 %all-gather.3.cloned.1.call-start = ((), (), s32[]{:S(2)}) async-start(), calls=%async_computation.6 | async-start | bytes 13844480 | tf_op jit(solution)/shard_map/all_gather | solution.py:251
  31.6 2.4 collective-permute-start
  43.2 1.2 collective-permute-start.1
  45.0 14.4 %all-to-all-start.1 = ((f32[16,2,128]{2,1,0:T(2,128)}), f32[16,2,128]{2,1,0:T(2,128)S(1)}, u32[]{:S(2)}, u32[]{:S(2)}) async-start(f32[16,2,128]{2,1,0:T(2,128)} %broadcast_in_dim.20), calls=%async_computation.1 | async-start | bytes 32768 | tf_op jit(solution)/shard_map/all_to_all | solution.py:32
  48.6 182.5 %all-gather.5.cloned.1.call-start = ((), (), s32[]{:S(2)}) async-start(), calls=%async_computation.7 | async-start | bytes 7028736 | tf_op jit(solution)/shard_map/all_gather | solution.py:285
  64.6 2.5 collective-permute-start.2
  107.1 2.4 collective-permute-start.3
  142.8 2.4 collective-permute-start.4
  167.1 2.7 %collective-permute-start.5 = (bf16[16,208,128]{2,1,0:T(8,128)(2,1)}, bf16[16,208,128]{2,1,0:T(8,128)(2,1)}, u32[]{:S(2)}, u32[]{:S(2)}) collective-permute-start(bf16[16,208,128]{2,1,0:T(8,128)(2,1)} %all_to_all.34.refs_0_), channel_id=1, source_target_pairs={{0,1},{1,0},{2,3},{3,2},{4,5},{5,4},{6,7},{7,6},{8,9},{9,8},{10,11... | collective-permute-start | bytes 2555912 | tf_op jit(solution)/shard_map/ppermute | solution.py:28
  167.2 15.4 %copy-start.1 = (bf16[1,208,6656]{2,1,0:T(8,128)(2,1)S(1)}, bf16[1,208,6656]{2,1,0:T(8,128)(2,1)}, u32[]{:S(2)}) copy-start(bf16[1,208,6656]{2,1,0:T(8,128)(2,1)} %param.11) | copy-start | bytes 8306692
  173.5 6.2 %collective-permute-start.7 = (bf16[208,128]{1,0:T(8,128)(2,1)S(1)}, bf16[208,128]{1,0:T(8,128)(2,1)S(1)}, u32[]{:S(2)}, u32[]{:S(2)}) collective-permute-start(bf16[208,128]{1,0:T(8,128)(2,1)S(1)} %get-tuple-element.30), channel_id=1, source_target_pairs={{0,64},{32,96},{64,0},{96,32},{1,65},{33,97},{65,1},{97,33},{2,66}... | collective-permute-start | bytes 159752 | tf_op jit(solution)/shard_map/ppermute | solution.py:65
  176.4 5.3 %collective-permute-start.8 = (bf16[208,128]{1,0:T(8,128)(2,1)S(1)}, bf16[208,128]{1,0:T(8,128)(2,1)S(1)}, u32[]{:S(2)}, u32[]{:S(2)}) collective-permute-start(bf16[208,128]{1,0:T(8,128)(2,1)S(1)} %get-tuple-element.29), channel_id=1, source_target_pairs={{0,32},{32,64},{64,96},{96,0},{1,33},{33,65},{65,97},{97,1},{2,34}... | collective-permute-start | bytes 159752 | tf_op jit(solution)/shard_map/ppermute | solution.py:65
  176.4 5.3 %collective-permute-start.6 = (bf16[208,128]{1,0:T(8,128)(2,1)S(1)}, bf16[208,128]{1,0:T(8,128)(2,1)S(1)}, u32[]{:S(2)}, u32[]{:S(2)}) collective-permute-start(bf16[208,128]{1,0:T(8,128)(2,1)S(1)} %get-tuple-element.31), channel_id=1, source_target_pairs={{0,96},{32,0},{64,32},{96,64},{1,97},{33,1},{65,33},{97,65},{2,98}... | collective-permute-start | bytes 159752 | tf_op jit(solution)/shard_map/ppermute | solution.py:65
  185.2 3.8 %collective-permute-start.9 = (f32[1]{0:T(128)}, f32[1]{0:T(128)}, u32[]{:S(2)}, u32[]{:S(2)}) collective-permute-start(f32[1]{0:T(128)} %bitcast.13), channel_id=1, source_target_pairs={{0,32},{32,0},{64,96},{96,64},{1,33},{33,1},{65,97},{97,65},{2,34}... | collective-permute-start | bytes 20 | tf_op jit(solution)/shard_map/ppermute | solution.py:288
  190.3 5.2 %collective-permute-start.10 = (f32[1]{0:T(128)}, f32[1]{0:T(128)}, u32[]{:S(2)}, u32[]{:S(2)}) collective-permute-start(f32[1]{0:T(128)} %add.89), channel_id=1, source_target_pairs={{0,64},{32,96},{64,0},{96,32},{1,65},{33,97},{65,1},{97,33},{2,66}... | collective-permute-start | bytes 20 | tf_op jit(solution)/shard_map/ppermute | solution.py:288
  231.1 15.1 %slice-start = ((s8[6815744]{0:T(1024)(128)(4,1)}), s8[4194304]{0:T(1024)(128)(4,1)S(1)}, s32[]{:S(2)}) async-start(s8[6815744]{0:T(1024)(128)(4,1)} %bitcast.72), calls=%async_computation.8 | async-start | bytes 8388608
  231.1 5.5 %copy-start.4 = (f32[1,208]{1,0:T(1,128)S(1)}, f32[1,208]{1,0:T(1,128)}, u32[]{:S(2)}) copy-start(f32[1,208]{1,0:T(1,128)} %param.12) | copy-start | bytes 2500
  231.1 15.1 %slice-start.1 = ((s8[6815744]{0:T(1024)(128)(4,1)}), s8[2621440]{0:T(1024)(128)(4,1)S(1)}, s32[]{:S(2)}) async-start(s8[6815744]{0:T(1024)(128)(4,1)} %bitcast.72), calls=%async_computation.9 | async-start | bytes 5242880
  236.6 12.0 %copy-start.3 = (f32[208,6656]{1,0:T(8,128)}, f32[208,6656]{1,0:T(8,128)S(1)}, u32[]{:S(2)}) copy-start(f32[208,6656]{1,0:T(8,128)S(1)} %get-tuple-element.37.gradient_ref) | copy-start | bytes 16613380
  240.7 1.3 collective-permute-start.11
  242.1 16.0 %copy-start.2 = (f32[1,6656]{1,0:T(1,128)S(1)}, f32[1,6656]{1,0:T(1,128)}, u32[]{:S(2)}) copy-start(f32[1,6656]{1,0:T(1,128)} %col_ref.1) | copy-start | bytes 79876
  242.1 6.5 %collective-permute-start.13 = (f32[2,6784]{1,0:T(2,128)S(1)}, f32[2,6784]{1,0:T(2,128)S(1)}, u32[]{:S(2)}, u32[]{:S(2)}) collective-permute-start(f32[2,6784]{1,0:T(2,128)S(1)} %fusion.13), channel_id=1, source_target_pairs={{0,6},{2,0},{4,2},{6,4},{1,7},{3,1},{5,3},{7,5},{8,14},{10,8},{12,... | collective-permute-start | bytes 162824 | tf_op jit(solution)/shard_map/ppermute | solution.py:51
  244.0 6.1 %collective-permute-start.14 = (f32[2,6784]{1,0:T(2,128)S(1)}, f32[2,6784]{1,0:T(2,128)S(1)}, u32[]{:S(2)}, u32[]{:S(2)}) collective-permute-start(f32[2,6784]{1,0:T(2,128)S(1)} %fusion.13), channel_id=1, source_target_pairs={{0,2},{2,4},{4,6},{6,0},{1,3},{3,5},{5,7},{7,1},{8,10},{10,12},{12... | collective-permute-start | bytes 162824 | tf_op jit(solution)/shard_map/ppermute | solution.py:51
  244.2 5.9 %collective-permute-start.12 = (f32[2,6784]{1,0:T(2,128)S(1)}, f32[2,6784]{1,0:T(2,128)S(1)}, u32[]{:S(2)}, u32[]{:S(2)}) collective-permute-start(f32[2,6784]{1,0:T(2,128)S(1)} %fusion.13), channel_id=1, source_target_pairs={{0,4},{2,6},{4,0},{6,2},{1,5},{3,7},{5,1},{7,3},{8,12},{10,14},{12... | collective-permute-start | bytes 162824 | tf_op jit(solution)/shard_map/ppermute | solution.py:51
  250.2 4.2 %collective-permute-start.16 = (f32[2,6784]{1,0:T(2,128)S(1)}, f32[2,6784]{1,0:T(2,128)S(1)}, u32[]{:S(2)}, u32[]{:S(2)}) collective-permute-start(f32[2,6784]{1,0:T(2,128)S(1)} %add_add_fusion.1), channel_id=1, source_target_pairs={{0,24},{8,0},{16,8},{24,16},{1,25},{9,1},{17,9},{25,17},{2,26},{10... | collective-permute-start | bytes 162824 | tf_op jit(solution)/shard_map/ppermute | solution.py:51
  252.0 5.4 %collective-permute-start.17 = (f32[2,6784]{1,0:T(2,128)S(1)}, f32[2,6784]{1,0:T(2,128)S(1)}, u32[]{:S(2)}, u32[]{:S(2)}) collective-permute-start(f32[2,6784]{1,0:T(2,128)S(1)} %add_add_fusion.1), channel_id=1, source_target_pairs={{0,8},{8,16},{16,24},{24,0},{1,9},{9,17},{17,25},{25,1},{2,10},{10... | collective-permute-start | bytes 162824 | tf_op jit(solution)/shard_map/ppermute | solution.py:51
  252.3 5.6 %collective-permute-start.15 = (f32[2,6784]{1,0:T(2,128)S(1)}, f32[2,6784]{1,0:T(2,128)S(1)}, u32[]{:S(2)}, u32[]{:S(2)}) collective-permute-start(f32[2,6784]{1,0:T(2,128)S(1)} %add_add_fusion.1), channel_id=1, source_target_pairs={{0,16},{8,24},{16,0},{24,8},{1,17},{9,25},{17,1},{25,9},{2,18},{10... | collective-permute-start | bytes 162824 | tf_op jit(solution)/shard_map/ppermute | solution.py:51
Sparse Core Ops, SparseCore 0:
  9.7 108.2 all-gather.2
  182.7 48.3 all-gather.4

commit v7 on v6

--- a/solution.py
+++ b/solution.py
@@ -181,7 +181,7 @@
     )(where, *pieces, carried, all_weights)
 
 
-def weights_kernel(totals_ref, row_new_ref, col_ref, gradient_ref, weight_ref, out_ref, col_new_ref, rows_ref, cols_ref):
+def weights_kernel(totals_ref, sums_ref, row_new_ref, col_ref, gradient_ref, weight_ref, out_ref, col_new_ref, rows_ref, cols_ref):
     step = pl.program_id(0)
     tile = weight_ref.shape[1]
     width = col_ref.shape[1]
@@ -192,8 +192,9 @@
         col_new = decay_rate * col_ref[...] + (1.0 - decay_rate) * (totals_ref[0:1, :width] / width)
         col_new_ref[...] = col_new
         cols_ref[...] = 1.0 / jnp.sqrt(col_new)
-        row_total = totals_ref[0:1, width : width + 1]
-        weight_total = totals_ref[1:2, width : width + 1]
+        squares_total = jnp.sum(totals_ref[0:1, :], axis=1, keepdims=True)
+        row_total = decay_rate * sums_ref[3:4, 0:1] + (1.0 - decay_rate) * (squares_total / width)
+        weight_total = sums_ref[2:3, 0:1]
         update_total = row_total * jnp.sum(totals_ref[1:2, :width] / col_new, axis=1, keepdims=True)
         factor = learn_rate * jnp.sqrt(weight_total / entries)
         factor = factor / jnp.maximum(1.0, jnp.sqrt(update_total / entries))
@@ -206,14 +207,14 @@
         out_ref[:, at : at + 128] = (weight - change).astype(jnp.bfloat16)
 
 
-def updated_weights(totals, row_new, col_state, gradient, weight, tile=1664):
+def updated_weights(totals, sums, row_new, col_state, gradient, weight, tile=1664):
     rows, width = weight.shape
     whole = lambda shape: pl.BlockSpec(shape, lambda i: (0,) * len(shape))
     block = pl.BlockSpec((rows, tile), lambda i: (0, i))
     return pl.pallas_call(
         weights_kernel,
         grid=(width // tile,),
-        in_specs=[whole(totals.shape), whole(row_new.shape), whole(col_state.shape), block, block],
+        in_specs=[whole(totals.shape), whole(sums.shape), whole(row_new.shape), whole(col_state.shape), block, block],
         out_specs=[block, whole(col_state.shape)],
         out_shape=[
             jax.ShapeDtypeStruct((rows, width), jnp.bfloat16),
@@ -221,7 +222,7 @@
         ],
         scratch_shapes=[pltpu.VMEM((rows, 128), jnp.float32), pltpu.VMEM((1, width), jnp.float32)],
         compiler_params=pltpu.CompilerParams(vmem_limit_bytes=wide_vmem),
-    )(totals, row_new, col_state, gradient, weight)
+    )(totals, sums, row_new, col_state, gradient, weight)
 
 
 def body(hidden_last, labels, head_weight, layer_inputs, weights, row_state, col_state):
@@ -258,10 +259,14 @@
     exponent = jnp.exp(logits)
     columns = tensor_index * vocab_local + lax.iota(jnp.int32, vocab_local)
     label_hit = labels_here[None, :] == columns[:, None]
+    weight_float = local_weight.astype(jnp.float32)
+    weight_part = jnp.broadcast_to(jnp.sum(weight_float * weight_float), (share,))
     sums = jnp.stack(
         [
             jnp.sum(exponent, axis=0),
             jnp.sum(jnp.where(label_hit, logits, jnp.zeros_like(logits)), axis=0),
+            weight_part,
+            jnp.broadcast_to(jnp.sum(row_state[0]), (share,)),
         ]
     )
     sums = summed_tensor(sums)
@@ -287,9 +292,7 @@
     for distance in (1, 2):
         loss = loss + lax.ppermute(loss, "x", [(i, i ^ distance) for i in range(section_count)])
     loss = loss[0] / all_rows
-    weight_float = local_weight.astype(jnp.float32)
-    weight_part = jnp.sum(weight_float * weight_float)
-    full, loss, weight_part = lax.optimization_barrier((full, loss, weight_part))
+    full, loss = lax.optimization_barrier((full, loss))
     gradient = lax.dot_general(
         saved_all, full, (((0,), (1,)), ((), ())), preferred_element_type=jnp.float32
     )
@@ -297,14 +300,13 @@
     row_new = decay_rate * row_state[0] + (1.0 - decay_rate) * jnp.mean(squares + tiny_term, axis=1)
     col_part = jnp.sum(squares + tiny_term, axis=0)
     scaled_part = jnp.sum(squares * (1.0 / row_new)[:, None], axis=0)
-    room = [(0, 128, 0)]
-    totals = jnp.stack([lax.pad(col_part, jnp.sum(row_new), room), lax.pad(scaled_part, weight_part, room)])
+    totals = jnp.stack([col_part, scaled_part])
     totals = totals + other_core(totals)
     totals = summed_ring(summed_ring(totals, "z"), "y")
     row_new = row_new[:, None]
     backward = jnp.dot(local_weight, full, preferred_element_type=jnp.float32)
     outputs = (dy.astype(jnp.float32) + backward).astype(jnp.bfloat16)
-    new_weight, col_new = updated_weights(totals, row_new, col_state, gradient, local_weight)
+    new_weight, col_new = updated_weights(totals, sums, row_new, col_state, gradient, local_weight)
     return (loss, outputs.T[None], new_weight[None], row_new.T, col_new)
 
 

time: 272 us -> 271 us (level)
  waiting for transfers between devices: 69.1 us -> 63.2 us
    all_gather x1, waiting for transfers between devices: 8.49 us -> 1.61 us  [body(): all_weights = lax.all_gather(local_weight, 'x', axis=0)]
  transfers between devices with their start and end apart: 21 -> 21, of which waited for: 15 -> 14; matrix products, arithmetic and copies ran while one was open for 10% -> 12% of each run, Pallas kernels for 2% -> 3%
where the time goes in v7:
time: 271 us; the launch traced here: 270 us
  blocking collectives  103 us (38%)
  waiting for transfers between devices  63.2 us (23%)
  matrix products  26.9 us (10%)
  Pallas kernels  23.4 us (9%)
  starting transfers between devices  23.2 us (9%)
  between operations  17.4 us (6%)
  other arithmetic  8.47 us (3%)
  local copies, waits for them, and re-layouts  4.72 us (2%)
    all_to_all x5, blocking collectives, swapped_chips(): return lax.all_to_all(blocks, chips, 0, 0, tiled=True)  103 us
    all_gather x1, waiting for transfers between devices, body(): full = lax.all_gather(dy, ('y', 'z', 'c'), axis=0, tiled=True)  37.2 us
    ppermute x7, waiting for transfers between devices, other_core(): return lax.ppermute(x, 'c', [(0, 1), (1, 0)])  11.8 us
    pallas_call x3, Pallas kernels, layer_back(): pl.pallas_call(layer_kernel, grid_spec=pltpu.PrefetchScalarGridSpec(num_s...  10.8 us
    dot_general x1, matrix products, body(): lax.dot_general(both, head_weight, (((0,), (1,)), ((), ())), preferred_el...  10.8 us
    dot_general x1, matrix products, body(): lax.dot_general(head_weight, hidden_all, (((0,), (0,)), ((), ())), prefer...  8.44 us
    ppermute x6, starting transfers between devices, summed_ring(): lax.ppermute(x, axis, [(i, (i - step) % 4) for i in range(4)])  8.26 us
    ppermute x3, starting transfers between devices, exchanged(): lax.ppermute(piece, axis, [(i, (i + step) % size) for i in range(size)])  6 us
  transfers between devices with their start and end apart: 21, of which 14 were waited for; matrix products, arithmetic and copies ran while one was open for 12% of the time, Pallas kernels for 3%

profile of v7, /device:TPU:0, one launch (start us, length us, event | category | flops | bytes accessed | tf_op | source)
XLA Modules:
  0.0 270.2 jit_solution(14401134490244761880)
XLA Ops:
  7.2 0.7 all-gather.3.cloned.1.call-update
  7.9 0.9 dynamic-slice_bitcast_fusion
  8.9 0.1 broadcast_in_dim.18
  9.0 22.8 %all_to_all.30.refs_0_ = bf16[16,208,128]{2,1,0:T(8,128)(2,1)} all-to-all(bf16[16,208,128]{2,1,0:T(8,128)(2,1)S(1)} %broadcast_in_dim.18), channel_id=1, replica_groups=mesh['x'=4,'y'=4,'z'=4,'c'=2] {'y','z'}, dimensions={0} | all-to-all | bytes 1703936 | tf_op jit(solution)/shard_map/all_to_all | solution.py:32
  31.8 0.8 dynamic_slice.7
  32.6 1.3 reduce_sum.96
  33.8 0.7 pad.9.clone
  34.6 2.0 multiply_reduce_fusion.1
  36.6 0.7 pad.8.clone
  37.3 0.1 stack.79.place_ref
  37.4 2.1 shard_map.110
  39.5 8.4 %exponential_reduce_fusion = (f32[128]{0:T(128)S(1)}, f32[128]{0:T(128)S(1)}, bf16[1000,128]{1,0:T(8,128)(2,1)S(1)}) fusion(s32[1000]{0:T(1024)S(1)} %iota_add_fusion, s32[128]{0:T(128)S(1)} %dynamic_slice.7, bf16[6656,128]{1,0:T(8,128)(2,1)S(1)} %shard_map.110, bf16[6656,1000]{0,1:T(8,128)(2,1)} %param.9), kind=kOutput, calls=%fused_computation.19 | convolution fusion | flops 1704703744 | bytes 15277472 | tf_op jit(solution)/shard_map/dot_general | solution.py:256
  48.0 0.5 collective-permute-start.1
  48.5 0.2 compare_convert_fusion
  48.7 0.6 collective-permute-done.1
  49.4 0.6 broadcast_in_dim.20
  50.0 3.9 %all-to-all-start.1 = ((f32[16,4,128]{2,1,0:T(4,128)}), f32[16,4,128]{2,1,0:T(4,128)S(1)}, u32[]{:S(2)}, u32[]{:S(2)}) async-start(f32[16,4,128]{2,1,0:T(4,128)} %broadcast_in_dim.20), calls=%async_computation.1 | async-start | bytes 65536 | tf_op jit(solution)/shard_map/all_to_all | solution.py:32
  54.0 10.8 %fusion.4.product_ref = f32[256,6656]{1,0:T(8,128)} fusion(bf16[6656,1000]{0,1:T(8,128)(2,1)} %param.9, bf16[1000,128]{1,0:T(8,128)(2,1)S(1)} %compare_convert_fusion, bf16[1000,128]{1,0:T(8,128)(2,1)S(1)} %get-tuple-element.23), kind=kOutput, calls=%fused_computation.14 | convolution fusion | flops 3408896000 | bytes 20639744 | tf_op jit(solution)/shard_map/dot_general | solution.py:276
  64.8 5.1 %shard_map.111 = (f32[4,4,208,128]{3,2,1,0:T(8,128)S(1)}, bf16[4,4,208,128]{3,2,1,0:T(8,128)(2,1)S(1)}) custom-call(s32[6]{0:T(128)S(1)} %stack.79.place_ref, f32[256,6656]{1,0:T(8,128)} %fusion.4.product_ref, f32[4,128]{1,0:T(4,128)S(1)} %reduce_sum.97.sums_ref), custom_call_target="tpu_custom_call" | custom-call | tf_op jit(solution)/shard_map/pallas_call | solution.py:121
  69.9 0.1 collective-permute-start.2
  70.0 2.3 collective-permute-done.2
  72.4 0.2 add_convert_fusion
  72.6 22.2 %all_to_all.31 = bf16[16,208,128]{2,1,0:T(8,128)(2,1)} all-to-all(bf16[16,208,128]{2,1,0:T(8,128)(2,1)S(1)} %bitcast.66), channel_id=1, replica_groups=mesh['x'=4,'y'=4,'z'=4,'c'=2] {'y','z'}, dimensions={0} | all-to-all | bytes 1703936 | tf_op jit(solution)/shard_map/all_to_all | solution.py:32
  94.8 1.3 reduce_sum.98.refs_2_
  96.0 0.1 broadcast_in_dim.21
  96.2 17.5 %all_to_all.32.refs_0_ = bf16[16,208,128]{2,1,0:T(8,128)(2,1)} all-to-all(bf16[16,208,128]{2,1,0:T(8,128)(2,1)S(1)} %broadcast_in_dim.21), channel_id=1, replica_groups=mesh['x'=4,'y'=4,'z'=4,'c'=2] {'y','z'}, dimensions={0} | all-to-all | bytes 1703936 | tf_op jit(solution)/shard_map/all_to_all | solution.py:32
  113.8 2.6 collective-permute-done.3.refs_1_
  116.4 1.6 all-gather.3.cloned.1.call-done.refs_3_
  118.0 3.6 %shard_map.112.refs_2_ = bf16[208,128]{1,0:T(8,128)(2,1)S(1)} custom-call(s32[6]{0:T(128)S(1)} %stack.78.place_ref, bf16[16,208,128]{2,1,0:T(8,128)(2,1)} %all_to_all.32.refs_0_, bf16[16,208,128]{2,1,0:T(8,128)(2,1)} %collective-permute-done.3.refs_1_, bf16[208,128]{1,0:T(8,128)(2,1)S(1)} %reduce_sum.98.refs_2_, ...), custom_call_target="tpu_custom_call" | custom-call | tf_op jit(solution)/shard_map/pallas_call | solution.py:163
  121.6 0.1 broadcast_in_dim.22
  121.8 21.7 %all_to_all.33.refs_0_ = bf16[16,208,128]{2,1,0:T(8,128)(2,1)} all-to-all(bf16[16,208,128]{2,1,0:T(8,128)(2,1)S(1)} %broadcast_in_dim.22), channel_id=1, replica_groups=mesh['x'=4,'y'=4,'z'=4,'c'=2] {'y','z'}, dimensions={0} | all-to-all | bytes 1703936 | tf_op jit(solution)/shard_map/all_to_all | solution.py:32
  143.5 2.6 collective-permute-done.4.refs_1_
  146.1 3.6 %shard_map.113.refs_2_ = bf16[208,128]{1,0:T(8,128)(2,1)S(1)} custom-call(s32[6]{0:T(128)S(1)} %stack.83.place_ref, bf16[16,208,128]{2,1,0:T(8,128)(2,1)} %all_to_all.33.refs_0_, bf16[16,208,128]{2,1,0:T(8,128)(2,1)} %collective-permute-done.4.refs_1_, bf16[208,128]{1,0:T(8,128)(2,1)S(1)} %shard_map.112.refs_2_, ...), custom_call_target="tpu_custom_call" | custom-call | tf_op jit(solution)/shard_map/pallas_call | solution.py:163
  149.8 0.1 broadcast_in_dim.23
  149.9 18.7 %all_to_all.34.refs_0_ = bf16[16,208,128]{2,1,0:T(8,128)(2,1)} all-to-all(bf16[16,208,128]{2,1,0:T(8,128)(2,1)S(1)} %broadcast_in_dim.23), channel_id=1, replica_groups=mesh['x'=4,'y'=4,'z'=4,'c'=2] {'y','z'}, dimensions={0} | all-to-all | bytes 1703936 | tf_op jit(solution)/shard_map/all_to_all | solution.py:32
  168.7 2.6 collective-permute-done.5.refs_1_
  171.3 3.6 %shard_map.114 = bf16[208,128]{1,0:T(8,128)(2,1)S(1)} custom-call(s32[6]{0:T(128)S(1)} %stack.84.place_ref, bf16[16,208,128]{2,1,0:T(8,128)(2,1)} %all_to_all.34.refs_0_, bf16[16,208,128]{2,1,0:T(8,128)(2,1)} %collective-permute-done.5.refs_1_, bf16[208,128]{1,0:T(8,128)(2,1)S(1)} %shard_map.113.refs_2_, ...), custom_call_target="tpu_custom_call" | custom-call | tf_op jit(solution)/shard_map/pallas_call | solution.py:163
  174.9 2.8 %collective-permute-start.7 = (bf16[208,128]{1,0:T(8,128)(2,1)S(1)}, bf16[208,128]{1,0:T(8,128)(2,1)S(1)}, u32[]{:S(2)}, u32[]{:S(2)}) collective-permute-start(bf16[208,128]{1,0:T(8,128)(2,1)S(1)} %get-tuple-element.28), channel_id=1, source_target_pairs={{0,64},{32,96},{64,0},{96,32},{1,65},{33,97},{65,1},{97,33},{2,66}... | collective-permute-start | bytes 159752 | tf_op jit(solution)/shard_map/ppermute | solution.py:65
  177.7 3.2 %collective-permute-start.6 = (bf16[208,128]{1,0:T(8,128)(2,1)S(1)}, bf16[208,128]{1,0:T(8,128)(2,1)S(1)}, u32[]{:S(2)}, u32[]{:S(2)}) collective-permute-start(bf16[208,128]{1,0:T(8,128)(2,1)S(1)} %get-tuple-element.29), channel_id=1, source_target_pairs={{0,96},{32,0},{64,32},{96,64},{1,97},{33,1},{65,33},{97,65},{2,98}... | collective-permute-start | bytes 159752 | tf_op jit(solution)/shard_map/ppermute | solution.py:65
  181.0 2.1 collective-permute-done.8
  183.1 0.7 copy_bitcast_fusion
  183.9 0.6 subtract_reduce_fusion
  184.5 3.6 %collective-permute-done.9 = f32[1]{0:T(128)} collective-permute-done((f32[1]{0:T(128)}, f32[1]{0:T(128)}, u32[]{:S(2)}, u32[]{:S(2)}) %collective-permute-start.9) | collective-permute-done | bytes 36 | tf_op jit(solution)/shard_map/ppermute | solution.py:293
  189.4 4.0 %collective-permute-start.10 = (f32[1]{0:T(128)}, f32[1]{0:T(128)}, u32[]{:S(2)}, u32[]{:S(2)}) collective-permute-start(f32[1]{0:T(128)} %add.85), channel_id=1, source_target_pairs={{0,64},{32,96},{64,0},{96,32},{1,65},{33,97},{65,1},{97,33},{2,66}... | collective-permute-start | bytes 20 | tf_op jit(solution)/shard_map/ppermute | solution.py:293
  193.5 1.0 collective-permute-done.10
  195.2 37.2 %all-gather.5.cloned.1.call-done = bf16[6656,512]{1,0:T(8,128)(2,1)} async-done(((bf16[208,512]{1,0:T(8,128)(2,1)}), bf16[6656,512]{1,0:T(8,128)(2,1)}) %all-gather.5.cloned.1.call-update) | async-done | bytes 6815760 | tf_op jit(solution)/shard_map/all_gather | solution.py:290
  232.4 5.4 %add_reduce_fusion = (f32[208]{0:T(256)S(1)}, f32[208,6656]{1,0:T(8,128)S(1)}) fusion(bf16[6656,512]{1,0:T(8,128)(2,1)} %all-gather.5.cloned.1.call-done, bf16[1,512,208]{1,2,0:T(8,128)(2,1)S(1)} %copy-done), kind=kOutput, calls=%fused_computation.3 | convolution fusion | flops 1421827840 | bytes 12567360 | tf_op jit(solution)/shard_map/dot_general | solution.py:296
  237.9 0.6 fusion.11
  238.5 1.0 add_reduce_fusion.1
  239.6 0.3 collective-permute-start.11
  240.0 1.0 collective-permute-done.11
  241.0 1.9 collective-permute-start.13
  243.0 0.1 collective-permute-start.14
  243.1 2.1 collective-permute-start.12
  245.2 2.3 fusion.2
  247.5 1.5 collective-permute-done.14
  249.0 0.1 add_add_fusion.1
  249.1 1.8 collective-permute-start.16
  250.9 0.3 collective-permute-start.17
  251.2 2.0 collective-permute-start.15
  253.2 0.1 copy.27.row_new_ref
  253.4 2.9 %collective-permute-done.17 = f32[2,6656]{1,0:T(2,128)S(1)} collective-permute-done((f32[2,6656]{1,0:T(2,128)S(1)}, f32[2,6656]{1,0:T(2,128)S(1)}, u32[]{:S(2)}, u32[]{:S(2)}) %collective-permute-start.17) | collective-permute-done | bytes 53280 | tf_op jit(solution)/shard_map/ppermute | solution.py:51
  256.3 0.6 collective-permute-done.15
  256.9 5.3 %shard_map.115 = (bf16[208,6656]{1,0:T(8,128)(2,1)}, f32[1,6656]{1,0:T(1,128)}) custom-call(f32[2,6656]{1,0:T(2,128)S(1)} %add_add_fusion.totals_ref, f32[4,128]{1,0:T(4,128)S(1)} %reduce_sum.97.sums_ref, f32[208,1]{1,0:T(8,128)S(1)} %copy.27.row_new_ref, f32[1,6656]{1,0:T(1,128)S(1)} %copy-done.2, f32[208,6656]{1,0:T(8,128)} %copy-done.3, ...), custom_call_target="tpu_custom_call" | custom-call | tf_op jit(solution)/shard_map/pallas_call | solution.py:214
  (49 shorter events, 0.9 us)
Async XLA Ops:
  7.2 225.3 %copy-start = (bf16[1,512,208]{1,2,0:T(8,128)(2,1)S(1)}, bf16[1,512,208]{1,2,0:T(8,128)(2,1)}, u32[]{:S(2)}) copy-start(bf16[1,512,208]{1,2,0:T(8,128)(2,1)} %param.10) | copy-start | bytes 638980
  7.2 27.4 %copy-start.1 = (bf16[1,208,6656]{2,1,0:T(8,128)(2,1)S(1)}, bf16[1,208,6656]{2,1,0:T(8,128)(2,1)}, u32[]{:S(2)}) copy-start(bf16[1,208,6656]{2,1,0:T(8,128)(2,1)} %param.11) | copy-start | bytes 8306692
  7.2 110.8 %all-gather.3.cloned.1.call-start = ((), (), s32[]{:S(2)}) async-start(), calls=%async_computation.6 | async-start | bytes 13844480 | tf_op jit(solution)/shard_map/all_gather | solution.py:252
  31.8 5.6 %collective-permute-start = (bf16[16,208,128]{2,1,0:T(8,128)(2,1)}, bf16[16,208,128]{2,1,0:T(8,128)(2,1)}, u32[]{:S(2)}, u32[]{:S(2)}) collective-permute-start(bf16[16,208,128]{2,1,0:T(8,128)(2,1)} %all_to_all.30.refs_0_), channel_id=1, source_target_pairs={{0,1},{1,0},{2,3},{3,2},{4,5},{5,4},{6,7},{7,6},{8,9},{9,8},{10,11... | collective-permute-start | bytes 2555912 | tf_op jit(solution)/shard_map/ppermute | solution.py:28
  48.0 1.3 collective-permute-start.1
  50.0 14.7 %all-to-all-start.1 = ((f32[16,4,128]{2,1,0:T(4,128)}), f32[16,4,128]{2,1,0:T(4,128)S(1)}, u32[]{:S(2)}, u32[]{:S(2)}) async-start(f32[16,4,128]{2,1,0:T(4,128)} %broadcast_in_dim.20), calls=%async_computation.1 | async-start | bytes 65536 | tf_op jit(solution)/shard_map/all_to_all | solution.py:32
  53.9 178.5 %all-gather.5.cloned.1.call-start = ((), (), s32[]{:S(2)}) async-start(), calls=%async_computation.7 | async-start | bytes 7028736 | tf_op jit(solution)/shard_map/all_gather | solution.py:290
  69.9 2.5 collective-permute-start.2
  113.7 2.7 %collective-permute-start.3 = (bf16[16,208,128]{2,1,0:T(8,128)(2,1)}, bf16[16,208,128]{2,1,0:T(8,128)(2,1)}, u32[]{:S(2)}, u32[]{:S(2)}) collective-permute-start(bf16[16,208,128]{2,1,0:T(8,128)(2,1)} %all_to_all.32.refs_0_), channel_id=1, source_target_pairs={{0,1},{1,0},{2,3},{3,2},{4,5},{5,4},{6,7},{7,6},{8,9},{9,8},{10,11... | collective-permute-start | bytes 2555912 | tf_op jit(solution)/shard_map/ppermute | solution.py:28
  143.4 2.7 %collective-permute-start.4 = (bf16[16,208,128]{2,1,0:T(8,128)(2,1)}, bf16[16,208,128]{2,1,0:T(8,128)(2,1)}, u32[]{:S(2)}, u32[]{:S(2)}) collective-permute-start(bf16[16,208,128]{2,1,0:T(8,128)(2,1)} %all_to_all.33.refs_0_), channel_id=1, source_target_pairs={{0,1},{1,0},{2,3},{3,2},{4,5},{5,4},{6,7},{7,6},{8,9},{9,8},{10,11... | collective-permute-start | bytes 2555912 | tf_op jit(solution)/shard_map/ppermute | solution.py:28
  168.6 2.7 %collective-permute-start.5 = (bf16[16,208,128]{2,1,0:T(8,128)(2,1)}, bf16[16,208,128]{2,1,0:T(8,128)(2,1)}, u32[]{:S(2)}, u32[]{:S(2)}) collective-permute-start(bf16[16,208,128]{2,1,0:T(8,128)(2,1)} %all_to_all.34.refs_0_), channel_id=1, source_target_pairs={{0,1},{1,0},{2,3},{3,2},{4,5},{5,4},{6,7},{7,6},{8,9},{9,8},{10,11... | collective-permute-start | bytes 2555912 | tf_op jit(solution)/shard_map/ppermute | solution.py:28
  174.9 6.0 %collective-permute-start.7 = (bf16[208,128]{1,0:T(8,128)(2,1)S(1)}, bf16[208,128]{1,0:T(8,128)(2,1)S(1)}, u32[]{:S(2)}, u32[]{:S(2)}) collective-permute-start(bf16[208,128]{1,0:T(8,128)(2,1)S(1)} %get-tuple-element.28), channel_id=1, source_target_pairs={{0,64},{32,96},{64,0},{96,32},{1,65},{33,97},{65,1},{97,33},{2,66}... | collective-permute-start | bytes 159752 | tf_op jit(solution)/shard_map/ppermute | solution.py:65
  177.7 5.3 %collective-permute-start.8 = (bf16[208,128]{1,0:T(8,128)(2,1)S(1)}, bf16[208,128]{1,0:T(8,128)(2,1)S(1)}, u32[]{:S(2)}, u32[]{:S(2)}) collective-permute-start(bf16[208,128]{1,0:T(8,128)(2,1)S(1)} %get-tuple-element.27), channel_id=1, source_target_pairs={{0,32},{32,64},{64,96},{96,0},{1,33},{33,65},{65,97},{97,1},{2,34}... | collective-permute-start | bytes 159752 | tf_op jit(solution)/shard_map/ppermute | solution.py:65
  177.7 5.3 %collective-permute-start.6 = (bf16[208,128]{1,0:T(8,128)(2,1)S(1)}, bf16[208,128]{1,0:T(8,128)(2,1)S(1)}, u32[]{:S(2)}, u32[]{:S(2)}) collective-permute-start(bf16[208,128]{1,0:T(8,128)(2,1)S(1)} %get-tuple-element.29), channel_id=1, source_target_pairs={{0,96},{32,0},{64,32},{96,64},{1,97},{33,1},{65,33},{97,65},{2,98}... | collective-permute-start | bytes 159752 | tf_op jit(solution)/shard_map/ppermute | solution.py:65
  184.5 3.6 %collective-permute-start.9 = (f32[1]{0:T(128)}, f32[1]{0:T(128)}, u32[]{:S(2)}, u32[]{:S(2)}) collective-permute-start(f32[1]{0:T(128)} %bitcast.14), channel_id=1, source_target_pairs={{0,32},{32,0},{64,96},{96,64},{1,33},{33,1},{65,97},{97,65},{2,34}... | collective-permute-start | bytes 20 | tf_op jit(solution)/shard_map/ppermute | solution.py:293
  189.4 5.1 %collective-permute-start.10 = (f32[1]{0:T(128)}, f32[1]{0:T(128)}, u32[]{:S(2)}, u32[]{:S(2)}) collective-permute-start(f32[1]{0:T(128)} %add.85), channel_id=1, source_target_pairs={{0,64},{32,96},{64,0},{96,32},{1,65},{33,97},{65,1},{97,33},{2,66}... | collective-permute-start | bytes 20 | tf_op jit(solution)/shard_map/ppermute | solution.py:293
  232.4 12.8 %slice-start = ((s8[6815744]{0:T(1024)(128)(4,1)}), s8[4194304]{0:T(1024)(128)(4,1)S(1)}, s32[]{:S(2)}) async-start(s8[6815744]{0:T(1024)(128)(4,1)} %bitcast.74), calls=%async_computation.8 | async-start | bytes 8388608
  232.4 5.5 %copy-start.4 = (f32[1,208]{1,0:T(1,128)S(1)}, f32[1,208]{1,0:T(1,128)}, u32[]{:S(2)}) copy-start(f32[1,208]{1,0:T(1,128)} %param.12) | copy-start | bytes 2500
  232.4 12.8 %slice-start.1 = ((s8[6815744]{0:T(1024)(128)(4,1)}), s8[2621440]{0:T(1024)(128)(4,1)S(1)}, s32[]{:S(2)}) async-start(s8[6815744]{0:T(1024)(128)(4,1)} %bitcast.74), calls=%async_computation.9 | async-start | bytes 5242880
  237.9 9.6 %copy-start.3 = (f32[208,6656]{1,0:T(8,128)}, f32[208,6656]{1,0:T(8,128)S(1)}, u32[]{:S(2)}) copy-start(f32[208,6656]{1,0:T(8,128)S(1)} %get-tuple-element.33.gradient_ref) | copy-start | bytes 16613380
  239.6 1.3 collective-permute-start.11
  241.0 15.9 %copy-start.2 = (f32[1,6656]{1,0:T(1,128)S(1)}, f32[1,6656]{1,0:T(1,128)}, u32[]{:S(2)}) copy-start(f32[1,6656]{1,0:T(1,128)} %col_ref.1) | copy-start | bytes 79876
  241.0 6.5 %collective-permute-start.13 = (f32[2,6656]{1,0:T(2,128)S(1)}, f32[2,6656]{1,0:T(2,128)S(1)}, u32[]{:S(2)}, u32[]{:S(2)}) collective-permute-start(f32[2,6656]{1,0:T(2,128)S(1)} %fusion.13), channel_id=1, source_target_pairs={{0,6},{2,0},{4,2},{6,4},{1,7},{3,1},{5,3},{7,5},{8,14},{10,8},{12,... | collective-permute-start | bytes 159752 | tf_op jit(solution)/shard_map/ppermute | solution.py:51
  243.0 6.1 %collective-permute-start.14 = (f32[2,6656]{1,0:T(2,128)S(1)}, f32[2,6656]{1,0:T(2,128)S(1)}, u32[]{:S(2)}, u32[]{:S(2)}) collective-permute-start(f32[2,6656]{1,0:T(2,128)S(1)} %fusion.13), channel_id=1, source_target_pairs={{0,2},{2,4},{4,6},{6,0},{1,3},{3,5},{5,7},{7,1},{8,10},{10,12},{12... | collective-permute-start | bytes 159752 | tf_op jit(solution)/shard_map/ppermute | solution.py:51
  243.1 5.9 %collective-permute-start.12 = (f32[2,6656]{1,0:T(2,128)S(1)}, f32[2,6656]{1,0:T(2,128)S(1)}, u32[]{:S(2)}, u32[]{:S(2)}) collective-permute-start(f32[2,6656]{1,0:T(2,128)S(1)} %fusion.13), channel_id=1, source_target_pairs={{0,4},{2,6},{4,0},{6,2},{1,5},{3,7},{5,1},{7,3},{8,12},{10,14},{12... | collective-permute-start | bytes 159752 | tf_op jit(solution)/shard_map/ppermute | solution.py:51
  249.1 4.2 %collective-permute-start.16 = (f32[2,6656]{1,0:T(2,128)S(1)}, f32[2,6656]{1,0:T(2,128)S(1)}, u32[]{:S(2)}, u32[]{:S(2)}) collective-permute-start(f32[2,6656]{1,0:T(2,128)S(1)} %add_add_fusion.1), channel_id=1, source_target_pairs={{0,24},{8,0},{16,8},{24,16},{1,25},{9,1},{17,9},{25,17},{2,26},{10... | collective-permute-start | bytes 159752 | tf_op jit(solution)/shard_map/ppermute | solution.py:51
  250.9 5.3 %collective-permute-start.17 = (f32[2,6656]{1,0:T(2,128)S(1)}, f32[2,6656]{1,0:T(2,128)S(1)}, u32[]{:S(2)}, u32[]{:S(2)}) collective-permute-start(f32[2,6656]{1,0:T(2,128)S(1)} %add_add_fusion.1), channel_id=1, source_target_pairs={{0,8},{8,16},{16,24},{24,0},{1,9},{9,17},{17,25},{25,1},{2,10},{10... | collective-permute-start | bytes 159752 | tf_op jit(solution)/shard_map/ppermute | solution.py:51
  251.2 5.6 %collective-permute-start.15 = (f32[2,6656]{1,0:T(2,128)S(1)}, f32[2,6656]{1,0:T(2,128)S(1)}, u32[]{:S(2)}, u32[]{:S(2)}) collective-permute-start(f32[2,6656]{1,0:T(2,128)S(1)} %add_add_fusion.1), channel_id=1, source_target_pairs={{0,16},{8,24},{16,0},{24,8},{1,17},{9,25},{17,1},{25,9},{2,18},{10... | collective-permute-start | bytes 159752 | tf_op jit(solution)/shard_map/ppermute | solution.py:51
Sparse Core Ops, SparseCore 0:
  9.7 108.2 all-gather.2
  184.0 48.3 all-gather.4
